TPU v7x, 128 devices: a whole 4x4x4 slice. The times are simulated.
128 devices in a mesh: seq: 16 (over x_lo, y, core), tp: 8 (over x_hi, z).
Axes of the slice: x: 4 (x_hi: 2, x_lo: 2; x = x_hi * 2 + x_lo), y: 4, z: 4, core: 2. Of those that a mesh axis runs over, the one named last changes fastest.
Arguments:
- embeddings: bfloat16 [6144, 4096], P('seq', 'tp'), may hold values from -6 to 6
- span_mask: int32 [6144], P('seq'), may hold values from 0 to 1, as said below
- sentinel_id: int32 [6144], P('seq'), may hold values from 0 to 99, as said below
- sentinel_table: bfloat16 [100, 4096], P(None, 'tp'), may hold values from -6 to 6
- gen_weight: bfloat16 [4096, 240], P(None, 'tp'), may hold values from -0.1875 to 0.1875
- up_weight: bfloat16 [4096, 8192], P(None, 'tp'), may hold values from -0.09375 to 0.09375
- down_weight: bfloat16 [8192, 4096], P('tp'), may hold values from -0.0625 to 0.0625
- cotangent: bfloat16 [6144, 4096], P('seq', 'tp'), may hold values from -0.59765625 to 0.59765625
Outputs:
- layer_output: bfloat16 [6144, 4096], P('seq', 'tp')
- embed_grad: float32 [6144, 4096], P('seq', 'tp')
- table_grad: float32 [100, 4096], P(None, 'tp')
- gen_grad: float32 [4096, 240], P(None, 'tp')
- up_grad: float32 [4096, 8192], P('seq', 'tp')
- down_grad: float32 [8192, 4096], P('tp', 'seq')
Inputs may be any that keep to these rules, and one draw needn't show every extreme that they name: `span_mask`: the tokens fall into aligned blocks of 16; each block holds exactly one span of 1 to 3 consecutive tokens marked 1, the rest 0. `sentinel_id`: all 16 tokens of an aligned block carry the same sentinel id.
All inputs are finite; a program needn't handle non-finite values.
Results may differ from a plain program's by a relative error of at most 0.035.
Values may be sent and summed in bfloat16 or wider, within the bound.
No kernel may reach another device: no remote copies, remote signals or barrier semaphores. Data moves between devices by JAX's collectives and lax.ppermute only.
A program may use at most 192 MiB of HBM per device.

v0:
```python
import jax
import jax.numpy as jnp
from jax import lax
from jax.sharding import PartitionSpec as P

KW = 15
SENT = 100


def with_halo(block, sides, width):
    for axis, dim in sides:
        count = lax.axis_size(axis)
        forward = [(i, i + 1) for i in range(count - 1)]
        backward = [(target, source) for source, target in forward]
        low = lax.ppermute(
            lax.slice_in_dim(block, block.shape[dim] - width, None, axis=dim), axis, forward
        )
        high = lax.ppermute(lax.slice_in_dim(block, 0, width, axis=dim), axis, backward)
        block = jnp.concatenate([low, block, high], axis=dim)
    return block


def gelu_tanh(values):
    return jax.nn.gelu(values, approximate=True)


def body(
    embeddings,
    span_mask,
    sentinel_id,
    sentinel_table,
    gen_weight,
    up_weight,
    down_weight,
    cotangent,
):
    tok_rows, feat_width = embeddings.shape
    head_count = gen_weight.shape[1] // KW
    head_width = feat_width // head_count
    tap_reach = (KW - 1) // 2
    sentinel_codes = jnp.arange(SENT, dtype=jnp.int32)
    onehot = sentinel_id[:, None] == sentinel_codes[None, :]
    picked = jnp.dot(
        onehot.astype(jnp.bfloat16), sentinel_table, preferred_element_type=jnp.float32
    ).astype(jnp.bfloat16)
    masked = span_mask[:, None] == 1
    hidden = jnp.where(masked, picked, embeddings)
    full_hidden = lax.all_gather(hidden, "tp", axis=1, tiled=True)
    logits = jnp.dot(full_hidden, gen_weight, preferred_element_type=jnp.float32)
    exp_logits = jnp.exp(logits.reshape(tok_rows, head_count, KW))
    kernel = exp_logits / jnp.sum(exp_logits, axis=-1, keepdims=True)
    padded = with_halo(hidden, (("seq", 0),), tap_reach)
    padded = padded.reshape(tok_rows + 2 * tap_reach, head_count, head_width)
    conv_sum = jnp.zeros((tok_rows, head_count, head_width), jnp.float32)
    for tap_index in range(KW):
        conv_sum = (
            conv_sum + kernel[:, :, tap_index, None] * padded[tap_index : tap_index + tok_rows]
        )
    act = (hidden.astype(jnp.float32) + conv_sum.reshape(tok_rows, feat_width)).astype(jnp.bfloat16)
    shard_piece = lax.all_gather(act, "tp", axis=1, tiled=True)
    up_rows = up_weight
    pre_sum = jnp.dot(shard_piece, up_rows, preferred_element_type=jnp.float32)
    full_copy = shard_piece
    middle, gelu_back = jax.vjp(gelu_tanh, pre_sum)
    middle = middle.astype(jnp.bfloat16)
    down_cols = down_weight
    ffn_total = lax.psum_scatter(
        lax.dot_general(
            down_cols, middle, (((0,), (1,)), ((), ())), preferred_element_type=jnp.float32
        ).astype(jnp.bfloat16),
        "tp",
        scatter_dimension=0,
        tiled=True,
    ).astype(jnp.float32)
    layer_output = (act.astype(jnp.float32) + ffn_total.T).astype(jnp.bfloat16)
    shard_piece = lax.all_gather(cotangent, "tp", axis=1, tiled=True)
    down_cols = down_weight
    middle_sum = lax.dot_general(
        shard_piece, down_cols, (((1,), (1,)), ((), ())), preferred_element_type=jnp.float32
    )
    block_term = lax.dot_general(
        middle, shard_piece, (((0,), (0,)), ((), ())), preferred_element_type=jnp.float32
    )
    down_term = block_term
    middle_grad, down_term = (middle_sum, down_term)
    down_grad = lax.psum_scatter(
        down_term.astype(jnp.bfloat16), "seq", scatter_dimension=1, tiled=True
    ).astype(jnp.float32)
    pre_grad = gelu_back(middle_grad)[0].astype(jnp.bfloat16)
    up_grad = lax.psum_scatter(
        lax.dot_general(
            full_copy, pre_grad, (((0,), (0,)), ((), ())), preferred_element_type=jnp.float32
        ).astype(jnp.bfloat16),
        "seq",
        scatter_dimension=0,
        tiled=True,
    ).astype(jnp.float32)
    up_rows = up_weight
    act_back = lax.psum_scatter(
        lax.dot_general(
            up_rows, pre_grad, (((1,), (1,)), ((), ())), preferred_element_type=jnp.float32
        ).astype(jnp.bfloat16),
        "tp",
        scatter_dimension=0,
        tiled=True,
    ).astype(jnp.float32)
    act_grad = cotangent.astype(jnp.float32) + act_back.T
    act_three = act_grad.reshape(tok_rows, head_count, head_width)
    kernel_grad = jnp.stack(
        [
            jnp.sum(act_three * padded[tap_index : tap_index + tok_rows], axis=-1)
            for tap_index in range(KW)
        ],
        axis=-1,
    )
    weighted = jnp.sum(kernel * kernel_grad, axis=-1, keepdims=True)
    logit_grad = (
        (kernel * (kernel_grad - weighted)).reshape(tok_rows, head_count * KW).astype(jnp.bfloat16)
    )
    joined = jnp.concatenate([act_grad, kernel.reshape(tok_rows, head_count * KW)], axis=1)
    joined_pad = with_halo(joined.astype(jnp.bfloat16), (("seq", 0),), tap_reach).astype(
        joined.dtype
    )
    grad_pad = joined_pad[:, :feat_width].reshape(tok_rows + 2 * tap_reach, head_count, head_width)
    kernel_pad = joined_pad[:, feat_width:].reshape(tok_rows + 2 * tap_reach, head_count, KW)
    conv_back = jnp.zeros((tok_rows, head_count, head_width), jnp.float32)
    for tap_index in range(KW):
        lower = 2 * tap_reach - tap_index
        conv_back = (
            conv_back
            + kernel_pad[lower : lower + tok_rows, :, tap_index, None]
            * grad_pad[lower : lower + tok_rows]
        )
    gen_part = lax.dot_general(
        full_hidden, logit_grad, (((0,), (0,)), ((), ())), preferred_element_type=jnp.float32
    )
    gen_back = (
        lax.psum_scatter(
            lax.dot_general(
                gen_weight, logit_grad, (((1,), (1,)), ((), ())), preferred_element_type=jnp.float32
            ).astype(jnp.bfloat16),
            "tp",
            scatter_dimension=0,
            tiled=True,
        )
        .astype(jnp.float32)
        .T
    )
    hidden_grad = act_grad + conv_back.reshape(tok_rows, feat_width) + gen_back
    embed_grad = jnp.where(masked, jnp.float32(0.0), hidden_grad)
    table_part = jnp.dot(
        onehot.astype(jnp.float32).T,
        jnp.where(masked, hidden_grad, jnp.float32(0.0)),
        precision=lax.Precision.HIGHEST,
    )
    gen_sum, table_grad = (
        lax.psum(gen_part.astype(jnp.bfloat16), "seq").astype(jnp.float32),
        lax.psum(table_part.astype(jnp.bfloat16), "seq").astype(jnp.float32),
    )
    return (layer_output, embed_grad, table_grad, gen_sum, up_grad, down_grad)


def solution(mesh):
    placed = (
        P("seq", "tp"),
        P("seq"),
        P("seq"),
        P(None, "tp"),
        P(None, "tp"),
        P(None, "tp"),
        P("tp", None),
        P("seq", "tp"),
    )
    return jax.shard_map(
        body,
        mesh=mesh,
        in_specs=placed,
        out_specs=(
            P("seq", "tp"),
            P("seq", "tp"),
            P(None, "tp"),
            P(None, "tp"),
            P("seq", "tp"),
            P("tp", "seq"),
        ),
        check_vma=False,
    )
```

profile of v0, /device:TPU:0, one launch (start us, length us, event | category | flops | bytes accessed | tf_op | source)
XLA Modules:
  0.0 786.1 jit_solution(15642379624280598113)
XLA Ops:
  7.9 2.1 fusion.11
  14.2 63.1 %all-gather.4.cloned.1.call-done = bf16[384,4096]{1,0:T(8,128)(2,1)} async-done(((bf16[384,512]{1,0:T(8,128)(2,1)}), bf16[384,4096]{1,0:T(8,128)(2,1)}) %all-gather.4.cloned.1.call-update) | async-done | bytes 3145744 | tf_op jit(solution)/shard_map/all_gather | solution.py:48
  77.3 2.9 convolution_exponential_fusion
  91.1 2.5 fusion.45
  93.8 47.6 %all-gather.8.cloned.1.call-done = bf16[384,4096]{1,0:T(8,128)(2,1)} async-done(((bf16[384,512]{1,0:T(8,128)(2,1)}), bf16[384,4096]{1,0:T(8,128)(2,1)}) %all-gather.8.cloned.1.call-update) | async-done | bytes 3145744 | tf_op jit(solution)/shard_map/all_gather | solution.py:76
  141.4 6.8 fusion.69
  148.3 57.8 %all-gather.6.cloned.1.call-done = bf16[384,4096]{1,0:T(8,128)(2,1)} async-done(((bf16[384,512]{1,0:T(8,128)(2,1)}), bf16[384,4096]{1,0:T(8,128)(2,1)}) %all-gather.6.cloned.1.call-update) | async-done | bytes 3145744 | tf_op jit(solution)/shard_map/all_gather | solution.py:60
  206.1 9.7 %fusion.10 = (bf16[384,1024]{1,0:T(8,128)(2,1)S(1)}, f32[384,1024]{1,0:T(8,128)}) fusion(f32[384,1024]{1,0:T(8,128)S(1)} %fusion.69, bf16[384,4096]{1,0:T(8,128)(2,1)} %all-gather.6.cloned.1.call-done, bf16[4096,1024]{1,0:T(8,128)(2,1)} %param.13), kind=kOutput, calls=%fused_computation.18 | convolution fusion | flops 3229089792 | bytes 15466496 | tf_op jit(solution)/shard_map/dot_general | solution.py:62
  215.7 10.6 %fusion.2 = bf16[4096,384]{0,1:T(8,128)(2,1)} fusion(bf16[384,1024]{1,0:T(8,128)(2,1)S(1)} %get-tuple-element.62, bf16[4096,1024]{1,0:T(8,128)(2,1)} %param.13), kind=kOutput, calls=%fused_computation.7 | convolution fusion | flops 3222798336 | bytes 12320768 | tf_op jit(solution)/shard_map/dot_general | solution.py:100
  226.9 76.9 %reduce-scatter.8.cloned.1.call-done = bf16[512,384]{0,1:T(8,128)(2,1)} async-done(((bf16[4096,384]{0,1:T(8,128)(2,1)}), bf16[512,384]{0,1:T(8,128)(2,1)}) %reduce-scatter.8.cloned.1.call-update) | async-done | bytes 393232 | tf_op jit(solution)/shard_map/reduce_scatter | solution.py:99
  303.8 3.5 convert_multiply_fusion.16
  311.8 1.7 mul.669
  316.2 1.7 mul.673
  321.8 2.7 convert_multiply_fusion.2
  326.7 1.7 mul.683
  335.8 1.7 mul.691
  340.6 2.7 fusion.3
  344.7 8.3 %fusion.1 = bf16[4096,384]{0,1:T(8,128)(2,1)} fusion(bf16[1024,4096]{1,0:T(8,128)(2,1)} %param.14, f32[384,1024]{1,0:T(8,128)S(1)} %copy-done.18), kind=kOutput, calls=%fused_computation.6 | convolution fusion | flops 3226337280 | bytes 13107200 | tf_op jit(solution)/shard_map/dot_general | solution.py:68
  358.4 1.9 collective-permute-done.3
  387.8 33.8 %reduce-scatter.10.cloned.1.call-done = bf16[512,384]{0,1:T(8,128)(2,1)} async-done(((bf16[4096,384]{0,1:T(8,128)(2,1)}), bf16[512,384]{0,1:T(8,128)(2,1)}) %reduce-scatter.10.cloned.1.call-update) | async-done | bytes 393232 | tf_op jit(solution)/shard_map/reduce_scatter | solution.py:138
  421.6 5.9 broadcast_select_fusion
  429.1 10.3 %convolution_convert_fusion = bf16[1024,4096]{1,0:T(8,128)(2,1)} fusion(bf16[384,4096]{1,0:T(8,128)(2,1)} %all-gather.8.cloned.1.call-done, f32[384,1024]{1,0:T(8,128)} %get-tuple-element.63), kind=kOutput, calls=%fused_computation.1 | convolution fusion | flops 3228958720 | bytes 13107200 | tf_op jit(solution)/shard_map/dot_general | solution.py:81
  439.5 1.8 copy-done.17
  441.4 7.9 %convolution_convert_fusion.1 = bf16[4096,1024]{1,0:T(8,128)(2,1)} fusion(bf16[384,4096]{1,0:T(8,128)(2,1)S(1)} %copy-done.17, bf16[384,1024]{1,0:T(8,128)(2,1)} %copy-done.19), kind=kOutput, calls=%fused_computation.2 | convolution fusion | flops 3225419776 | bytes 12320768 | tf_op jit(solution)/shard_map/dot_general | solution.py:91
  449.2 54.4 %reduce-scatter.6.cloned.1.call-done = bf16[512,384]{0,1:T(8,128)(2,1)} async-done(((bf16[4096,384]{0,1:T(8,128)(2,1)}), bf16[512,384]{0,1:T(8,128)(2,1)}) %reduce-scatter.6.cloned.1.call-update) | async-done | bytes 393232 | tf_op jit(solution)/shard_map/reduce_scatter | solution.py:67
  503.6 1.8 fusion.43
  505.5 117.2 %all-reduce.3.cloned.1.call-done = (bf16[100,512]{1,0:T(8,128)(2,1)}, bf16[4096,30]{0,1:T(8,128)(2,1)}) async-done(((bf16[100,512]{1,0:T(8,128)(2,1)}, bf16[4096,30]{0,1:T(8,128)(2,1)}), (bf16[100,512]{1,0:T(8,128)(2,1)}, bf16[4096,30]{0,1:T(8,128)(2,1)})) %all-reduce.3.cloned.1.call-update) | async-done | bytes 348176 | tf_op jit(solution)/shard_map/psum | solution.py:158
  624.2 1.8 convert_element_type.199
  626.1 75.2 %reduce-scatter.14.cloned.1.call-done = bf16[1024,256]{1,0:T(8,128)(2,1)} async-done(((bf16[1024,4096]{1,0:T(8,128)(2,1)}), bf16[1024,256]{1,0:T(8,128)(2,1)}) %reduce-scatter.14.cloned.1.call-update) | async-done | bytes 524304 | tf_op jit(solution)/shard_map/reduce_scatter | solution.py:86
  701.3 2.1 convert_element_type.203
  703.4 73.6 %reduce-scatter.12.cloned.1.call-done = bf16[256,1024]{1,0:T(8,128)(2,1)} async-done(((bf16[4096,1024]{1,0:T(8,128)(2,1)}), bf16[256,1024]{1,0:T(8,128)(2,1)}) %reduce-scatter.12.cloned.1.call-update) | async-done | bytes 524304 | tf_op jit(solution)/shard_map/reduce_scatter | solution.py:90
  777.0 2.1 convert_element_type.201
  (217 shorter events, 77.1 us)
Async XLA Ops:
  7.2 70.2 %copy-start = (bf16[4096,30]{0,1:T(8,128)(2,1)S(1)}, bf16[4096,30]{0,1:T(8,128)(2,1)}, u32[]{:S(2)}) copy-start(bf16[4096,30]{0,1:T(8,128)(2,1)} %param.12) | copy-start | bytes 737284
  7.2 70.2 %all-gather.4.cloned.1.call-start = ((), (), s32[]{:S(2)}) async-start(), calls=%async_computation.5 | async-start | bytes 3538944 | tf_op jit(solution)/shard_map/all_gather | solution.py:48
  10.1 131.3 %all-gather.8.cloned.1.call-start = ((), (), s32[]{:S(2)}) async-start(), calls=%async_computation.8 | async-start | bytes 3538944 | tf_op jit(solution)/shard_map/all_gather | solution.py:76
  10.9 195.2 %all-gather.6.cloned.1.call-start = ((), (), s32[]{:S(2)}) async-start(), calls=%async_computation.6 | async-start | bytes 3538944 | tf_op jit(solution)/shard_map/all_gather | solution.py:60
  11.6 79.0 %collective-permute-start = (bf16[7,512]{1,0:T(8,128)(2,1)S(1)}, bf16[7,512]{1,0:T(8,128)(2,1)S(1)}, u32[]{:S(2)}, u32[]{:S(2)}) collective-permute-start(bf16[7,512]{1,0:T(8,128)(2,1)S(1)} %get-tuple-element.28), channel_id=1, source_target_pairs={{0,8},{8,16},{16,24},{24,32},{32,40},{40,48},{48,56},{56,64},{64,7... | collective-permute-start | bytes 21512 | tf_op jit(solution)/shard_map/ppermute | solution.py:15
  12.9 77.7 %collective-permute-start.1 = (bf16[7,512]{1,0:T(8,128)(2,1)S(1)}, bf16[7,512]{1,0:T(8,128)(2,1)S(1)}, u32[]{:S(2)}, u32[]{:S(2)}) collective-permute-start(bf16[7,512]{1,0:T(8,128)(2,1)S(1)} %get-tuple-element.29), channel_id=1, source_target_pairs={{8,0},{16,8},{24,16},{32,24},{40,32},{48,40},{56,48},{64,56},{72,6... | collective-permute-start | bytes 21512 | tf_op jit(solution)/shard_map/ppermute | solution.py:18
  90.1 1.0 copy-start.3
  93.6 210.2 %reduce-scatter.8.cloned.1.call-start = ((), (), s32[]{:S(2)}) async-start(), calls=%async_computation.9 | async-start | bytes 3538944 | tf_op jit(solution)/shard_map/reduce_scatter | solution.py:99
  215.7 10.6 %copy-start.19 = (bf16[384,1024]{1,0:T(8,128)(2,1)}, bf16[384,1024]{1,0:T(8,128)(2,1)S(1)}, u32[]{:S(2)}) copy-start(bf16[384,1024]{1,0:T(8,128)(2,1)S(1)} %get-tuple-element.62) | copy-start | bytes 2359300
  226.4 77.4 %copy-start.4 = (bf16[384,512]{1,0:T(8,128)(2,1)S(1)}, bf16[384,512]{1,0:T(8,128)(2,1)}, u32[]{:S(2)}) copy-start(bf16[384,512]{1,0:T(8,128)(2,1)} %param.15) | copy-start | bytes 1179652
  226.4 195.2 %reduce-scatter.10.cloned.1.call-start = ((), (), s32[]{:S(2)}) async-start(), calls=%async_computation.10 | async-start | bytes 3538944 | tf_op jit(solution)/shard_map/reduce_scatter | solution.py:138
  320.6 1.2 copy-start.7
  343.3 1.4 copy-start.18
  343.3 160.3 %reduce-scatter.6.cloned.1.call-start = ((), (), s32[]{:S(2)}) async-start(), calls=%async_computation.7 | async-start | bytes 3538944 | tf_op jit(solution)/shard_map/reduce_scatter | solution.py:67
  353.0 4.0 copy-start.2
  353.0 269.6 %all-reduce.3.cloned.1.call-start = ((), (), s32[]{:S(2)}) async-start(), calls=%async_computation.13 | async-start | bytes 737280 | tf_op jit(solution)/shard_map/psum | solution.py:158
  354.1 4.3 collective-permute-start.2
  355.4 5.0 copy-start.9
  355.4 4.9 collective-permute-start.3
  367.6 1.8 copy-start.14
  369.4 1.5 copy-start.13
  370.9 1.4 copy-start.12
  372.3 1.4 copy-start.11
  373.7 1.4 copy-start.10
  386.4 35.2 %copy-start.5 = (bf16[384,512]{1,0:T(8,128)(2,1)S(1)}, bf16[384,512]{1,0:T(8,128)(2,1)}, u32[]{:S(2)}) copy-start(bf16[384,512]{1,0:T(8,128)(2,1)} %param.15) | copy-start | bytes 1179652
  386.4 35.2 %copy-start.8 = (bf16[512,384]{0,1:T(8,128)(2,1)S(1)}, bf16[512,384]{0,1:T(8,128)(2,1)}, u32[]{:S(2)}) copy-start(bf16[512,384]{0,1:T(8,128)(2,1)} %reduce-scatter.8.cloned.1.call-done) | copy-start | bytes 1179652
  421.6 5.9 copy-start.16
  428.8 272.5 %reduce-scatter.14.cloned.1.call-start = ((), (), s32[]{:S(2)}) async-start(), calls=%async_computation.12 | async-start | bytes 8912896 | tf_op jit(solution)/shard_map/reduce_scatter | solution.py:86
  439.4 1.9 copy-start.17
  439.5 337.6 %reduce-scatter.12.cloned.1.call-start = ((), (), s32[]{:S(2)}) async-start(), calls=%async_computation.11 | async-start | bytes 8912896 | tf_op jit(solution)/shard_map/reduce_scatter | solution.py:90
  449.2 54.4 %copy-start.6 = (bf16[384,512]{1,0:T(8,128)(2,1)S(1)}, bf16[384,512]{1,0:T(8,128)(2,1)}, u32[]{:S(2)}) copy-start(bf16[384,512]{1,0:T(8,128)(2,1)} %fusion.45) | copy-start | bytes 1179652
  624.2 154.9 %copy-start.1 = (bf16[4096,30]{0,1:T(8,128)(2,1)S(1)}, bf16[4096,30]{0,1:T(8,128)(2,1)}, u32[]{:S(2)}) copy-start(bf16[4096,30]{0,1:T(8,128)(2,1)} %param.12) | copy-start | bytes 737284
  (1 other events, 0.9 us)
Sparse Core Ops, SparseCore 0:
  10.8 66.5 all-gather.3
  79.5 61.8 all-gather.7
  144.2 61.8 all-gather.5
  226.5 77.2 reduce-scatter.7
  343.4 78.1 reduce-scatter.9
  425.3 78.2 reduce-scatter.5
  506.7 115.8 all-reduce.2
  625.2 76.0 reduce-scatter.13
  703.9 73.1 reduce-scatter.11
where the time goes:
time: 795 us; the launch traced here: 786 us
  waiting for transfers between devices  602 us (76%)
  local copies, waits for them, and re-layouts  64.7 us (8%)
  matrix products  64 us (8%)
  other arithmetic  33.2 us (4%)
  between operations  15.1 us (2%)
    psum x1, waiting for transfers between devices, body(): lax.psum(table_part.astype(jnp.bfloat16), 'seq').astype(jnp.float32)  117 us
    reduce_scatter x1, waiting for transfers between devices, body(): lax.psum_scatter(lax.dot_general(up_rows, pre_grad, (((1,), (1,)), ((), (...  76.9 us
    reduce_scatter x1, waiting for transfers between devices, body(): lax.psum_scatter(down_term.astype(jnp.bfloat16), 'seq', scatter_dimension...  75.2 us
    reduce_scatter x1, waiting for transfers between devices, body(): lax.psum_scatter(lax.dot_general(full_copy, pre_grad, (((0,), (0,)), ((),...  73.6 us
    all_gather x1, waiting for transfers between devices, body(): full_hidden = lax.all_gather(hidden, 'tp', axis=1, tiled=True)  63.1 us
    all_gather x1, waiting for transfers between devices, body(): shard_piece = lax.all_gather(act, 'tp', axis=1, tiled=True)  57.8 us
    reduce_scatter x1, waiting for transfers between devices, body(): lax.psum_scatter(lax.dot_general(down_cols, middle, (((0,), (1,)), ((), (...  54.4 us
    all_gather x1, waiting for transfers between devices, body(): shard_piece = lax.all_gather(cotangent, 'tp', axis=1, tiled=True)  47.6 us
  transfers between devices with their start and end apart: 13, of which 10 were waited for; matrix products, arithmetic and copies ran while one was open for 12% of the time, Pallas kernels for 0%

commit v1 on v0

v1 whole, which is shorter than its diff:
```python
import functools

import jax
import jax.numpy as jnp
from jax import lax
from jax.experimental import pallas as pl
from jax.experimental.pallas import tpu as pltpu
from jax.sharding import PartitionSpec as P

KW = 15
REACH = 7
PAD = 8
ROWS = 32
F32 = jnp.float32
BF16 = jnp.bfloat16
NT = (((1,), (1,)), ((), ()))
TN = (((0,), (0,)), ((), ()))


def params(megabytes):
    return pltpu.CompilerParams(vmem_limit_bytes=megabytes << 20)


def flip(value, axis, bit):
    count = lax.axis_size(axis)
    return lax.ppermute(value, axis, [(i, i ^ bit) for i in range(count)])


def halo(value):
    count = lax.axis_size("seq")
    forward = [(i, i + 1) for i in range(count - 1)]
    backward = [(i + 1, i) for i in range(count - 1)]
    low = lax.ppermute(value[-PAD:], "seq", forward)
    high = lax.ppermute(value[:PAD], "seq", backward)
    return low, high


def exchange(blocks):
    shape = blocks.shape
    cube = blocks.reshape((2, 2, 2) + shape[1:])
    for place, bit in enumerate((4, 2, 1)):
        keep = lax.index_in_dim(cube, 0, place, keepdims=True)
        send = lax.index_in_dim(cube, 1, place, keepdims=True)
        cube = jnp.concatenate([keep, flip(send, "tp", bit)], axis=place)
    return cube.reshape(shape)


def reduce_blocks(blocks):
    half = blocks.shape[0] // 2
    while half:
        blocks = blocks[:half] + flip(blocks[half:], "tp", half)
        half //= 2
    return blocks[0]


def gather_small(value):
    blocks = value[None]
    for bit in (1, 2, 4):
        blocks = jnp.concatenate([blocks, flip(blocks, "tp", bit)], axis=0)
    return blocks


def sum_over_seq(value):
    for bit in (1, 2, 4, 8):
        sent = value.astype(BF16)
        value = sent.astype(F32) + flip(sent, "seq", bit).astype(F32)
    return value


def gather_pieces(value):
    half = value.shape[0] // 2
    four = flip(value, "tp", 4)
    one = flip(value, "tp", 1)
    three = flip(value, "tp", 3)
    five = flip(four, "tp", 1)
    seven = flip(four, "tp", 3)
    two_a = flip(one[:half], "tp", 3)
    two_b = flip(three[half:], "tp", 1)
    six_a = flip(five[:half], "tp", 3)
    six_b = flip(seven[half:], "tp", 1)
    return value, one, three, four, five, seven, two_a, two_b, six_a, six_b


def conv_forward_kernel(logit_ref, hidden_ref, low_ref, high_ref, act_ref, tap_ref, padded):
    rows = hidden_ref.shape[0]
    width = hidden_ref.shape[1]
    heads = 2
    exps = jnp.exp(logit_ref[...])
    first = exps[0:KW]
    second = exps[KW : 2 * KW]
    first = first / jnp.sum(first, axis=0, keepdims=True)
    second = second / jnp.sum(second, axis=0, keepdims=True)
    blank = jnp.zeros((ROWS - 2 * KW, rows), F32)
    tap_ref[...] = jnp.concatenate([first, second, blank], axis=0).T
    padded[0:PAD] = low_ref[...].astype(F32)
    padded[PAD : PAD + rows] = hidden_ref[...].astype(F32)
    padded[PAD + rows :] = high_ref[...].astype(F32)
    step = 32
    head_width = width // heads

    def run(index, carry):
        base = pl.multiple_of(index * step, step)
        taps = tap_ref[pl.ds(base, step), :]
        for head in range(heads):
            lanes = slice(head * head_width, (head + 1) * head_width)
            window = padded[pl.ds(base, step + 2 * PAD), lanes]
            total = jnp.zeros((step, head_width), F32)
            for tap in range(KW):
                column = head * KW + tap
                total = total + taps[:, column : column + 1] * window[tap + 1 : tap + 1 + step]
            act_ref[pl.ds(base, step), lanes] = (window[PAD : PAD + step] + total).astype(BF16)
        return carry

    lax.fori_loop(0, rows // step, run, 0)


def conv_forward(logits, hidden, low, high):
    rows, width = hidden.shape
    return pl.pallas_call(
        conv_forward_kernel,
        out_shape=(
            jax.ShapeDtypeStruct((rows, width), BF16),
            jax.ShapeDtypeStruct((rows, ROWS), F32),
        ),
        scratch_shapes=[pltpu.VMEM((rows + 2 * PAD, width), F32)],
        name="conv_forward",
    )(logits, hidden, low, high)


def grad_middle_kernel(cot_ref, down_ref, out_ref):
    width = cot_ref.shape[2]
    total = jnp.zeros(out_ref.shape, F32)
    for piece in range(cot_ref.shape[0]):
        total = total + lax.dot_general(
            cot_ref[piece],
            down_ref[:, piece * width : (piece + 1) * width],
            NT,
            preferred_element_type=F32,
        )
    out_ref[...] = total


def grad_middle(cot_full, down_weight):
    pieces, rows, width = cot_full.shape
    units = down_weight.shape[0]
    block = 256
    return pl.pallas_call(
        grad_middle_kernel,
        grid=(units // block,),
        in_specs=[
            pl.BlockSpec((pieces, rows, width), lambda i: (0, 0, 0)),
            pl.BlockSpec((block, pieces * width), lambda i: (i, 0)),
        ],
        out_specs=pl.BlockSpec((rows, block), lambda i: (0, i)),
        out_shape=jax.ShapeDtypeStruct((rows, units), F32),
        compiler_params=params(40),
        name="grad_middle",
    )(cot_full, down_weight)


def up_kernel(order, *refs):
    pieces = refs[:10]
    up_ref, grad_ref, full_ref, middle_ref, pre_grad_ref = refs[10:]
    half = full_ref.shape[1] // 2
    width = full_ref.shape[2]

    @pl.when(pl.program_id(0) == 0)
    def _():
        for at, ref in zip((0, 1, 3, 4, 5, 7), pieces[:6]):
            full_ref[order[at]] = ref[...]
        full_ref[order[2], 0:half] = pieces[6][...]
        full_ref[order[2], half:] = pieces[7][...]
        full_ref[order[6], 0:half] = pieces[8][...]
        full_ref[order[6], half:] = pieces[9][...]

    pre = jnp.zeros(middle_ref.shape, F32)
    for piece in range(full_ref.shape[0]):
        pre = pre + jnp.dot(
            full_ref[piece],
            up_ref[piece * width : (piece + 1) * width, :],
            preferred_element_type=F32,
        )
    scale = 0.7978845608028654
    square = pre * pre
    bent = jnp.tanh(scale * (pre + 0.044715 * (square * pre)))
    middle_ref[...] = (0.5 * pre * (1.0 + bent)).astype(BF16)
    slope = 0.5 * (1.0 + bent) + 0.5 * pre * (1.0 - bent * bent) * (
        scale * (1.0 + 3.0 * 0.044715 * square)
    )
    pre_grad_ref[...] = (grad_ref[...] * slope).astype(BF16)


def up_project(order, pieces, up_weight, middle_grad):
    rows, width = pieces[0].shape
    depth, units = up_weight.shape
    block = 256
    whole = [pl.BlockSpec(p.shape, lambda i, o: (0, 0)) for p in pieces]
    return pl.pallas_call(
        up_kernel,
        grid_spec=pltpu.PrefetchScalarGridSpec(
            num_scalar_prefetch=1,
            grid=(units // block,),
            in_specs=whole
            + [
                pl.BlockSpec((depth, block), lambda i, o: (0, i)),
                pl.BlockSpec((rows, block), lambda i, o: (0, i)),
            ],
            out_specs=[
                pl.BlockSpec((depth // width, rows, width), lambda i, o: (0, 0, 0)),
                pl.BlockSpec((rows, block), lambda i, o: (0, i)),
                pl.BlockSpec((rows, block), lambda i, o: (0, i)),
            ],
        ),
        out_shape=(
            jax.ShapeDtypeStruct((depth // width, rows, width), BF16),
            jax.ShapeDtypeStruct((rows, units), BF16),
            jax.ShapeDtypeStruct((rows, units), BF16),
        ),
        compiler_params=params(48),
        name="up_project",
    )(order, *pieces, up_weight, middle_grad)


def spread_kernel(dims, order, value_ref, weight_ref, *out_refs):
    result = lax.dot_general(
        value_ref[...], weight_ref[...], dims, preferred_element_type=F32
    ).astype(BF16)
    for index, ref in enumerate(out_refs):

        @pl.when(pl.program_id(0) == index)
        def _(ref=ref):
            ref[...] = result


def spread(order, value, weight, transposed, name):
    rows, units = value.shape
    if transposed:
        width = weight.shape[0] // 8
        spec = pl.BlockSpec((width, units), lambda k, o: (o[k], 0))
        dims = NT
    else:
        width = weight.shape[1] // 8
        spec = pl.BlockSpec((units, width), lambda k, o: (0, o[k]))
        dims = (((1,), (0,)), ((), ()))
    return pl.pallas_call(
        functools.partial(spread_kernel, dims),
        grid_spec=pltpu.PrefetchScalarGridSpec(
            num_scalar_prefetch=1,
            grid=(8,),
            in_specs=[pl.BlockSpec((rows, units), lambda k, o: (0, 0)), spec],
            out_specs=[pl.BlockSpec((rows, width), lambda k, o: (0, 0))] * 8,
        ),
        out_shape=[jax.ShapeDtypeStruct((rows, width), BF16)] * 8,
        compiler_params=params(40),
        name=name,
    )(order, value, weight)


def weight_grads_kernel(act_ref, cot_ref, pre_grad_ref, middle_ref, out_ref):
    up = lax.dot_general(act_ref[0], pre_grad_ref[...], TN, preferred_element_type=F32)
    down = lax.dot_general(cot_ref[0], middle_ref[...], TN, preferred_element_type=F32)
    chunk = out_ref.shape[1] // 2
    for index in range(out_ref.shape[0]):
        rows = slice(index * chunk, (index + 1) * chunk)
        out_ref[index, 0:chunk] = up[rows].astype(BF16)
        out_ref[index, chunk:] = down[rows].astype(BF16)


def weight_grads(act_full, cot_full, pre_grad, middle):
    pieces, rows, width = act_full.shape
    units = middle.shape[1]
    chunks = lax.axis_size("seq")
    per = chunks // pieces
    chunk = width // per
    return pl.pallas_call(
        weight_grads_kernel,
        grid=(pieces,),
        in_specs=[
            pl.BlockSpec((1, rows, width), lambda i: (i, 0, 0)),
            pl.BlockSpec((1, rows, width), lambda i: (i, 0, 0)),
            pl.BlockSpec((rows, units), lambda i: (0, 0)),
            pl.BlockSpec((rows, units), lambda i: (0, 0)),
        ],
        out_specs=pl.BlockSpec((per, 2 * chunk, units), lambda i: (i, 0, 0)),
        out_shape=jax.ShapeDtypeStruct((chunks, 2 * chunk, units), BF16),
        compiler_params=params(40),
        name="weight_grads",
    )(act_full, cot_full, pre_grad, middle)


def kernel_grad_kernel(*refs):
    terms = refs[:8]
    cot_ref, hidden_ref, low_ref, high_ref, tap_ref, grad_ref, logit_ref, padded = refs[8:]
    rows, width = hidden_ref.shape
    heads = 2
    head_width = width // heads
    padded[0:PAD] = low_ref[...].astype(F32)
    padded[PAD : PAD + rows] = hidden_ref[...].astype(F32)
    padded[PAD + rows :] = high_ref[...].astype(F32)
    step = 32
    lane = lax.broadcasted_iota(jnp.int32, (step, ROWS), 1)

    def run(index, carry):
        base = pl.multiple_of(index * step, step)
        at = pl.ds(base, step)
        grad = terms[0][at, :].astype(F32)
        for ref in terms[1:]:
            grad = grad + ref[at, :].astype(F32)
        grad = grad + cot_ref[at, :].astype(F32)
        grad_ref[at, :] = grad
        taps = tap_ref[at, :]
        found = jnp.zeros((step, ROWS), F32)
        for head in range(heads):
            lanes = slice(head * head_width, (head + 1) * head_width)
            window = padded[pl.ds(base, step + 2 * PAD), lanes]
            part = grad[:, lanes]
            for tap in range(KW):
                column = head * KW + tap
                value = jnp.sum(part * window[tap + 1 : tap + 1 + step], axis=1, keepdims=True)
                found = jnp.where(lane == column, value, found)
        product = taps * found
        in_first = lane < KW
        one = jnp.sum(jnp.where(in_first, product, 0.0), axis=1, keepdims=True)
        two = jnp.sum(jnp.where(in_first, 0.0, product), axis=1, keepdims=True)
        logit_ref[at, :] = taps * (found - jnp.where(in_first, one, two))
        return carry

    lax.fori_loop(0, rows // step, run, 0)


def kernel_grads(terms, cotangent, hidden, low, high, taps):
    rows, width = hidden.shape
    return pl.pallas_call(
        kernel_grad_kernel,
        out_shape=(
            jax.ShapeDtypeStruct((rows, width), F32),
            jax.ShapeDtypeStruct((rows, ROWS), F32),
        ),
        scratch_shapes=[pltpu.VMEM((rows + 2 * PAD, width), F32)],
        compiler_params=params(32),
        name="kernel_grads",
    )(*terms, cotangent, hidden, low, high, taps)


def hidden_grad_kernel(
    grad_ref,
    glow_ref,
    ghigh_ref,
    tap_ref,
    tlow_ref,
    thigh_ref,
    logit_ref,
    gen_ref,
    mask_ref,
    code_ref,
    embed_ref,
    table_ref,
    padded,
    tapped,
    back,
):
    rows, width = grad_ref.shape
    heads = 2
    head_width = width // heads
    padded[0:PAD] = glow_ref[...].astype(F32)
    padded[PAD : PAD + rows] = grad_ref[...]
    padded[PAD + rows :] = ghigh_ref[...].astype(F32)
    tapped[0:PAD] = tlow_ref[...]
    tapped[PAD : PAD + rows] = tap_ref[...]
    tapped[PAD + rows :] = thigh_ref[...]
    back[...] = lax.dot_general(logit_ref[...], gen_ref[...], TN, preferred_element_type=F32)
    step = 32

    def run(index, carry):
        base = pl.multiple_of(index * step, step)
        at = pl.ds(base, step)
        picked = mask_ref[at, :] == 1
        taps = tapped[pl.ds(base, step + 2 * PAD), :]
        for head in range(heads):
            lanes = slice(head * head_width, (head + 1) * head_width)
            window = padded[pl.ds(base, step + 2 * PAD), lanes]
            total = window[PAD : PAD + step] + back[at, lanes]
            for tap in range(KW):
                column = head * KW + tap
                lower = 2 * PAD - 1 - tap
                total = (
                    total
                    + taps[lower : lower + step, column : column + 1]
                    * window[lower : lower + step]
                )
            embed_ref[at, lanes] = jnp.where(picked, 0.0, total)
            back[at, lanes] = jnp.where(picked, total, 0.0)
        return carry

    lax.fori_loop(0, rows // step, run, 0)
    codes = lax.broadcasted_iota(jnp.int32, (table_ref.shape[0], rows), 0)
    chosen = jnp.where(codes == code_ref[...], 1.0, 0.0).astype(BF16)
    value = back[...]
    upper = value.astype(BF16)
    lower = (value - upper.astype(F32)).astype(BF16)
    table_ref[...] = jnp.dot(chosen, upper, preferred_element_type=F32) + jnp.dot(
        chosen, lower, preferred_element_type=F32
    )


def hidden_grads(grad, glow, ghigh, taps, tlow, thigh, logit_full, gen_full, mask, code, codes):
    rows, width = grad.shape
    return pl.pallas_call(
        hidden_grad_kernel,
        out_shape=(
            jax.ShapeDtypeStruct((rows, width), F32),
            jax.ShapeDtypeStruct((codes, width), F32),
        ),
        scratch_shapes=[
            pltpu.VMEM((rows + 2 * PAD, width), F32),
            pltpu.VMEM((rows + 2 * PAD, ROWS), F32),
            pltpu.VMEM((rows, width), F32),
        ],
        compiler_params=params(32),
        name="hidden_grads",
    )(grad, glow, ghigh, taps, tlow, thigh, logit_full, gen_full, mask, code)


def place_kernel(order, blocks_ref, out_ref):
    width = blocks_ref.shape[2]
    for piece in range(blocks_ref.shape[0]):
        at = pl.multiple_of(order[piece] * width, width)
        out_ref[:, pl.ds(at, width)] = blocks_ref[piece, 0 : out_ref.shape[0]]


def place(order, blocks, rows):
    pieces, _, width = blocks.shape
    return pl.pallas_call(
        place_kernel,
        grid_spec=pltpu.PrefetchScalarGridSpec(
            num_scalar_prefetch=1,
            grid=(1,),
            in_specs=[pl.BlockSpec(blocks.shape, lambda i, o: (0, 0, 0))],
            out_specs=pl.BlockSpec((rows, pieces * width), lambda i, o: (0, 0)),
        ),
        out_shape=jax.ShapeDtypeStruct((rows, pieces * width), F32),
        name="place",
    )(order, blocks)


def body(
    embeddings,
    span_mask,
    sentinel_id,
    sentinel_table,
    gen_weight,
    up_weight,
    down_weight,
    cotangent,
):
    rows, width = embeddings.shape
    codes = sentinel_table.shape[0]
    members = lax.axis_size("tp")
    me = lax.axis_index("tp")
    order = jnp.arange(members, dtype=jnp.int32) ^ me.astype(jnp.int32)

    columns = gen_weight.shape[1]
    gen_rows = jnp.pad(gen_weight.T, ((0, ROWS - columns), (0, 0)))
    gen_own = jnp.stack(
        [
            lax.dynamic_slice(gen_rows, (jnp.int32(0), order[k] * width), (ROWS, width))
            for k in range(members)
        ]
    )
    gen_full = exchange(gen_own).reshape(members * ROWS, width)
    cot_full = lax.all_gather(cotangent, "tp", axis=0, tiled=False)

    sentinel_codes = jnp.arange(codes, dtype=jnp.int32)
    onehot = (sentinel_id[:, None] == sentinel_codes[None, :]).astype(BF16)
    picked = jnp.dot(onehot, sentinel_table, preferred_element_type=F32).astype(BF16)
    hidden = jnp.where(span_mask[:, None] == 1, picked, embeddings)
    low, high = halo(hidden)

    logit_part = lax.dot_general(gen_full, hidden, NT, preferred_element_type=F32)
    logits = reduce_blocks(logit_part.reshape(members, ROWS, rows))
    act, taps = conv_forward(logits, hidden, low, high)
    tap_low, tap_high = halo(taps)

    pieces = gather_pieces(act)
    middle_grad = grad_middle(cot_full, down_weight)
    act_full, middle, pre_grad = up_project(order, pieces, up_weight, middle_grad)

    back_terms = spread(order, pre_grad, up_weight, True, "act_back")
    back_terms = [back_terms[0]] + [flip(back_terms[k], "tp", k) for k in range(1, members)]
    summed = weight_grads(act_full, cot_full, pre_grad, middle)
    summed = lax.psum_scatter(summed, "seq", scatter_dimension=0, tiled=False)

    grad, logit_grad = kernel_grads(back_terms, cotangent, hidden, low, high, taps)
    grad_low, grad_high = halo(grad.astype(BF16))
    logit_full = gather_small(logit_grad.astype(BF16).T)
    logit_full = logit_full.reshape(members * ROWS, rows)
    embed_grad, table_part = hidden_grads(
        grad,
        grad_low,
        grad_high,
        taps,
        tap_low,
        tap_high,
        logit_full,
        gen_full,
        span_mask[:, None],
        sentinel_id[None, :],
        codes,
    )
    gen_part = jnp.dot(logit_full, hidden, preferred_element_type=F32).astype(BF16)
    gen_part = exchange(gen_part.reshape(members, ROWS, width)).astype(F32)
    gen_sum = sum_over_seq(gen_part)
    table_grad = sum_over_seq(table_part)
    gen_grad = place(order, gen_sum, columns).T

    terms = spread(order, middle, down_weight, False, "ffn_out")
    total = terms[0].astype(F32)
    for k in range(1, members):
        total = total + flip(terms[k], "tp", k).astype(F32)
    layer_output = (act.astype(F32) + total).astype(BF16)

    chunk = summed.shape[0] // 2
    up_grad = summed[:chunk].astype(F32)
    down_grad = summed[chunk:].astype(F32).T
    return (layer_output, embed_grad, table_grad, gen_grad, up_grad, down_grad)


def solution(mesh):
    placed = (
        P("seq", "tp"),
        P("seq"),
        P("seq"),
        P(None, "tp"),
        P(None, "tp"),
        P(None, "tp"),
        P("tp", None),
        P("seq", "tp"),
    )
    return jax.shard_map(
        body,
        mesh=mesh,
        in_specs=placed,
        out_specs=(
            P("seq", "tp"),
            P("seq", "tp"),
            P(None, "tp"),
            P(None, "tp"),
            P("seq", "tp"),
            P("tp", "seq"),
        ),
        check_vma=False,
    )
```

time: 795 us -> 357 us (0.45)
  waiting for transfers between devices: 602 us -> 141 us
  starting transfers between devices: 6.72 us -> 101 us
  matrix products: 64 us -> 1.92 us
  Pallas kernels: 0 us -> 53.3 us
  local copies, waits for them, and re-layouts: 64.7 us -> 30.4 us
  other arithmetic: 33.2 us -> 7.1 us
    reduce_scatter x5 -> x1, waiting for transfers between devices: 314 us -> 0.01 us  [body(): summed = lax.psum_scatter(summed, 'seq', scatter_dimension=0, tiled=False)]
    all_gather x3 -> x1, waiting for transfers between devices: 169 us -> 0.01 us  [body(): cot_full = lax.all_gather(cotangent, 'tp', axis=0, tiled=False)]
    ppermute x4 -> x49, waiting for transfers between devices: 1.95 us -> 141 us  [the longest x43 136 us: flip(): return lax.ppermute(value, axis, [(i, i ^ bit) for i in range(count)])]
    psum x1 -> x0, waiting for transfers between devices: 117 us -> none  [body(): lax.psum(table_part.astype(jnp.bfloat16), 'seq').astype(jnp.float32)]
    ppermute x4 -> x49, starting transfers between devices: 5.48 us -> 101 us  [the longest x43 90.7 us: flip(): return lax.ppermute(value, axis, [(i, i ^ bit) for i in range(count)])]
    dot_general x11 -> x3, matrix products: 64 us -> 1.92 us  [the longest x1 1.32 us: body(): jnp.dot(onehot, sentinel_table, preferred_element_type=F32).astype(BF16)]
    pallas_call x0 -> x9, Pallas kernels: none -> 53.3 us  [the longest x2 12.4 us: spread(): pl.pallas_call(functools.partial(spread_kernel, dims), grid_spec=pltpu.Pr...]
    mul x75 -> x0, local copies, waits for them, and re-layouts: 43.8 us -> none  [the longest x15 21.4 us: body(): act_three * padded[tap_index:tap_index + tok_rows]]
  transfers between devices with their start and end apart: 13 -> 51, of which waited for: 10 -> 25; matrix products, arithmetic and copies ran while one was open for 12% -> 3% of each run, Pallas kernels for 0% -> 9%
where the time goes in v1:
time: 357 us; the launch traced here: 355 us
  waiting for transfers between devices  141 us (39%)
  starting transfers between devices  101 us (28%)
  Pallas kernels  53.3 us (15%)
  local copies, waits for them, and re-layouts  30.4 us (9%)
  between operations  19.8 us (6%)
  other arithmetic  7.1 us (2%)
    ppermute x43, waiting for transfers between devices, flip(): return lax.ppermute(value, axis, [(i, i ^ bit) for i in range(count)])  136 us
    ppermute x43, starting transfers between devices, flip(): return lax.ppermute(value, axis, [(i, i ^ bit) for i in range(count)])  90.7 us
    unnamed x67, local copies, waits for them, and re-layouts  25.6 us
    pallas_call x2, Pallas kernels, spread(): pl.pallas_call(functools.partial(spread_kernel, dims), grid_spec=pltpu.Pr...  12.4 us
    pallas_call x1, Pallas kernels, weight_grads(): pl.pallas_call(weight_grads_kernel, grid=(pieces,), in_specs=[pl.BlockSpe...  11.9 us
    pallas_call x1, Pallas kernels, up_project(): pl.pallas_call(up_kernel, grid_spec=pltpu.PrefetchScalarGridSpec(num_scal...  8.9 us
  transfers between devices with their start and end apart: 51, of which 25 were waited for; matrix products, arithmetic and copies ran while one was open for 3% of the time, Pallas kernels for 9%

profile of v1, /device:TPU:0, one launch (start us, length us, event | category | flops | bytes accessed | tf_op | source)
XLA Modules:
  0.0 355.4 jit_solution(12154261908013670979)
XLA Ops:
  21.6 4.2 %collective-permute-start.1 = (bf16[2,1,2,32,512]{4,3,2,1,0:T(8,128)(2,1)S(1)}, bf16[2,1,2,32,512]{4,3,2,1,0:T(8,128)(2,1)S(1)}, u32[]{:S(2)}, u32[]{:S(2)}) collective-permute-start(bf16[2,1,2,32,512]{4,3,2,1,0:T(8,128)(2,1)S(1)} %get-tuple-element.91), channel_id=1, source_target_pairs={{0,2},{1,3},{2,0},{3,1},{4,6},{5,7},{6,4},{7,5},{8,10},{9,11},{10,... | collective-permute-start | bytes 393224 | tf_op jit(solution)/shard_map/ppermute | solution.py:26
  26.5 4.4 %collective-permute-done.1 = bf16[2,1,2,32,512]{4,3,2,1,0:T(8,128)(2,1)S(1)} collective-permute-done((bf16[2,1,2,32,512]{4,3,2,1,0:T(8,128)(2,1)S(1)}, bf16[2,1,2,32,512]{4,3,2,1,0:T(8,128)(2,1)S(1)}, u32[]{:S(2)}, u32[]{:S(2)}) %collective-permute-start.1) | collective-permute-done | bytes 131104 | tf_op jit(solution)/shard_map/ppermute | solution.py:26
  33.3 4.1 %collective-permute-done.2 = bf16[2,2,1,32,512]{4,3,2,1,0:T(8,128)(2,1)S(1)} collective-permute-done((bf16[2,2,1,32,512]{4,3,2,1,0:T(8,128)(2,1)S(1)}, bf16[2,2,1,32,512]{4,3,2,1,0:T(8,128)(2,1)S(1)}, u32[]{:S(2)}, u32[]{:S(2)}) %collective-permute-start.2) | collective-permute-done | bytes 131104 | tf_op jit(solution)/shard_map/ppermute | solution.py:26
  45.0 4.2 %collective-permute-start.4 = (f32[2,32,384]{2,1,0:T(8,128)S(1)}, f32[2,32,384]{2,1,0:T(8,128)S(1)}, u32[]{:S(2)}, u32[]{:S(2)}) collective-permute-start(f32[2,32,384]{2,1,0:T(8,128)S(1)} %slice.181), channel_id=1, source_target_pairs={{0,2},{1,3},{2,0},{3,1},{4,6},{5,7},{6,4},{7,5},{8,10},{9,11},{10,... | collective-permute-start | bytes 294920 | tf_op jit(solution)/shard_map/ppermute | solution.py:26
  49.2 4.5 %collective-permute-done.4 = f32[2,32,384]{2,1,0:T(8,128)S(1)} collective-permute-done((f32[2,32,384]{2,1,0:T(8,128)S(1)}, f32[2,32,384]{2,1,0:T(8,128)S(1)}, u32[]{:S(2)}, u32[]{:S(2)}) %collective-permute-start.4) | collective-permute-done | bytes 98336 | tf_op jit(solution)/shard_map/ppermute | solution.py:26
  61.8 4.9 %conv_forward.1 = (bf16[384,512]{1,0:T(8,128)(2,1)}, f32[384,32]{1,0:T(8,128)}) custom-call(f32[32,384]{1,0:T(8,128)} %fusion.7.logit_ref, bf16[384,512]{1,0:T(8,128)(2,1)} %copy-done.7, bf16[8,512]{1,0:T(8,128)(2,1)} %copy-done.27, bf16[8,512]{1,0:T(8,128)(2,1)} %copy-done.29), custom_call_target="tpu_custom_call" | custom-call | tf_op jit(solution)/shard_map/conv_forward/pallas_call | solution.py:119
  73.3 5.1 %collective-permute-done.10.refs_3_ = bf16[384,512]{1,0:T(8,128)(2,1)S(1)} collective-permute-done((bf16[384,512]{1,0:T(8,128)(2,1)}, bf16[384,512]{1,0:T(8,128)(2,1)S(1)}, u32[]{:S(2)}, u32[]{:S(2)}) %collective-permute-start.10) | collective-permute-done | bytes 393248 | tf_op jit(solution)/shard_map/ppermute | solution.py:26
  79.1 4.5 %collective-permute-start.12 = (bf16[384,512]{1,0:T(8,128)(2,1)S(1)}, bf16[384,512]{1,0:T(8,128)(2,1)S(1)}, u32[]{:S(2)}, u32[]{:S(2)}) collective-permute-start(bf16[384,512]{1,0:T(8,128)(2,1)S(1)} %collective-permute-done.10.refs_3_), channel_id=1, source_target_pairs={{0,3},{1,2},{2,1},{3,0},{4,7},{5,6},{6,5},{7,4},{8,11},{9,10},{10,... | collective-permute-start | bytes 1179656 | tf_op jit(solution)/shard_map/ppermute | solution.py:26
  85.1 5.2 %collective-permute-done.11.refs_4_ = bf16[384,512]{1,0:T(8,128)(2,1)S(1)} collective-permute-done((bf16[384,512]{1,0:T(8,128)(2,1)S(1)}, bf16[384,512]{1,0:T(8,128)(2,1)S(1)}, u32[]{:S(2)}, u32[]{:S(2)}) %collective-permute-start.11) | collective-permute-done | bytes 393248 | tf_op jit(solution)/shard_map/ppermute | solution.py:26
  101.0 4.2 %grad_middle.1.refs_11_ = f32[384,1024]{1,0:T(8,128)S(1)} custom-call(bf16[8,384,512]{2,1,0:T(8,128)(2,1)S(1)} %bitcast.60, bf16[1024,4096]{1,0:T(8,128)(2,1)S(1)} %copy-done.3), custom_call_target="tpu_custom_call" | custom-call | tf_op jit(solution)/shard_map/grad_middle/pallas_call | solution.py:147
  114.8 8.9 %up_project.1 = (bf16[8,384,512]{2,1,0:T(8,128)(2,1)}, bf16[384,1024]{1,0:T(8,128)(2,1)S(1)}, bf16[384,1024]{1,0:T(8,128)(2,1)S(1)}) custom-call(s32[8]{0:T(128)S(1)} %iota_xor_fusion.order, bf16[384,512]{1,0:T(8,128)(2,1)S(1)} %copy-done.11, bf16[384,512]{1,0:T(8,128)(2,1)S(1)} %collective-permute-done.8.refs_1_, ...), custom_call_target="tpu_custom_call" | custom-call | tf_op jit(solution)/shard_map/up_project/pallas_call | solution.py:198
  125.6 11.9 %weight_grads.1 = bf16[16,512,1024]{2,1,0:T(8,128)(2,1)} custom-call(bf16[8,384,512]{2,1,0:T(8,128)(2,1)S(1)} %copy-done.10, bf16[8,384,512]{2,1,0:T(8,128)(2,1)S(1)} %bitcast.61, bf16[384,1024]{1,0:T(8,128)(2,1)S(1)} %get-tuple-element.41.value_ref.pre_grad_ref, bf16[384,1024]{1,0:T(8,128)(2,1)S(1)} %get-tuple-element.32.value_ref.middle_ref), custom_call_target="tpu_custom_call" | custom-call | tf_op jit(solution)/shard_map/weight_grads/pallas_call | solution.py:275
  141.0 6.0 %act_back.1 = (bf16[384,512]{1,0:T(8,128)(2,1)S(1)}, bf16[384,512]{1,0:T(8,128)(2,1)S(1)}, bf16[384,512]{1,0:T(8,128)(2,1)S(1)}, bf16[384,512]{1,0:T(8,128)(2,1)...) custom-call(s32[8]{0:T(128)S(1)} %iota_xor_fusion.order, ...), custom_call_target="tpu_custom_call" | custom-call | tf_op jit(solution)/shard_map/act_back/pallas_call | solution.py:245
  154.4 4.7 %collective-permute-done.24.refs_1_ = bf16[384,512]{1,0:T(8,128)(2,1)S(1)} collective-permute-done((bf16[384,512]{1,0:T(8,128)(2,1)S(1)}, bf16[384,512]{1,0:T(8,128)(2,1)S(1)}, u32[]{:S(2)}, u32[]{:S(2)}) %collective-permute-start.24) | collective-permute-done | bytes 393248 | tf_op jit(solution)/shard_map/ppermute | solution.py:26
  162.8 5.6 %collective-permute-done.25.refs_2_ = bf16[384,512]{1,0:T(8,128)(2,1)S(1)} collective-permute-done((bf16[384,512]{1,0:T(8,128)(2,1)S(1)}, bf16[384,512]{1,0:T(8,128)(2,1)S(1)}, u32[]{:S(2)}, u32[]{:S(2)}) %collective-permute-start.25) | collective-permute-done | bytes 393248 | tf_op jit(solution)/shard_map/ppermute | solution.py:26
  171.2 9.9 %collective-permute-done.28.refs_5_ = bf16[384,512]{1,0:T(8,128)(2,1)S(1)} collective-permute-done((bf16[384,512]{1,0:T(8,128)(2,1)S(1)}, bf16[384,512]{1,0:T(8,128)(2,1)S(1)}, u32[]{:S(2)}, u32[]{:S(2)}) %collective-permute-start.28) | collective-permute-done | bytes 393248 | tf_op jit(solution)/shard_map/ppermute | solution.py:26
  181.1 14.8 %collective-permute-done.29.refs_6_ = bf16[384,512]{1,0:T(8,128)(2,1)S(1)} collective-permute-done((bf16[384,512]{1,0:T(8,128)(2,1)S(1)}, bf16[384,512]{1,0:T(8,128)(2,1)S(1)}, u32[]{:S(2)}, u32[]{:S(2)}) %collective-permute-start.29) | collective-permute-done | bytes 393248 | tf_op jit(solution)/shard_map/ppermute | solution.py:26
  195.9 12.0 %collective-permute-done.30.refs_7_ = bf16[384,512]{1,0:T(8,128)(2,1)S(1)} collective-permute-done((bf16[384,512]{1,0:T(8,128)(2,1)S(1)}, bf16[384,512]{1,0:T(8,128)(2,1)S(1)}, u32[]{:S(2)}, u32[]{:S(2)}) %collective-permute-start.30) | collective-permute-done | bytes 393248 | tf_op jit(solution)/shard_map/ppermute | solution.py:26
  212.1 4.5 %collective-permute-done.35 = bf16[1,32,384]{1,2,0:T(8,128)(2,1)S(1)} collective-permute-done((bf16[1,32,384]{1,2,0:T(8,128)(2,1)S(1)}, bf16[1,32,384]{1,2,0:T(8,128)(2,1)S(1)}, u32[]{:S(2)}, u32[]{:S(2)}) %collective-permute-start.35) | collective-permute-done | bytes 24608 | tf_op jit(solution)/shard_map/ppermute | solution.py:26
  218.0 4.4 %collective-permute-done.36 = bf16[2,32,384]{2,1,0:T(8,128)(2,1)S(1)} collective-permute-done((bf16[2,32,384]{2,1,0:T(8,128)(2,1)S(1)}, bf16[2,32,384]{2,1,0:T(8,128)(2,1)S(1)}, u32[]{:S(2)}, u32[]{:S(2)}) %collective-permute-start.36) | collective-permute-done | bytes 49184 | tf_op jit(solution)/shard_map/ppermute | solution.py:26
  224.0 5.8 %collective-permute-done.37 = bf16[4,32,384]{2,1,0:T(8,128)(2,1)S(1)} collective-permute-done((bf16[4,32,384]{2,1,0:T(8,128)(2,1)S(1)}, bf16[4,32,384]{2,1,0:T(8,128)(2,1)S(1)}, u32[]{:S(2)}, u32[]{:S(2)}) %collective-permute-start.37) | collective-permute-done | bytes 98336 | tf_op jit(solution)/shard_map/ppermute | solution.py:26
  231.7 6.5 %collective-permute-done.42 = bf16[1,2,2,32,512]{4,3,2,1,0:T(8,128)(2,1)S(1)} collective-permute-done((bf16[1,2,2,32,512]{4,3,2,1,0:T(8,128)(2,1)S(1)}, bf16[1,2,2,32,512]{4,3,2,1,0:T(8,128)(2,1)S(1)}, u32[]{:S(2)}, u32[]{:S(2)}) %collective-permute-start.42) | collective-permute-done | bytes 131104 | tf_op jit(solution)/shard_map/ppermute | solution.py:26
  239.5 6.0 %collective-permute-done.43 = bf16[2,1,2,32,512]{4,3,2,1,0:T(8,128)(2,1)S(1)} collective-permute-done((bf16[2,1,2,32,512]{4,3,2,1,0:T(8,128)(2,1)S(1)}, bf16[2,1,2,32,512]{4,3,2,1,0:T(8,128)(2,1)S(1)}, u32[]{:S(2)}, u32[]{:S(2)}) %collective-permute-start.43) | collective-permute-done | bytes 131104 | tf_op jit(solution)/shard_map/ppermute | solution.py:26
  246.0 4.5 %collective-permute-done.44 = bf16[2,2,1,32,512]{4,3,2,1,0:T(8,128)(2,1)S(1)} collective-permute-done((bf16[2,2,1,32,512]{4,3,2,1,0:T(8,128)(2,1)S(1)}, bf16[2,2,1,32,512]{4,3,2,1,0:T(8,128)(2,1)S(1)}, u32[]{:S(2)}, u32[]{:S(2)}) %collective-permute-start.44) | collective-permute-done | bytes 131104 | tf_op jit(solution)/shard_map/ppermute | solution.py:26
  261.3 4.8 %hidden_grads.1 = (f32[384,512]{1,0:T(8,128)}, f32[100,512]{1,0:T(8,128)S(1)}) custom-call(f32[384,512]{1,0:T(8,128)S(1)} %get-tuple-element.51.grad_ref, bf16[8,512]{1,0:T(8,128)(2,1)S(1)} %collective-permute-done.31.glow_ref, bf16[8,512]{1,0:T(8,128)(2,1)S(1)} %collective-permute-done.32.ghigh_ref, f32[384,32]{1,0:T(8,128)S(1)} %copy-done.15, ...), custom_call_target="tpu_custom_call" | custom-call | tf_op jit(solution)/shard_map/hidden_grads/pallas_call | solution.py:408
  273.4 6.4 %ffn_out.1 = (bf16[384,512]{1,0:T(8,128)(2,1)S(1)}, bf16[384,512]{1,0:T(8,128)(2,1)S(1)}, bf16[384,512]{1,0:T(8,128)(2,1)S(1)}, bf16[384,512]{1,0:T(8,128)(2,1)S...) custom-call(s32[8]{0:T(128)S(1)} %iota_xor_fusion.order, ...), custom_call_target="tpu_custom_call" | custom-call | tf_op jit(solution)/shard_map/ffn_out/pallas_call | solution.py:245
  285.1 7.6 %collective-permute-start.47 = (bf16[8,32,512]{2,1,0:T(8,128)(2,1)S(1)}, bf16[8,32,512]{2,1,0:T(8,128)(2,1)S(1)}, u32[]{:S(2)}, u32[]{:S(2)}) collective-permute-start(bf16[8,32,512]{2,1,0:T(8,128)(2,1)S(1)} %add_convert_fusion.2), channel_id=1, source_target_pairs={{0,32},{8,40},{16,48},{24,56},{32,0},{40,8},{48,16},{56,24},{64,96... | collective-permute-start | bytes 786440 | tf_op jit(solution)/shard_map/ppermute | solution.py:26
  292.7 5.8 %collective-permute-start.40 = (bf16[100,512]{1,0:T(8,128)(2,1)S(1)}, bf16[100,512]{1,0:T(8,128)(2,1)S(1)}, u32[]{:S(2)}, u32[]{:S(2)}) collective-permute-start(bf16[100,512]{1,0:T(8,128)(2,1)S(1)} %add_convert_fusion.5), channel_id=1, source_target_pairs={{0,32},{8,40},{16,48},{24,56},{32,0},{40,8},{48,16},{56,24},{64,96... | collective-permute-start | bytes 307208 | tf_op jit(solution)/shard_map/ppermute | solution.py:26
  302.8 4.5 %collective-permute-start.22 = (bf16[384,512]{1,0:T(8,128)(2,1)S(1)}, bf16[384,512]{1,0:T(8,128)(2,1)S(1)}, u32[]{:S(2)}, u32[]{:S(2)}) collective-permute-start(bf16[384,512]{1,0:T(8,128)(2,1)S(1)} %get-tuple-element.39), channel_id=1, source_target_pairs={{0,6},{1,7},{2,4},{3,5},{4,2},{5,3},{6,0},{7,1},{8,14},{9,15},{10,... | collective-permute-start | bytes 1179656 | tf_op jit(solution)/shard_map/ppermute | solution.py:26
  314.1 5.4 %collective-permute-done.21 = bf16[384,512]{1,0:T(8,128)(2,1)S(1)} collective-permute-done((bf16[384,512]{1,0:T(8,128)(2,1)S(1)}, bf16[384,512]{1,0:T(8,128)(2,1)S(1)}, u32[]{:S(2)}, u32[]{:S(2)}) %collective-permute-start.21) | collective-permute-done | bytes 393248 | tf_op jit(solution)/shard_map/ppermute | solution.py:26
  319.4 10.2 %collective-permute-done.22 = bf16[384,512]{1,0:T(8,128)(2,1)S(1)} collective-permute-done((bf16[384,512]{1,0:T(8,128)(2,1)S(1)}, bf16[384,512]{1,0:T(8,128)(2,1)S(1)}, u32[]{:S(2)}, u32[]{:S(2)}) %collective-permute-start.22) | collective-permute-done | bytes 393248 | tf_op jit(solution)/shard_map/ppermute | solution.py:26
  329.6 9.9 %collective-permute-done.23 = bf16[384,512]{1,0:T(8,128)(2,1)S(1)} collective-permute-done((bf16[384,512]{1,0:T(8,128)(2,1)S(1)}, bf16[384,512]{1,0:T(8,128)(2,1)S(1)}, u32[]{:S(2)}, u32[]{:S(2)}) %collective-permute-start.23) | collective-permute-done | bytes 393248 | tf_op jit(solution)/shard_map/ppermute | solution.py:26
  (197 shorter events, 130.5 us)
Async XLA Ops:
  7.2 88.5 %all-gather.3.cloned.1.call-start = ((), (), s32[]{:S(2)}) async-start(), calls=%async_computation.2 | async-start | bytes 3538944 | tf_op jit(solution)/shard_map/all_gather | solution.py:471
  7.9 337.0 %reduce-scatter.2.cloned.1.call-start = ((), (), s32[]{:S(2)}) async-start(), calls=%async_computation.1 | async-start | bytes 17825792 | tf_op jit(solution)/shard_map/reduce_scatter | solution.py:491
  66.6 11.8 %collective-permute-start.10 = (bf16[384,512]{1,0:T(8,128)(2,1)}, bf16[384,512]{1,0:T(8,128)(2,1)S(1)}, u32[]{:S(2)}, u32[]{:S(2)}) collective-permute-start(bf16[384,512]{1,0:T(8,128)(2,1)} %get-tuple-element.31.refs_0_), channel_id=1, source_target_pairs={{0,4},{1,5},{2,6},{3,7},{4,0},{5,1},{6,2},{7,3},{8,12},{9,13},{10,... | collective-permute-start | bytes 1179656 | tf_op jit(solution)/shard_map/ppermute | solution.py:26
  69.2 14.4 %collective-permute-start.8 = (bf16[384,512]{1,0:T(8,128)(2,1)}, bf16[384,512]{1,0:T(8,128)(2,1)S(1)}, u32[]{:S(2)}, u32[]{:S(2)}) collective-permute-start(bf16[384,512]{1,0:T(8,128)(2,1)} %get-tuple-element.31.refs_0_), channel_id=1, source_target_pairs={{0,1},{1,0},{2,3},{3,2},{4,5},{5,4},{6,7},{7,6},{8,9},{9,8},{10,11... | collective-permute-start | bytes 1179656 | tf_op jit(solution)/shard_map/ppermute | solution.py:26
  70.3 14.0 %collective-permute-start.9 = (bf16[384,512]{1,0:T(8,128)(2,1)}, bf16[384,512]{1,0:T(8,128)(2,1)S(1)}, u32[]{:S(2)}, u32[]{:S(2)}) collective-permute-start(bf16[384,512]{1,0:T(8,128)(2,1)} %get-tuple-element.31.refs_0_), channel_id=1, source_target_pairs={{0,3},{1,2},{2,1},{3,0},{4,7},{5,6},{6,5},{7,4},{8,11},{9,10},{10,... | collective-permute-start | bytes 1179656 | tf_op jit(solution)/shard_map/ppermute | solution.py:26
  78.5 11.8 %collective-permute-start.11 = (bf16[384,512]{1,0:T(8,128)(2,1)S(1)}, bf16[384,512]{1,0:T(8,128)(2,1)S(1)}, u32[]{:S(2)}, u32[]{:S(2)}) collective-permute-start(bf16[384,512]{1,0:T(8,128)(2,1)S(1)} %collective-permute-done.10.refs_3_), channel_id=1, source_target_pairs={{0,1},{1,0},{2,3},{3,2},{4,5},{5,4},{6,7},{7,6},{8,9},{9,8},{10,11... | collective-permute-start | bytes 1179656 | tf_op jit(solution)/shard_map/ppermute | solution.py:26
  79.1 14.2 %collective-permute-start.12 = (bf16[384,512]{1,0:T(8,128)(2,1)S(1)}, bf16[384,512]{1,0:T(8,128)(2,1)S(1)}, u32[]{:S(2)}, u32[]{:S(2)}) collective-permute-start(bf16[384,512]{1,0:T(8,128)(2,1)S(1)} %collective-permute-done.10.refs_3_), channel_id=1, source_target_pairs={{0,3},{1,2},{2,1},{3,0},{4,7},{5,6},{6,5},{7,4},{8,11},{9,10},{10,... | collective-permute-start | bytes 1179656 | tf_op jit(solution)/shard_map/ppermute | solution.py:26
  84.3 22.1 %collective-permute-start.13 = (bf16[192,512]{1,0:T(8,128)(2,1)}, bf16[192,512]{1,0:T(8,128)(2,1)S(1)}, u32[]{:S(2)}, u32[]{:S(2)}) collective-permute-start(bf16[192,512]{1,0:T(8,128)(2,1)} %slice.186), channel_id=1, source_target_pairs={{0,3},{1,2},{2,1},{3,0},{4,7},{5,6},{6,5},{7,4},{8,11},{9,10},{10,... | collective-permute-start | bytes 589832 | tf_op jit(solution)/shard_map/ppermute | solution.py:26
  85.0 22.0 %collective-permute-start.14 = (bf16[192,512]{1,0:T(8,128)(2,1)}, bf16[192,512]{1,0:T(8,128)(2,1)S(1)}, u32[]{:S(2)}, u32[]{:S(2)}) collective-permute-start(bf16[192,512]{1,0:T(8,128)(2,1)} %slice.187), channel_id=1, source_target_pairs={{0,1},{1,0},{2,3},{3,2},{4,5},{5,4},{6,7},{7,6},{8,9},{9,8},{10,11... | collective-permute-start | bytes 589832 | tf_op jit(solution)/shard_map/ppermute | solution.py:26
  91.0 16.8 %collective-permute-start.15 = (bf16[192,512]{1,0:T(8,128)(2,1)}, bf16[192,512]{1,0:T(8,128)(2,1)S(1)}, u32[]{:S(2)}, u32[]{:S(2)}) collective-permute-start(bf16[192,512]{1,0:T(8,128)(2,1)} %slice.188), channel_id=1, source_target_pairs={{0,3},{1,2},{2,1},{3,0},{4,7},{5,6},{6,5},{7,4},{8,11},{9,10},{10,... | collective-permute-start | bytes 589832 | tf_op jit(solution)/shard_map/ppermute | solution.py:26
  94.0 14.4 %collective-permute-start.16 = (bf16[192,512]{1,0:T(8,128)(2,1)}, bf16[192,512]{1,0:T(8,128)(2,1)S(1)}, u32[]{:S(2)}, u32[]{:S(2)}) collective-permute-start(bf16[192,512]{1,0:T(8,128)(2,1)} %slice.189), channel_id=1, source_target_pairs={{0,1},{1,0},{2,3},{3,2},{4,5},{5,4},{6,7},{7,6},{8,9},{9,8},{10,11... | collective-permute-start | bytes 589832 | tf_op jit(solution)/shard_map/ppermute | solution.py:26
  147.0 12.1 %collective-permute-start.24 = (bf16[384,512]{1,0:T(8,128)(2,1)S(1)}, bf16[384,512]{1,0:T(8,128)(2,1)S(1)}, u32[]{:S(2)}, u32[]{:S(2)}) collective-permute-start(bf16[384,512]{1,0:T(8,128)(2,1)S(1)} %get-tuple-element.43), channel_id=1, source_target_pairs={{0,1},{1,0},{2,3},{3,2},{4,5},{5,4},{6,7},{7,6},{8,9},{9,8},{10,11... | collective-permute-start | bytes 1179656 | tf_op jit(solution)/shard_map/ppermute | solution.py:26
  147.4 21.0 %collective-permute-start.25 = (bf16[384,512]{1,0:T(8,128)(2,1)S(1)}, bf16[384,512]{1,0:T(8,128)(2,1)S(1)}, u32[]{:S(2)}, u32[]{:S(2)}) collective-permute-start(bf16[384,512]{1,0:T(8,128)(2,1)S(1)} %get-tuple-element.44), channel_id=1, source_target_pairs={{0,2},{1,3},{2,0},{3,1},{4,6},{5,7},{6,4},{7,5},{8,10},{9,11},{10,... | collective-permute-start | bytes 1179656 | tf_op jit(solution)/shard_map/ppermute | solution.py:26
  150.1 21.1 %collective-permute-start.26 = (bf16[384,512]{1,0:T(8,128)(2,1)S(1)}, bf16[384,512]{1,0:T(8,128)(2,1)S(1)}, u32[]{:S(2)}, u32[]{:S(2)}) collective-permute-start(bf16[384,512]{1,0:T(8,128)(2,1)S(1)} %get-tuple-element.45), channel_id=1, source_target_pairs={{0,3},{1,2},{2,1},{3,0},{4,7},{5,6},{6,5},{7,4},{8,11},{9,10},{10,... | collective-permute-start | bytes 1179656 | tf_op jit(solution)/shard_map/ppermute | solution.py:26
  151.8 19.4 %collective-permute-start.27 = (bf16[384,512]{1,0:T(8,128)(2,1)S(1)}, bf16[384,512]{1,0:T(8,128)(2,1)S(1)}, u32[]{:S(2)}, u32[]{:S(2)}) collective-permute-start(bf16[384,512]{1,0:T(8,128)(2,1)S(1)} %get-tuple-element.46), channel_id=1, source_target_pairs={{0,4},{1,5},{2,6},{3,7},{4,0},{5,1},{6,2},{7,3},{8,12},{9,13},{10,... | collective-permute-start | bytes 1179656 | tf_op jit(solution)/shard_map/ppermute | solution.py:26
  153.3 27.8 %collective-permute-start.28 = (bf16[384,512]{1,0:T(8,128)(2,1)S(1)}, bf16[384,512]{1,0:T(8,128)(2,1)S(1)}, u32[]{:S(2)}, u32[]{:S(2)}) collective-permute-start(bf16[384,512]{1,0:T(8,128)(2,1)S(1)} %get-tuple-element.47), channel_id=1, source_target_pairs={{0,5},{1,4},{2,7},{3,6},{4,1},{5,0},{6,3},{7,2},{8,13},{9,12},{10,... | collective-permute-start | bytes 1179656 | tf_op jit(solution)/shard_map/ppermute | solution.py:26
  159.1 36.8 %collective-permute-start.29 = (bf16[384,512]{1,0:T(8,128)(2,1)S(1)}, bf16[384,512]{1,0:T(8,128)(2,1)S(1)}, u32[]{:S(2)}, u32[]{:S(2)}) collective-permute-start(bf16[384,512]{1,0:T(8,128)(2,1)S(1)} %get-tuple-element.48), channel_id=1, source_target_pairs={{0,6},{1,7},{2,4},{3,5},{4,2},{5,3},{6,0},{7,1},{8,14},{9,15},{10,... | collective-permute-start | bytes 1179656 | tf_op jit(solution)/shard_map/ppermute | solution.py:26
  168.4 39.5 %collective-permute-start.30 = (bf16[384,512]{1,0:T(8,128)(2,1)S(1)}, bf16[384,512]{1,0:T(8,128)(2,1)S(1)}, u32[]{:S(2)}, u32[]{:S(2)}) collective-permute-start(bf16[384,512]{1,0:T(8,128)(2,1)S(1)} %get-tuple-element.49), channel_id=1, source_target_pairs={{0,7},{1,6},{2,5},{3,4},{4,3},{5,2},{6,1},{7,0},{8,15},{9,14},{10,... | collective-permute-start | bytes 1179656 | tf_op jit(solution)/shard_map/ppermute | solution.py:26
  250.6 18.4 %collective-permute-start.45 = (bf16[8,32,512]{2,1,0:T(8,128)(2,1)S(1)}, bf16[8,32,512]{2,1,0:T(8,128)(2,1)S(1)}, u32[]{:S(2)}, u32[]{:S(2)}) collective-permute-start(bf16[8,32,512]{2,1,0:T(8,128)(2,1)S(1)} %bitcast.66), channel_id=1, source_target_pairs={{0,8},{8,0},{16,24},{24,16},{32,40},{40,32},{48,56},{56,48},{64,72... | collective-permute-start | bytes 786440 | tf_op jit(solution)/shard_map/ppermute | solution.py:26
  250.7 10.6 %collective-permute-start.31 = (bf16[8,512]{1,0:T(8,128)(2,1)S(1)}, bf16[8,512]{1,0:T(8,128)(2,1)S(1)}, u32[]{:S(2)}, u32[]{:S(2)}) collective-permute-start(bf16[8,512]{1,0:T(8,128)(2,1)S(1)} %get-tuple-element.77), channel_id=1, source_target_pairs={{0,8},{8,16},{16,24},{24,32},{32,40},{40,48},{48,56},{56,64},{64,7... | collective-permute-start | bytes 24584 | tf_op jit(solution)/shard_map/ppermute | solution.py:33
  266.1 17.5 %collective-permute-start.38 = (bf16[100,512]{1,0:T(8,128)(2,1)S(1)}, bf16[100,512]{1,0:T(8,128)(2,1)S(1)}, u32[]{:S(2)}, u32[]{:S(2)}) collective-permute-start(bf16[100,512]{1,0:T(8,128)(2,1)S(1)} %convert_element_type.139), channel_id=1, source_target_pairs={{0,8},{8,0},{16,24},{24,16},{32,40},{40,32},{48,56},{56,48},{64,72... | collective-permute-start | bytes 307208 | tf_op jit(solution)/shard_map/ppermute | solution.py:26
  269.1 15.9 %collective-permute-start.46 = (bf16[8,32,512]{2,1,0:T(8,128)(2,1)S(1)}, bf16[8,32,512]{2,1,0:T(8,128)(2,1)S(1)}, u32[]{:S(2)}, u32[]{:S(2)}) collective-permute-start(bf16[8,32,512]{2,1,0:T(8,128)(2,1)S(1)} %add_convert_fusion.3), channel_id=1, source_target_pairs={{0,16},{8,24},{16,0},{24,8},{32,48},{40,56},{48,32},{56,40},{64,80... | collective-permute-start | bytes 786440 | tf_op jit(solution)/shard_map/ppermute | solution.py:26
  279.8 20.0 %collective-permute-start.17 = (bf16[384,512]{1,0:T(8,128)(2,1)S(1)}, bf16[384,512]{1,0:T(8,128)(2,1)S(1)}, u32[]{:S(2)}, u32[]{:S(2)}) collective-permute-start(bf16[384,512]{1,0:T(8,128)(2,1)S(1)} %get-tuple-element.34), channel_id=1, source_target_pairs={{0,1},{1,0},{2,3},{3,2},{4,5},{5,4},{6,7},{7,6},{8,9},{9,8},{10,11... | collective-permute-start | bytes 1179656 | tf_op jit(solution)/shard_map/ppermute | solution.py:26
  280.5 20.9 %collective-permute-start.18 = (bf16[384,512]{1,0:T(8,128)(2,1)S(1)}, bf16[384,512]{1,0:T(8,128)(2,1)S(1)}, u32[]{:S(2)}, u32[]{:S(2)}) collective-permute-start(bf16[384,512]{1,0:T(8,128)(2,1)S(1)} %get-tuple-element.35), channel_id=1, source_target_pairs={{0,2},{1,3},{2,0},{3,1},{4,6},{5,7},{6,4},{7,5},{8,10},{9,11},{10,... | collective-permute-start | bytes 1179656 | tf_op jit(solution)/shard_map/ppermute | solution.py:26
  285.1 22.2 %collective-permute-start.47 = (bf16[8,32,512]{2,1,0:T(8,128)(2,1)S(1)}, bf16[8,32,512]{2,1,0:T(8,128)(2,1)S(1)}, u32[]{:S(2)}, u32[]{:S(2)}) collective-permute-start(bf16[8,32,512]{2,1,0:T(8,128)(2,1)S(1)} %add_convert_fusion.2), channel_id=1, source_target_pairs={{0,32},{8,40},{16,48},{24,56},{32,0},{40,8},{48,16},{56,24},{64,96... | collective-permute-start | bytes 786440 | tf_op jit(solution)/shard_map/ppermute | solution.py:26
  298.5 11.5 %collective-permute-start.19 = (bf16[384,512]{1,0:T(8,128)(2,1)S(1)}, bf16[384,512]{1,0:T(8,128)(2,1)S(1)}, u32[]{:S(2)}, u32[]{:S(2)}) collective-permute-start(bf16[384,512]{1,0:T(8,128)(2,1)S(1)} %get-tuple-element.36), channel_id=1, source_target_pairs={{0,3},{1,2},{2,1},{3,0},{4,7},{5,6},{6,5},{7,4},{8,11},{9,10},{10,... | collective-permute-start | bytes 1179656 | tf_op jit(solution)/shard_map/ppermute | solution.py:26
  299.8 14.1 %collective-permute-start.20 = (bf16[384,512]{1,0:T(8,128)(2,1)S(1)}, bf16[384,512]{1,0:T(8,128)(2,1)S(1)}, u32[]{:S(2)}, u32[]{:S(2)}) collective-permute-start(bf16[384,512]{1,0:T(8,128)(2,1)S(1)} %get-tuple-element.37), channel_id=1, source_target_pairs={{0,4},{1,5},{2,6},{3,7},{4,0},{5,1},{6,2},{7,3},{8,12},{9,13},{10,... | collective-permute-start | bytes 1179656 | tf_op jit(solution)/shard_map/ppermute | solution.py:26
  301.4 18.0 %collective-permute-start.21 = (bf16[384,512]{1,0:T(8,128)(2,1)S(1)}, bf16[384,512]{1,0:T(8,128)(2,1)S(1)}, u32[]{:S(2)}, u32[]{:S(2)}) collective-permute-start(bf16[384,512]{1,0:T(8,128)(2,1)S(1)} %get-tuple-element.38), channel_id=1, source_target_pairs={{0,5},{1,4},{2,7},{3,6},{4,1},{5,0},{6,3},{7,2},{8,13},{9,12},{10,... | collective-permute-start | bytes 1179656 | tf_op jit(solution)/shard_map/ppermute | solution.py:26
  302.8 26.8 %collective-permute-start.22 = (bf16[384,512]{1,0:T(8,128)(2,1)S(1)}, bf16[384,512]{1,0:T(8,128)(2,1)S(1)}, u32[]{:S(2)}, u32[]{:S(2)}) collective-permute-start(bf16[384,512]{1,0:T(8,128)(2,1)S(1)} %get-tuple-element.39), channel_id=1, source_target_pairs={{0,6},{1,7},{2,4},{3,5},{4,2},{5,3},{6,0},{7,1},{8,14},{9,15},{10,... | collective-permute-start | bytes 1179656 | tf_op jit(solution)/shard_map/ppermute | solution.py:26
  307.2 32.3 %collective-permute-start.23 = (bf16[384,512]{1,0:T(8,128)(2,1)S(1)}, bf16[384,512]{1,0:T(8,128)(2,1)S(1)}, u32[]{:S(2)}, u32[]{:S(2)}) collective-permute-start(bf16[384,512]{1,0:T(8,128)(2,1)S(1)} %get-tuple-element.40), channel_id=1, source_target_pairs={{0,7},{1,6},{2,5},{3,4},{4,3},{5,2},{6,1},{7,0},{8,15},{9,14},{10,... | collective-permute-start | bytes 1179656 | tf_op jit(solution)/shard_map/ppermute | solution.py:26
  310.0 30.7 %collective-permute-start.41 = (bf16[100,512]{1,0:T(8,128)(2,1)S(1)}, bf16[100,512]{1,0:T(8,128)(2,1)S(1)}, u32[]{:S(2)}, u32[]{:S(2)}) collective-permute-start(bf16[100,512]{1,0:T(8,128)(2,1)S(1)} %add_convert_fusion.4), channel_id=1, source_target_pairs={{0,64},{8,72},{16,80},{24,88},{32,96},{40,104},{48,112},{56,120},{... | collective-permute-start | bytes 307208 | tf_op jit(solution)/shard_map/ppermute | solution.py:26
  314.0 27.5 %collective-permute-start.48 = (bf16[8,32,512]{2,1,0:T(8,128)(2,1)S(1)}, bf16[8,32,512]{2,1,0:T(8,128)(2,1)S(1)}, u32[]{:S(2)}, u32[]{:S(2)}) collective-permute-start(bf16[8,32,512]{2,1,0:T(8,128)(2,1)S(1)} %add_convert_fusion.1), channel_id=1, source_target_pairs={{0,64},{8,72},{16,80},{24,88},{32,96},{40,104},{48,112},{56,120},{... | collective-permute-start | bytes 786440 | tf_op jit(solution)/shard_map/ppermute | solution.py:26
  (52 other events, 1215.3 us)
Sparse Core Ops, SparseCore 0:
  10.3 65.4 all-gather.2
  137.7 138.3 reduce-scatter.1

commit v2 on v1

--- a/solution.py
+++ b/solution.py
@@ -43,14 +43,6 @@
         send = lax.index_in_dim(cube, 1, place, keepdims=True)
         cube = jnp.concatenate([keep, flip(send, "tp", bit)], axis=place)
     return cube.reshape(shape)
-
-
-def reduce_blocks(blocks):
-    half = blocks.shape[0] // 2
-    while half:
-        blocks = blocks[:half] + flip(blocks[half:], "tp", half)
-        half //= 2
-    return blocks[0]
 
 
 def gather_small(value):
@@ -81,50 +73,172 @@
     return value, one, three, four, five, seven, two_a, two_b, six_a, six_b
 
 
-def conv_forward_kernel(logit_ref, hidden_ref, low_ref, high_ref, act_ref, tap_ref, padded):
-    rows = hidden_ref.shape[0]
-    width = hidden_ref.shape[1]
-    heads = 2
-    exps = jnp.exp(logit_ref[...])
+def hidden_logits_kernel(order, *refs):
+    pieces = refs[:10]
+    gen_ref, full_ref, edge_ref, flat_ref, tap_ref = refs[10:]
+    members, rows, width = full_ref.shape
+    half = rows // 2
+    for at, ref in zip((0, 1, 3, 4, 5, 7), pieces[:6]):
+        full_ref[order[at]] = ref[...]
+    full_ref[order[2], 0:half] = pieces[6][...]
+    full_ref[order[2], half:] = pieces[7][...]
+    full_ref[order[6], 0:half] = pieces[8][...]
+    full_ref[order[6], half:] = pieces[9][...]
+    logits = jnp.zeros((gen_ref.shape[0], rows), F32)
+    for piece in range(members):
+        edge_ref[0, piece] = full_ref[piece, 0:PAD]
+        edge_ref[1, piece] = full_ref[piece, rows - PAD :]
+        logits = logits + lax.dot_general(
+            gen_ref[:, piece * width : (piece + 1) * width],
+            full_ref[piece],
+            NT,
+            preferred_element_type=F32,
+        )
+    exps = jnp.exp(logits)
     first = exps[0:KW]
     second = exps[KW : 2 * KW]
     first = first / jnp.sum(first, axis=0, keepdims=True)
     second = second / jnp.sum(second, axis=0, keepdims=True)
     blank = jnp.zeros((ROWS - 2 * KW, rows), F32)
-    tap_ref[...] = jnp.concatenate([first, second, blank], axis=0).T
-    padded[0:PAD] = low_ref[...].astype(F32)
-    padded[PAD : PAD + rows] = hidden_ref[...].astype(F32)
-    padded[PAD + rows :] = high_ref[...].astype(F32)
-    step = 32
+    flat = jnp.concatenate([first, second, blank], axis=0)
+    flat_ref[...] = flat
+    tap_ref[...] = flat.T
+
+
+def hidden_logits(order, pieces, gen_rows):
+    rows, width = pieces[0].shape
+    columns, depth = gen_rows.shape
+    members = depth // width
+    whole = [pl.BlockSpec(p.shape, lambda i, o: (0, 0)) for p in pieces]
+    return pl.pallas_call(
+        hidden_logits_kernel,
+        grid_spec=pltpu.PrefetchScalarGridSpec(
+            num_scalar_prefetch=1,
+            grid=(1,),
+            in_specs=whole + [pl.BlockSpec((columns, depth), lambda i, o: (0, 0))],
+            out_specs=[
+                pl.BlockSpec((members, rows, width), lambda i, o: (0, 0, 0)),
+                pl.BlockSpec((2, members, PAD, width), lambda i, o: (0, 0, 0, 0)),
+                pl.BlockSpec((ROWS, rows), lambda i, o: (0, 0)),
+                pl.BlockSpec((rows, ROWS), lambda i, o: (0, 0)),
+            ],
+        ),
+        out_shape=(
+            jax.ShapeDtypeStruct((members, rows, width), BF16),
+            jax.ShapeDtypeStruct((2, members, PAD, width), BF16),
+            jax.ShapeDtypeStruct((ROWS, rows), F32),
+            jax.ShapeDtypeStruct((rows, ROWS), F32),
+        ),
+        compiler_params=params(32),
+        name="hidden_logits",
+    )(order, *pieces, gen_rows)
+
+
+def conv_up_kernel(
+    order,
+    hidden_ref,
+    low_ref,
+    high_ref,
+    flat_ref,
+    up_ref,
+    grad_ref,
+    act_ref,
+    middle_ref,
+    pre_grad_ref,
+    padded,
+    pre,
+):
+    _, rows, width = hidden_ref.shape
+    step = 64
+    reach = 2 * step
+    heads = 2
     head_width = width // heads
-
-    def run(index, carry):
-        base = pl.multiple_of(index * step, step)
-        taps = tap_ref[pl.ds(base, step), :]
+    padded[0:PAD] = low_ref[0]
+    padded[PAD : PAD + rows] = hidden_ref[0]
+    padded[PAD + rows : 2 * PAD + rows] = high_ref[0]
+    padded[2 * PAD + rows :] = jnp.zeros((padded.shape[0] - 2 * PAD - rows, width), BF16)
+    flat = flat_ref[0]
+    taps = jnp.concatenate([flat, jnp.zeros((reach - ROWS, rows), F32)], axis=0).T
+    lane = lax.broadcasted_iota(jnp.int32, (step, reach), 1)
+    for base in range(0, rows, step):
         for head in range(heads):
             lanes = slice(head * head_width, (head + 1) * head_width)
-            window = padded[pl.ds(base, step + 2 * PAD), lanes]
-            total = jnp.zeros((step, head_width), F32)
-            for tap in range(KW):
-                column = head * KW + tap
-                total = total + taps[:, column : column + 1] * window[tap + 1 : tap + 1 + step]
-            act_ref[pl.ds(base, step), lanes] = (window[PAD : PAD + step] + total).astype(BF16)
-        return carry
-
-    lax.fori_loop(0, rows // step, run, 0)
-
-
-def conv_forward(logits, hidden, low, high):
-    rows, width = hidden.shape
-    return pl.pallas_call(
-        conv_forward_kernel,
+            mine = (lane >= head * KW) & (lane < (head + 1) * KW)
+            own = jnp.where(mine, taps[base : base + step], 0.0)
+            own = pltpu.roll(own, (1 - head * KW) % reach, 1)
+            band = pltpu.roll(own, 0, 1, stride=1, stride_axis=0)
+            upper = band.astype(BF16)
+            lower = (band - upper.astype(F32)).astype(BF16)
+            window = padded[base : base + reach, lanes]
+            total = jnp.dot(upper, window, preferred_element_type=F32) + jnp.dot(
+                lower, window, preferred_element_type=F32
+            )
+            value = hidden_ref[0, base : base + step, lanes].astype(F32) + total
+            act_ref[0, base : base + step, lanes] = value.astype(BF16)
+    term = jnp.dot(act_ref[0], up_ref[...], preferred_element_type=F32)
+
+    @pl.when(pl.program_id(0) == 0)
+    def _():
+        pre[...] = term
+
+    @pl.when(pl.program_id(0) > 0)
+    def _():
+        pre[...] += term
+
+    @pl.when(pl.program_id(0) == pl.num_programs(0) - 1)
+    def _():
+        scale = 0.7978845608028654
+        chunk = 64
+
+        def run(index, carry):
+            at = pl.ds(pl.multiple_of(index * chunk, chunk), chunk)
+            value = pre[at, :]
+            square = value * value
+            bent = jnp.tanh(scale * (value + 0.044715 * (square * value)))
+            middle_ref[at, :] = (0.5 * value * (1.0 + bent)).astype(BF16)
+            slope = 0.5 * (1.0 + bent) + 0.5 * value * (1.0 - bent * bent) * (
+                scale * (1.0 + 3.0 * 0.044715 * square)
+            )
+            pre_grad_ref[at, :] = (grad_ref[at, :] * slope).astype(BF16)
+            return carry
+
+        lax.fori_loop(0, rows // chunk, run, 0)
+
+
+def conv_up(order, hidden_full, low, high, flat_full, up_weight, middle_grad):
+    members, rows, width = hidden_full.shape
+    units = up_weight.shape[1]
+    return pl.pallas_call(
+        conv_up_kernel,
+        grid_spec=pltpu.PrefetchScalarGridSpec(
+            num_scalar_prefetch=1,
+            grid=(members,),
+            in_specs=[
+                pl.BlockSpec((1, rows, width), lambda i, o: (i, 0, 0)),
+                pl.BlockSpec((1, PAD, width), lambda i, o: (i, 0, 0)),
+                pl.BlockSpec((1, PAD, width), lambda i, o: (i, 0, 0)),
+                pl.BlockSpec((1, ROWS, rows), lambda i, o: (o[i], 0, 0)),
+                pl.BlockSpec((width, units), lambda i, o: (i, 0)),
+                pl.BlockSpec((rows, units), lambda i, o: (0, 0)),
+            ],
+            out_specs=[
+                pl.BlockSpec((1, rows, width), lambda i, o: (i, 0, 0)),
+                pl.BlockSpec((rows, units), lambda i, o: (0, 0)),
+                pl.BlockSpec((rows, units), lambda i, o: (0, 0)),
+            ],
+            scratch_shapes=[
+                pltpu.VMEM((rows + 64, width), BF16),
+                pltpu.VMEM((rows, units), F32),
+            ],
+        ),
         out_shape=(
-            jax.ShapeDtypeStruct((rows, width), BF16),
-            jax.ShapeDtypeStruct((rows, ROWS), F32),
-        ),
-        scratch_shapes=[pltpu.VMEM((rows + 2 * PAD, width), F32)],
-        name="conv_forward",
-    )(logits, hidden, low, high)
+            jax.ShapeDtypeStruct((members, rows, width), BF16),
+            jax.ShapeDtypeStruct((rows, units), BF16),
+            jax.ShapeDtypeStruct((rows, units), BF16),
+        ),
+        compiler_params=params(40),
+        name="conv_up",
+    )(order, hidden_full, low, high, flat_full, up_weight, middle_grad)
 
 
 def grad_middle_kernel(cot_ref, down_ref, out_ref):
@@ -158,78 +272,15 @@
     )(cot_full, down_weight)
 
 
-def up_kernel(order, *refs):
-    pieces = refs[:10]
-    up_ref, grad_ref, full_ref, middle_ref, pre_grad_ref = refs[10:]
-    half = full_ref.shape[1] // 2
-    width = full_ref.shape[2]
-
-    @pl.when(pl.program_id(0) == 0)
-    def _():
-        for at, ref in zip((0, 1, 3, 4, 5, 7), pieces[:6]):
-            full_ref[order[at]] = ref[...]
-        full_ref[order[2], 0:half] = pieces[6][...]
-        full_ref[order[2], half:] = pieces[7][...]
-        full_ref[order[6], 0:half] = pieces[8][...]
-        full_ref[order[6], half:] = pieces[9][...]
-
-    pre = jnp.zeros(middle_ref.shape, F32)
-    for piece in range(full_ref.shape[0]):
-        pre = pre + jnp.dot(
-            full_ref[piece],
-            up_ref[piece * width : (piece + 1) * width, :],
-            preferred_element_type=F32,
-        )
-    scale = 0.7978845608028654
-    square = pre * pre
-    bent = jnp.tanh(scale * (pre + 0.044715 * (square * pre)))
-    middle_ref[...] = (0.5 * pre * (1.0 + bent)).astype(BF16)
-    slope = 0.5 * (1.0 + bent) + 0.5 * pre * (1.0 - bent * bent) * (
-        scale * (1.0 + 3.0 * 0.044715 * square)
-    )
-    pre_grad_ref[...] = (grad_ref[...] * slope).astype(BF16)
-
-
-def up_project(order, pieces, up_weight, middle_grad):
-    rows, width = pieces[0].shape
-    depth, units = up_weight.shape
-    block = 256
-    whole = [pl.BlockSpec(p.shape, lambda i, o: (0, 0)) for p in pieces]
-    return pl.pallas_call(
-        up_kernel,
-        grid_spec=pltpu.PrefetchScalarGridSpec(
-            num_scalar_prefetch=1,
-            grid=(units // block,),
-            in_specs=whole
-            + [
-                pl.BlockSpec((depth, block), lambda i, o: (0, i)),
-                pl.BlockSpec((rows, block), lambda i, o: (0, i)),
-            ],
-            out_specs=[
-                pl.BlockSpec((depth // width, rows, width), lambda i, o: (0, 0, 0)),
-                pl.BlockSpec((rows, block), lambda i, o: (0, i)),
-                pl.BlockSpec((rows, block), lambda i, o: (0, i)),
-            ],
-        ),
-        out_shape=(
-            jax.ShapeDtypeStruct((depth // width, rows, width), BF16),
-            jax.ShapeDtypeStruct((rows, units), BF16),
-            jax.ShapeDtypeStruct((rows, units), BF16),
-        ),
-        compiler_params=params(48),
-        name="up_project",
-    )(order, *pieces, up_weight, middle_grad)
-
-
 def spread_kernel(dims, order, value_ref, weight_ref, *out_refs):
     result = lax.dot_general(
         value_ref[...], weight_ref[...], dims, preferred_element_type=F32
     ).astype(BF16)
     for index, ref in enumerate(out_refs):
 
-        @pl.when(pl.program_id(0) == index)
+        @pl.when(lax.rem(pl.program_id(0), 4) == index)
         def _(ref=ref):
-            ref[...] = result
+            ref[0] = result
 
 
 def spread(order, value, weight, transposed, name):
@@ -248,9 +299,9 @@
             num_scalar_prefetch=1,
             grid=(8,),
             in_specs=[pl.BlockSpec((rows, units), lambda k, o: (0, 0)), spec],
-            out_specs=[pl.BlockSpec((rows, width), lambda k, o: (0, 0))] * 8,
-        ),
-        out_shape=[jax.ShapeDtypeStruct((rows, width), BF16)] * 8,
+            out_specs=[pl.BlockSpec((1, rows, width), lambda k, o: (k // 4, 0, 0))] * 4,
+        ),
+        out_shape=[jax.ShapeDtypeStruct((2, rows, width), BF16)] * 4,
         compiler_params=params(40),
         name=name,
     )(order, value, weight)
@@ -289,8 +340,9 @@
 
 
 def kernel_grad_kernel(*refs):
-    terms = refs[:8]
-    cot_ref, hidden_ref, low_ref, high_ref, tap_ref, grad_ref, logit_ref, padded = refs[8:]
+    terms = refs[:5]
+    cot_ref, hidden_ref, low_ref, high_ref, tap_ref = refs[5:10]
+    grad_ref, logit_ref, padded, found_ref = refs[10:]
     rows, width = hidden_ref.shape
     heads = 2
     head_width = width // heads
@@ -322,24 +374,34 @@
         in_first = lane < KW
         one = jnp.sum(jnp.where(in_first, product, 0.0), axis=1, keepdims=True)
         two = jnp.sum(jnp.where(in_first, 0.0, product), axis=1, keepdims=True)
-        logit_ref[at, :] = taps * (found - jnp.where(in_first, one, two))
+        found_ref[at, :] = taps * (found - jnp.where(in_first, one, two))
         return carry
 
     lax.fori_loop(0, rows // step, run, 0)
-
-
-def kernel_grads(terms, cotangent, hidden, low, high, taps):
+    logit_ref[...] = found_ref[...].T.astype(BF16)
+
+
+def kernel_grads(pairs, last, cotangent, hidden, low, high, taps):
     rows, width = hidden.shape
+    flat = pl.BlockSpec((rows, width), lambda i: (0, 0))
+    edge = pl.BlockSpec((PAD, width), lambda i: (0, 0))
     return pl.pallas_call(
         kernel_grad_kernel,
+        grid=(1,),
+        in_specs=[pl.BlockSpec((None, rows, width), lambda i: (0, 0, 0))] * 4
+        + [flat, flat, flat, edge, edge, pl.BlockSpec((rows, ROWS), lambda i: (0, 0))],
+        out_specs=[flat, pl.BlockSpec((ROWS, rows), lambda i: (0, 0))],
         out_shape=(
             jax.ShapeDtypeStruct((rows, width), F32),
-            jax.ShapeDtypeStruct((rows, ROWS), F32),
-        ),
-        scratch_shapes=[pltpu.VMEM((rows + 2 * PAD, width), F32)],
+            jax.ShapeDtypeStruct((ROWS, rows), BF16),
+        ),
+        scratch_shapes=[
+            pltpu.VMEM((rows + 2 * PAD, width), F32),
+            pltpu.VMEM((rows, ROWS), F32),
+        ],
         compiler_params=params(32),
         name="kernel_grads",
-    )(*terms, cotangent, hidden, low, high, taps)
+    )(*pairs, last, cotangent, hidden, low, high, taps)
 
 
 def hidden_grad_kernel(
@@ -421,26 +483,38 @@
     )(grad, glow, ghigh, taps, tlow, thigh, logit_full, gen_full, mask, code)
 
 
-def place_kernel(order, blocks_ref, out_ref):
-    width = blocks_ref.shape[2]
-    for piece in range(blocks_ref.shape[0]):
-        at = pl.multiple_of(order[piece] * width, width)
-        out_ref[:, pl.ds(at, width)] = blocks_ref[piece, 0 : out_ref.shape[0]]
-
-
-def place(order, blocks, rows):
-    pieces, _, width = blocks.shape
-    return pl.pallas_call(
-        place_kernel,
-        grid_spec=pltpu.PrefetchScalarGridSpec(
-            num_scalar_prefetch=1,
-            grid=(1,),
-            in_specs=[pl.BlockSpec(blocks.shape, lambda i, o: (0, 0, 0))],
-            out_specs=pl.BlockSpec((rows, pieces * width), lambda i, o: (0, 0)),
-        ),
-        out_shape=jax.ShapeDtypeStruct((rows, pieces * width), F32),
-        name="place",
-    )(order, blocks)
+def gen_grads_kernel(logit_ref, hidden_ref, out_ref):
+    width = hidden_ref.shape[2]
+    for piece in range(hidden_ref.shape[0]):
+        out_ref[:, piece * width : (piece + 1) * width] = jnp.dot(
+            logit_ref[...], hidden_ref[piece], preferred_element_type=F32
+        )
+
+
+def gen_grads(logit_grad, hidden_full):
+    members, rows, width = hidden_full.shape
+    heads = logit_grad.shape[0]
+    return pl.pallas_call(
+        gen_grads_kernel,
+        out_shape=jax.ShapeDtypeStruct((heads, members * width), F32),
+        compiler_params=params(32),
+        name="gen_grads",
+    )(logit_grad, hidden_full)
+
+
+def after(value, *others):
+    return lax.optimization_barrier((value, *others))[0]
+
+
+def add_pairs(pairs, index):
+    total = pairs[0][index].astype(F32)
+    for pair in pairs[1:]:
+        total = total + pair[index].astype(F32)
+    return total
+
+
+def swap_pairs(pairs):
+    return [pairs[0]] + [flip(pairs[z], "tp", z) for z in (1, 2, 3)]
 
 
 def body(
@@ -459,6 +533,29 @@
     me = lax.axis_index("tp")
     order = jnp.arange(members, dtype=jnp.int32) ^ me.astype(jnp.int32)
 
+    sentinel_codes = jnp.arange(codes, dtype=jnp.int32)
+    onehot = (sentinel_id[:, None] == sentinel_codes[None, :]).astype(BF16)
+    picked = jnp.dot(onehot, sentinel_table, preferred_element_type=F32).astype(BF16)
+    hidden = jnp.where(span_mask[:, None] == 1, picked, embeddings)
+    pieces = gather_pieces(hidden)
+    cot_full = lax.all_gather(cotangent, "tp", axis=0, tiled=False)
+
+    hidden_full, edges, flat, taps = hidden_logits(order, pieces, gen_weight.T)
+    high_full, low_full = edges[0], edges[1]
+    count = lax.axis_size("seq")
+    low_full = lax.ppermute(low_full, "seq", [(i, i + 1) for i in range(count - 1)])
+    high_full = lax.ppermute(high_full, "seq", [(i + 1, i) for i in range(count - 1)])
+    flat_full = gather_small(flat)
+    middle_grad = grad_middle(cot_full, down_weight)
+    act_full, middle, pre_grad = conv_up(
+        order, hidden_full, low_full, high_full, flat_full, up_weight, middle_grad
+    )
+
+    summed = weight_grads(act_full, cot_full, pre_grad, middle)
+    back_pairs = swap_pairs(spread(order, pre_grad, up_weight, True, "act_back"))
+    summed = lax.psum_scatter(summed, "seq", scatter_dimension=0, tiled=False)
+    out_pairs = spread(order, middle, down_weight, False, "ffn_out")
+
     columns = gen_weight.shape[1]
     gen_rows = jnp.pad(gen_weight.T, ((0, ROWS - columns), (0, 0)))
     gen_own = jnp.stack(
@@ -467,33 +564,17 @@
             for k in range(members)
         ]
     )
-    gen_full = exchange(gen_own).reshape(members * ROWS, width)
-    cot_full = lax.all_gather(cotangent, "tp", axis=0, tiled=False)
-
-    sentinel_codes = jnp.arange(codes, dtype=jnp.int32)
-    onehot = (sentinel_id[:, None] == sentinel_codes[None, :]).astype(BF16)
-    picked = jnp.dot(onehot, sentinel_table, preferred_element_type=F32).astype(BF16)
-    hidden = jnp.where(span_mask[:, None] == 1, picked, embeddings)
-    low, high = halo(hidden)
-
-    logit_part = lax.dot_general(gen_full, hidden, NT, preferred_element_type=F32)
-    logits = reduce_blocks(logit_part.reshape(members, ROWS, rows))
-    act, taps = conv_forward(logits, hidden, low, high)
+    gen_full = exchange(after(gen_own, pre_grad)).reshape(members * ROWS, width)
     tap_low, tap_high = halo(taps)
 
-    pieces = gather_pieces(act)
-    middle_grad = grad_middle(cot_full, down_weight)
-    act_full, middle, pre_grad = up_project(order, pieces, up_weight, middle_grad)
-
-    back_terms = spread(order, pre_grad, up_weight, True, "act_back")
-    back_terms = [back_terms[0]] + [flip(back_terms[k], "tp", k) for k in range(1, members)]
-    summed = weight_grads(act_full, cot_full, pre_grad, middle)
-    summed = lax.psum_scatter(summed, "seq", scatter_dimension=0, tiled=False)
-
-    grad, logit_grad = kernel_grads(back_terms, cotangent, hidden, low, high, taps)
+    back_last = flip(add_pairs(back_pairs, 1).astype(BF16), "tp", 4)
+    low = lax.dynamic_index_in_dim(low_full, me, 0, keepdims=False)
+    high = lax.dynamic_index_in_dim(high_full, me, 0, keepdims=False)
+    grad, logit_grad = kernel_grads(
+        back_pairs, back_last, after(cotangent, *out_pairs, gen_full), hidden, low, high, taps
+    )
     grad_low, grad_high = halo(grad.astype(BF16))
-    logit_full = gather_small(logit_grad.astype(BF16).T)
-    logit_full = logit_full.reshape(members * ROWS, rows)
+    logit_full = gather_small(logit_grad).reshape(members * ROWS, rows)
     embed_grad, table_part = hidden_grads(
         grad,
         grad_low,
@@ -507,16 +588,15 @@
         sentinel_id[None, :],
         codes,
     )
-    gen_part = jnp.dot(logit_full, hidden, preferred_element_type=F32).astype(BF16)
-    gen_part = exchange(gen_part.reshape(members, ROWS, width)).astype(F32)
-    gen_sum = sum_over_seq(gen_part)
+    gen_sum = sum_over_seq(gen_grads(logit_grad, hidden_full))
+    gen_grad = gen_sum[:columns].T
     table_grad = sum_over_seq(table_part)
-    gen_grad = place(order, gen_sum, columns).T
-
-    terms = spread(order, middle, down_weight, False, "ffn_out")
-    total = terms[0].astype(F32)
-    for k in range(1, members):
-        total = total + flip(terms[k], "tp", k).astype(F32)
+
+    out_pairs = swap_pairs([after(pair, grad) for pair in out_pairs])
+    total = add_pairs(out_pairs, 0) + flip(
+        add_pairs(out_pairs, 1).astype(BF16), "tp", 4
+    ).astype(F32)
+    act = lax.dynamic_index_in_dim(act_full, me, 0, keepdims=False)
     layer_output = (act.astype(F32) + total).astype(BF16)
 
     chunk = summed.shape[0] // 2

time: 357 us -> 317 us (0.89)
  starting transfers between devices: 101 us -> 66.9 us
  waiting for transfers between devices: 141 us -> 125 us
  local copies, waits for them, and re-layouts: 30.4 us -> 34.9 us
  Pallas kernels: 53.3 us -> 56.9 us
    ppermute x43 -> x34, starting transfers between devices: 90.7 us -> 53.3 us  [flip(): return lax.ppermute(value, axis, [(i, i ^ bit) for i in range(count)])]
    ppermute x43 -> x34, waiting for transfers between devices: 136 us -> 124 us  [flip(): return lax.ppermute(value, axis, [(i, i ^ bit) for i in range(count)])]
    unnamed x67 -> x88, local copies, waits for them, and re-layouts: 25.6 us -> 31.9 us
    ppermute x0 -> x2, starting transfers between devices: none -> 4.95 us  [the longest x1 3.67 us: body(): lax.ppermute(low_full, 'seq', [(i, i + 1) for i in range(count - 1)])]
    ppermute x3 -> x2, waiting for transfers between devices: 4.7 us -> 0.01 us  [halo(): high = lax.ppermute(value[:PAD], 'seq', backward)]
  transfers between devices with their start and end apart: 51 -> 42, of which waited for: 25 -> 26; matrix products, arithmetic and copies ran while one was open for 3% -> 4% of each run, Pallas kernels for 9% -> 10%
where the time goes in v2:
time: 317 us; the launch traced here: 313 us
  waiting for transfers between devices  125 us (39%)
  starting transfers between devices  66.9 us (21%)
  Pallas kernels  56.9 us (18%)
  local copies, waits for them, and re-layouts  34.9 us (11%)
  between operations  19.6 us (6%)
  other arithmetic  9 us (3%)
    ppermute x34, waiting for transfers between devices, flip(): return lax.ppermute(value, axis, [(i, i ^ bit) for i in range(count)])  124 us
    ppermute x34, starting transfers between devices, flip(): return lax.ppermute(value, axis, [(i, i ^ bit) for i in range(count)])  53.3 us
    unnamed x88, local copies, waits for them, and re-layouts  31.9 us
    pallas_call x1, Pallas kernels, conv_up(): pl.pallas_call(conv_up_kernel, grid_spec=pltpu.PrefetchScalarGridSpec(num...  14.8 us
    pallas_call x2, Pallas kernels, spread(): pl.pallas_call(functools.partial(spread_kernel, dims), grid_spec=pltpu.Pr...  13.7 us
    pallas_call x1, Pallas kernels, weight_grads(): pl.pallas_call(weight_grads_kernel, grid=(pieces,), in_specs=[pl.BlockSpe...  11.9 us
  transfers between devices with their start and end apart: 42, of which 26 were waited for; matrix products, arithmetic and copies ran while one was open for 4% of the time, Pallas kernels for 10%

profile of v2, /device:TPU:0, one launch (start us, length us, event | category | flops | bytes accessed | tf_op | source)
XLA Modules:
  0.0 313.2 jit_solution(13645600811185702094)
XLA Ops:
  10.0 3.2 %collective-permute-start.2 = (bf16[384,512]{1,0:T(8,128)(2,1)S(1)}, bf16[384,512]{1,0:T(8,128)(2,1)S(1)}, u32[]{:S(2)}, u32[]{:S(2)}) collective-permute-start(bf16[384,512]{1,0:T(8,128)(2,1)S(1)} %fusion.refs_0_.refs_6_), channel_id=1, source_target_pairs={{0,4},{1,5},{2,6},{3,7},{4,0},{5,1},{6,2},{7,3},{8,12},{9,13},{10,... | collective-permute-start | bytes 1179656 | tf_op jit(solution)/shard_map/ppermute | solution.py:26
  13.2 4.0 %collective-permute-start.1 = (bf16[384,512]{1,0:T(8,128)(2,1)S(1)}, bf16[384,512]{1,0:T(8,128)(2,1)S(1)}, u32[]{:S(2)}, u32[]{:S(2)}) collective-permute-start(bf16[384,512]{1,0:T(8,128)(2,1)S(1)} %fusion.refs_0_.refs_6_), channel_id=1, source_target_pairs={{0,3},{1,2},{2,1},{3,0},{4,7},{5,6},{6,5},{7,4},{8,11},{9,10},{10,... | collective-permute-start | bytes 1179656 | tf_op jit(solution)/shard_map/ppermute | solution.py:26
  18.0 4.3 %collective-permute-done.2.refs_3_ = bf16[384,512]{1,0:T(8,128)(2,1)S(1)} collective-permute-done((bf16[384,512]{1,0:T(8,128)(2,1)S(1)}, bf16[384,512]{1,0:T(8,128)(2,1)S(1)}, u32[]{:S(2)}, u32[]{:S(2)}) %collective-permute-start.2) | collective-permute-done | bytes 393248 | tf_op jit(solution)/shard_map/ppermute | solution.py:26
  22.3 4.3 %collective-permute-start.4 = (bf16[384,512]{1,0:T(8,128)(2,1)S(1)}, bf16[384,512]{1,0:T(8,128)(2,1)S(1)}, u32[]{:S(2)}, u32[]{:S(2)}) collective-permute-start(bf16[384,512]{1,0:T(8,128)(2,1)S(1)} %collective-permute-done.2.refs_3_), channel_id=1, source_target_pairs={{0,3},{1,2},{2,1},{3,0},{4,7},{5,6},{6,5},{7,4},{8,11},{9,10},{10,... | collective-permute-start | bytes 1179656 | tf_op jit(solution)/shard_map/ppermute | solution.py:26
  32.3 9.8 %collective-permute-done.4.refs_5_ = bf16[384,512]{1,0:T(8,128)(2,1)S(1)} collective-permute-done((bf16[384,512]{1,0:T(8,128)(2,1)S(1)}, bf16[384,512]{1,0:T(8,128)(2,1)S(1)}, u32[]{:S(2)}, u32[]{:S(2)}) %collective-permute-start.4) | collective-permute-done | bytes 393248 | tf_op jit(solution)/shard_map/ppermute | solution.py:26
  64.9 4.7 %collective-permute-done.11 = f32[1,32,384]{2,1,0:T(8,128)S(1)} collective-permute-done((f32[1,32,384]{2,1,0:T(8,128)S(1)}, f32[1,32,384]{2,1,0:T(8,128)S(1)}, u32[]{:S(2)}, u32[]{:S(2)}) %collective-permute-start.11) | collective-permute-done | bytes 49184 | tf_op jit(solution)/shard_map/ppermute | solution.py:26
  69.6 7.9 %collective-permute-done.12 = f32[2,32,384]{2,1,0:T(8,128)S(1)} collective-permute-done((f32[2,32,384]{2,1,0:T(8,128)S(1)}, f32[2,32,384]{2,1,0:T(8,128)S(1)}, u32[]{:S(2)}, u32[]{:S(2)}) %collective-permute-start.12) | collective-permute-done | bytes 98336 | tf_op jit(solution)/shard_map/ppermute | solution.py:26
  79.6 3.7 %collective-permute-start.9 = (bf16[8,8,512]{2,1,0:T(8,128)(2,1)}, bf16[8,8,512]{2,1,0:T(8,128)(2,1)}, u32[]{:S(2)}, u32[]{:S(2)}) collective-permute-start(bf16[8,8,512]{2,1,0:T(8,128)(2,1)} %get-tuple-element.81), channel_id=1, source_target_pairs={{0,8},{8,16},{16,24},{24,32},{32,40},{40,48},{48,56},{56,64},{64,7... | collective-permute-start | bytes 196616 | tf_op jit(solution)/shard_map/ppermute | solution.py:546
  84.9 3.4 %copy-done.3 = bf16[1024,4096]{1,0:T(8,128)(2,1)S(1)} copy-done((bf16[1024,4096]{1,0:T(8,128)(2,1)S(1)}, bf16[1024,4096]{1,0:T(8,128)(2,1)}, u32[]{:S(2)}) %copy-start.3) | copy-done | bytes 8388632
  90.2 4.1 %grad_middle.1.grad_ref = f32[384,1024]{1,0:T(8,128)S(1)} custom-call(bf16[8,384,512]{2,1,0:T(8,128)(2,1)S(1)} %bitcast.75, bf16[1024,4096]{1,0:T(8,128)(2,1)S(1)} %copy-done.3), custom_call_target="tpu_custom_call" | custom-call | tf_op jit(solution)/shard_map/grad_middle/pallas_call | solution.py:261
  94.3 14.8 %conv_up.1 = (bf16[8,384,512]{2,1,0:T(8,128)(2,1)S(1)}, bf16[384,1024]{1,0:T(8,128)(2,1)S(1)}, bf16[384,1024]{1,0:T(8,128)(2,1)S(1)}) custom-call(s32[8]{0:T(128)S(1)} %iota_xor_fusion.order, bf16[8,384,512]{2,1,0:T(8,128)(2,1)S(1)} %get-tuple-element.31.hidden_ref, bf16[8,8,512]{2,1,0:T(8,128)(2,1)} %collective-permute-done.9.low_ref, ...), custom_call_target="tpu_custom_call" | custom-call | tf_op jit(solution)/shard_map/conv_up/pallas_call | solution.py:211
  109.1 11.9 %weight_grads.1 = bf16[16,512,1024]{2,1,0:T(8,128)(2,1)} custom-call(bf16[8,384,512]{2,1,0:T(8,128)(2,1)S(1)} %get-tuple-element.34.act_ref, bf16[8,384,512]{2,1,0:T(8,128)(2,1)S(1)} %bitcast.76, bf16[384,1024]{1,0:T(8,128)(2,1)S(1)} %get-tuple-element.37.value_ref.pre_grad_ref, bf16[384,1024]{1,0:T(8,128)(2,1)S(1)} %get-tuple-element.35.value_ref.middle_ref), custom_call_target="tpu_custom_call" | custom-call | tf_op jit(solution)/shard_map/weight_grads/pallas_call | solution.py:326
  130.3 4.1 %copy-done.2 = bf16[4096,1024]{1,0:T(8,128)(2,1)S(1)} copy-done((bf16[4096,1024]{1,0:T(8,128)(2,1)S(1)}, bf16[4096,1024]{1,0:T(8,128)(2,1)}, u32[]{:S(2)}) %copy-start.2) | copy-done | bytes 8388632
  135.5 7.4 %act_back.1 = (bf16[2,384,512]{2,1,0:T(8,128)(2,1)S(1)}, bf16[2,384,512]{2,1,0:T(8,128)(2,1)}, bf16[2,384,512]{2,1,0:T(8,128)(2,1)}, bf16[2,384,512]{2,1,0:T(8,128)(2,1)}) custom-call(s32[8]{0:T(128)S(1)} %iota_xor_fusion.order, bf16[384,1024]{1,0:T(8,128)(2,1)S(1)} %copy-done.16, bf16[4096,1024]{1,0:T(8,128)(2,1)S(1)} %copy-done.2), custom_call_target="tpu_custom_call" | custom-call | tf_op jit(solution)/shard_map/act_back/pallas_call | solution.py:296
  149.8 6.1 %collective-permute-done.18 = bf16[1,2,2,32,512]{4,3,2,1,0:T(8,128)(2,1)S(1)} collective-permute-done((bf16[1,2,2,32,512]{4,3,2,1,0:T(8,128)(2,1)S(1)}, bf16[1,2,2,32,512]{4,3,2,1,0:T(8,128)(2,1)S(1)}, u32[]{:S(2)}, u32[]{:S(2)}) %collective-permute-start.18) | collective-permute-done | bytes 131104 | tf_op jit(solution)/shard_map/ppermute | solution.py:26
  156.0 7.7 %collective-permute-done.14.refs_1_ = bf16[2,384,512]{2,1,0:T(8,128)(2,1)} collective-permute-done((bf16[2,384,512]{2,1,0:T(8,128)(2,1)}, bf16[2,384,512]{2,1,0:T(8,128)(2,1)}, u32[]{:S(2)}, u32[]{:S(2)}) %collective-permute-start.14) | collective-permute-done | bytes 786464 | tf_op jit(solution)/shard_map/ppermute | solution.py:26
  163.7 16.8 %collective-permute-done.15.refs_2_ = bf16[2,384,512]{2,1,0:T(8,128)(2,1)} collective-permute-done((bf16[2,384,512]{2,1,0:T(8,128)(2,1)}, bf16[2,384,512]{2,1,0:T(8,128)(2,1)}, u32[]{:S(2)}, u32[]{:S(2)}) %collective-permute-start.15) | collective-permute-done | bytes 786464 | tf_op jit(solution)/shard_map/ppermute | solution.py:26
  180.5 5.0 %collective-permute-done.16.refs_3_ = bf16[2,384,512]{2,1,0:T(8,128)(2,1)} collective-permute-done((bf16[2,384,512]{2,1,0:T(8,128)(2,1)}, bf16[2,384,512]{2,1,0:T(8,128)(2,1)}, u32[]{:S(2)}, u32[]{:S(2)}) %collective-permute-start.16) | collective-permute-done | bytes 786464 | tf_op jit(solution)/shard_map/ppermute | solution.py:26
  190.6 3.5 %copy-done.4 = bf16[1024,4096]{1,0:T(8,128)(2,1)S(1)} copy-done((bf16[1024,4096]{1,0:T(8,128)(2,1)S(1)}, bf16[1024,4096]{1,0:T(8,128)(2,1)}, u32[]{:S(2)}) %copy-start.4) | copy-done | bytes 8388632
  194.1 6.3 %ffn_out.1 = (bf16[2,384,512]{2,1,0:T(8,128)(2,1)S(1)}, bf16[2,384,512]{2,1,0:T(8,128)(2,1)S(1)}, bf16[2,384,512]{2,1,0:T(8,128)(2,1)S(1)}, bf16[2,384,512]{2,1,0:T(8,128)(2,1)S(1)}) custom-call(s32[8]{0:T(128)S(1)} %iota_xor_fusion.order, bf16[384,1024]{1,0:T(8,128)(2,1)S(1)} %copy-done.14, bf16[1024,4096]{1,0:T(8,128)(2,1)S(1)} %copy-done.4), custom_call_target="tpu_custom_call" | custom-call | tf_op jit(solution)/shard_map/ffn_out/pallas_call | solution.py:296
  200.5 3.6 %collective-permute-done.17.refs_4_ = bf16[384,512]{1,0:T(8,128)(2,1)S(1)} collective-permute-done((bf16[384,512]{1,0:T(8,128)(2,1)S(1)}, bf16[384,512]{1,0:T(8,128)(2,1)S(1)}, u32[]{:S(2)}, u32[]{:S(2)}) %collective-permute-start.17) | collective-permute-done | bytes 393248 | tf_op jit(solution)/shard_map/ppermute | solution.py:26
  204.1 5.0 %kernel_grads.1 = (f32[384,512]{1,0:T(8,128)S(1)}, bf16[32,384]{1,0:T(8,128)(2,1)S(1)}) custom-call(bf16[2,384,512]{2,1,0:T(8,128)(2,1)S(1)} %copy-done.18, bf16[2,384,512]{2,1,0:T(8,128)(2,1)} %collective-permute-done.14.refs_1_, bf16[2,384,512]{2,1,0:T(8,128)(2,1)} %collective-permute-done.15.refs_2_, ...), custom_call_target="tpu_custom_call" | custom-call | tf_op jit(solution)/shard_map/kernel_grads/pallas_call | solution.py:388
  209.3 3.7 %collective-permute-done.29 = bf16[1,32,384]{2,1,0:T(8,128)(2,1)S(1)} collective-permute-done((bf16[1,32,384]{2,1,0:T(8,128)(2,1)S(1)}, bf16[1,32,384]{2,1,0:T(8,128)(2,1)S(1)}, u32[]{:S(2)}, u32[]{:S(2)}) %collective-permute-start.29) | collective-permute-done | bytes 24608 | tf_op jit(solution)/shard_map/ppermute | solution.py:26
  215.2 3.0 collective-permute-start.27
  218.7 3.1 collective-permute-start.31
  223.1 3.0 collective-permute-start.25
  227.1 4.8 %hidden_grads.1 = (f32[384,512]{1,0:T(8,128)}, f32[100,512]{1,0:T(8,128)S(1)}) custom-call(f32[384,512]{1,0:T(8,128)S(1)} %get-tuple-element.48.grad_ref, bf16[8,512]{1,0:T(8,128)(2,1)S(1)} %collective-permute-done.25.glow_ref, bf16[8,512]{1,0:T(8,128)(2,1)S(1)} %collective-permute-done.26.ghigh_ref, f32[384,32]{1,0:T(8,128)S(1)} %copy-done.27, ...), custom_call_target="tpu_custom_call" | custom-call | tf_op jit(solution)/shard_map/hidden_grads/pallas_call | solution.py:470
  239.6 3.4 %collective-permute-start.34 = (bf16[100,512]{1,0:T(8,128)(2,1)S(1)}, bf16[100,512]{1,0:T(8,128)(2,1)S(1)}, u32[]{:S(2)}, u32[]{:S(2)}) collective-permute-start(bf16[100,512]{1,0:T(8,128)(2,1)S(1)} %add_convert_fusion.6), channel_id=1, source_target_pairs={{0,32},{8,40},{16,48},{24,56},{32,0},{40,8},{48,16},{56,24},{64,96... | collective-permute-start | bytes 307208 | tf_op jit(solution)/shard_map/ppermute | solution.py:26
  246.7 5.9 %collective-permute-start.35 = (bf16[100,512]{1,0:T(8,128)(2,1)S(1)}, bf16[100,512]{1,0:T(8,128)(2,1)S(1)}, u32[]{:S(2)}, u32[]{:S(2)}) collective-permute-start(bf16[100,512]{1,0:T(8,128)(2,1)S(1)} %add_convert_fusion.5), channel_id=1, source_target_pairs={{0,64},{8,72},{16,80},{24,88},{32,96},{40,104},{48,112},{56,120},{... | collective-permute-start | bytes 307208 | tf_op jit(solution)/shard_map/ppermute | solution.py:26
  263.3 10.7 %collective-permute-done.21 = bf16[2,384,512]{2,1,0:T(8,128)(2,1)S(1)} collective-permute-done((bf16[2,384,512]{2,1,0:T(8,128)(2,1)S(1)}, bf16[2,384,512]{2,1,0:T(8,128)(2,1)S(1)}, u32[]{:S(2)}, u32[]{:S(2)}) %collective-permute-start.21) | collective-permute-done | bytes 786464 | tf_op jit(solution)/shard_map/ppermute | solution.py:26
  274.0 14.5 %collective-permute-done.22 = bf16[2,384,512]{2,1,0:T(8,128)(2,1)S(1)} collective-permute-done((bf16[2,384,512]{2,1,0:T(8,128)(2,1)S(1)}, bf16[2,384,512]{2,1,0:T(8,128)(2,1)S(1)}, u32[]{:S(2)}, u32[]{:S(2)}) %collective-permute-start.22) | collective-permute-done | bytes 786464 | tf_op jit(solution)/shard_map/ppermute | solution.py:26
  294.2 6.4 %collective-permute-done.24 = bf16[384,512]{1,0:T(8,128)(2,1)S(1)} collective-permute-done((bf16[384,512]{1,0:T(8,128)(2,1)S(1)}, bf16[384,512]{1,0:T(8,128)(2,1)S(1)}, u32[]{:S(2)}, u32[]{:S(2)}) %collective-permute-start.24) | collective-permute-done | bytes 393248 | tf_op jit(solution)/shard_map/ppermute | solution.py:26
  (192 shorter events, 93.6 us)
Async XLA Ops:
  7.2 77.7 %all-gather.3.cloned.1.call-start = ((), (), s32[]{:S(2)}) async-start(), calls=%async_computation.2 | async-start | bytes 3538944 | tf_op jit(solution)/shard_map/all_gather | solution.py:541
  7.9 294.8 %reduce-scatter.2.cloned.1.call-start = ((), (), s32[]{:S(2)}) async-start(), calls=%async_computation.1 | async-start | bytes 17825792 | tf_op jit(solution)/shard_map/reduce_scatter | solution.py:556
  10.0 12.3 %collective-permute-start.2 = (bf16[384,512]{1,0:T(8,128)(2,1)S(1)}, bf16[384,512]{1,0:T(8,128)(2,1)S(1)}, u32[]{:S(2)}, u32[]{:S(2)}) collective-permute-start(bf16[384,512]{1,0:T(8,128)(2,1)S(1)} %fusion.refs_0_.refs_6_), channel_id=1, source_target_pairs={{0,4},{1,5},{2,6},{3,7},{4,0},{5,1},{6,2},{7,3},{8,12},{9,13},{10,... | collective-permute-start | bytes 1179656 | tf_op jit(solution)/shard_map/ppermute | solution.py:26
  13.2 15.2 %collective-permute-start.1 = (bf16[384,512]{1,0:T(8,128)(2,1)S(1)}, bf16[384,512]{1,0:T(8,128)(2,1)S(1)}, u32[]{:S(2)}, u32[]{:S(2)}) collective-permute-start(bf16[384,512]{1,0:T(8,128)(2,1)S(1)} %fusion.refs_0_.refs_6_), channel_id=1, source_target_pairs={{0,3},{1,2},{2,1},{3,0},{4,7},{5,6},{6,5},{7,4},{8,11},{9,10},{10,... | collective-permute-start | bytes 1179656 | tf_op jit(solution)/shard_map/ppermute | solution.py:26
  17.2 13.4 %collective-permute-start = (bf16[384,512]{1,0:T(8,128)(2,1)S(1)}, bf16[384,512]{1,0:T(8,128)(2,1)S(1)}, u32[]{:S(2)}, u32[]{:S(2)}) collective-permute-start(bf16[384,512]{1,0:T(8,128)(2,1)S(1)} %fusion.refs_0_.refs_6_), channel_id=1, source_target_pairs={{0,1},{1,0},{2,3},{3,2},{4,5},{5,4},{6,7},{7,6},{8,9},{9,8},{10,11... | collective-permute-start | bytes 1179656 | tf_op jit(solution)/shard_map/ppermute | solution.py:26
  22.3 19.8 %collective-permute-start.4 = (bf16[384,512]{1,0:T(8,128)(2,1)S(1)}, bf16[384,512]{1,0:T(8,128)(2,1)S(1)}, u32[]{:S(2)}, u32[]{:S(2)}) collective-permute-start(bf16[384,512]{1,0:T(8,128)(2,1)S(1)} %collective-permute-done.2.refs_3_), channel_id=1, source_target_pairs={{0,3},{1,2},{2,1},{3,0},{4,7},{5,6},{6,5},{7,4},{8,11},{9,10},{10,... | collective-permute-start | bytes 1179656 | tf_op jit(solution)/shard_map/ppermute | solution.py:26
  26.5 16.7 %collective-permute-start.3 = (bf16[384,512]{1,0:T(8,128)(2,1)S(1)}, bf16[384,512]{1,0:T(8,128)(2,1)S(1)}, u32[]{:S(2)}, u32[]{:S(2)}) collective-permute-start(bf16[384,512]{1,0:T(8,128)(2,1)S(1)} %collective-permute-done.2.refs_3_), channel_id=1, source_target_pairs={{0,1},{1,0},{2,3},{3,2},{4,5},{5,4},{6,7},{7,6},{8,9},{9,8},{10,11... | collective-permute-start | bytes 1179656 | tf_op jit(solution)/shard_map/ppermute | solution.py:26
  28.3 19.1 %collective-permute-start.6 = (bf16[192,512]{1,0:T(8,128)(2,1)S(1)}, bf16[192,512]{1,0:T(8,128)(2,1)S(1)}, u32[]{:S(2)}, u32[]{:S(2)}) collective-permute-start(bf16[192,512]{1,0:T(8,128)(2,1)S(1)} %slice.167), channel_id=1, source_target_pairs={{0,1},{1,0},{2,3},{3,2},{4,5},{5,4},{6,7},{7,6},{8,9},{9,8},{10,11... | collective-permute-start | bytes 589832 | tf_op jit(solution)/shard_map/ppermute | solution.py:26
  30.6 17.5 %collective-permute-start.5 = (bf16[192,512]{1,0:T(8,128)(2,1)S(1)}, bf16[192,512]{1,0:T(8,128)(2,1)S(1)}, u32[]{:S(2)}, u32[]{:S(2)}) collective-permute-start(bf16[192,512]{1,0:T(8,128)(2,1)S(1)} %slice.166), channel_id=1, source_target_pairs={{0,3},{1,2},{2,1},{3,0},{4,7},{5,6},{6,5},{7,4},{8,11},{9,10},{10,... | collective-permute-start | bytes 589832 | tf_op jit(solution)/shard_map/ppermute | solution.py:26
  42.1 9.4 %collective-permute-start.8 = (bf16[192,512]{1,0:T(8,128)(2,1)S(1)}, bf16[192,512]{1,0:T(8,128)(2,1)S(1)}, u32[]{:S(2)}, u32[]{:S(2)}) collective-permute-start(bf16[192,512]{1,0:T(8,128)(2,1)S(1)} %slice.169), channel_id=1, source_target_pairs={{0,1},{1,0},{2,3},{3,2},{4,5},{5,4},{6,7},{7,6},{8,9},{9,8},{10,11... | collective-permute-start | bytes 589832 | tf_op jit(solution)/shard_map/ppermute | solution.py:26
  43.2 9.0 %collective-permute-start.7 = (bf16[192,512]{1,0:T(8,128)(2,1)S(1)}, bf16[192,512]{1,0:T(8,128)(2,1)S(1)}, u32[]{:S(2)}, u32[]{:S(2)}) collective-permute-start(bf16[192,512]{1,0:T(8,128)(2,1)S(1)} %slice.168), channel_id=1, source_target_pairs={{0,3},{1,2},{2,1},{3,0},{4,7},{5,6},{6,5},{7,4},{8,11},{9,10},{10,... | collective-permute-start | bytes 589832 | tf_op jit(solution)/shard_map/ppermute | solution.py:26
  69.5 8.0 %collective-permute-start.12 = (f32[2,32,384]{2,1,0:T(8,128)S(1)}, f32[2,32,384]{2,1,0:T(8,128)S(1)}, u32[]{:S(2)}, u32[]{:S(2)}) collective-permute-start(f32[2,32,384]{2,1,0:T(8,128)S(1)} %pad_maximum_fusion.6), channel_id=1, source_target_pairs={{0,2},{1,3},{2,0},{3,1},{4,6},{5,7},{6,4},{7,5},{8,10},{9,11},{10,... | collective-permute-start | bytes 294920 | tf_op jit(solution)/shard_map/ppermute | solution.py:26
  78.3 16.0 %collective-permute-start.10 = (bf16[8,8,512]{2,1,0:T(8,128)(2,1)}, bf16[8,8,512]{2,1,0:T(8,128)(2,1)}, u32[]{:S(2)}, u32[]{:S(2)}) collective-permute-start(bf16[8,8,512]{2,1,0:T(8,128)(2,1)} %get-tuple-element.80), channel_id=1, source_target_pairs={{8,0},{16,8},{24,16},{32,24},{40,32},{48,40},{56,48},{64,56},{72,6... | collective-permute-start | bytes 196616 | tf_op jit(solution)/shard_map/ppermute | solution.py:547
  79.6 14.7 %collective-permute-start.9 = (bf16[8,8,512]{2,1,0:T(8,128)(2,1)}, bf16[8,8,512]{2,1,0:T(8,128)(2,1)}, u32[]{:S(2)}, u32[]{:S(2)}) collective-permute-start(bf16[8,8,512]{2,1,0:T(8,128)(2,1)} %get-tuple-element.81), channel_id=1, source_target_pairs={{0,8},{8,16},{16,24},{24,32},{32,40},{40,48},{48,56},{56,64},{64,7... | collective-permute-start | bytes 196616 | tf_op jit(solution)/shard_map/ppermute | solution.py:546
  142.9 20.8 %collective-permute-start.14 = (bf16[2,384,512]{2,1,0:T(8,128)(2,1)}, bf16[2,384,512]{2,1,0:T(8,128)(2,1)}, u32[]{:S(2)}, u32[]{:S(2)}) collective-permute-start(bf16[2,384,512]{2,1,0:T(8,128)(2,1)} %get-tuple-element.39), channel_id=1, source_target_pairs={{0,1},{1,0},{2,3},{3,2},{4,5},{5,4},{6,7},{7,6},{8,9},{9,8},{10,11... | collective-permute-start | bytes 2359304 | tf_op jit(solution)/shard_map/ppermute | solution.py:26
  142.9 37.6 %collective-permute-start.15 = (bf16[2,384,512]{2,1,0:T(8,128)(2,1)}, bf16[2,384,512]{2,1,0:T(8,128)(2,1)}, u32[]{:S(2)}, u32[]{:S(2)}) collective-permute-start(bf16[2,384,512]{2,1,0:T(8,128)(2,1)} %get-tuple-element.40), channel_id=1, source_target_pairs={{0,2},{1,3},{2,0},{3,1},{4,6},{5,7},{6,4},{7,5},{8,10},{9,11},{10,... | collective-permute-start | bytes 2359304 | tf_op jit(solution)/shard_map/ppermute | solution.py:26
  144.9 40.6 %collective-permute-start.16 = (bf16[2,384,512]{2,1,0:T(8,128)(2,1)}, bf16[2,384,512]{2,1,0:T(8,128)(2,1)}, u32[]{:S(2)}, u32[]{:S(2)}) collective-permute-start(bf16[2,384,512]{2,1,0:T(8,128)(2,1)} %get-tuple-element.41), channel_id=1, source_target_pairs={{0,3},{1,2},{2,1},{3,0},{4,7},{5,6},{6,5},{7,4},{8,11},{9,10},{10,... | collective-permute-start | bytes 2359304 | tf_op jit(solution)/shard_map/ppermute | solution.py:26
  147.7 8.2 %collective-permute-start.18 = (bf16[1,2,2,32,512]{4,3,2,1,0:T(8,128)(2,1)S(1)}, bf16[1,2,2,32,512]{4,3,2,1,0:T(8,128)(2,1)S(1)}, u32[]{:S(2)}, u32[]{:S(2)}) collective-permute-start(bf16[1,2,2,32,512]{4,3,2,1,0:T(8,128)(2,1)S(1)} %bitcast.88), channel_id=1, source_target_pairs={{0,4},{1,5},{2,6},{3,7},{4,0},{5,1},{6,2},{7,3},{8,12},{9,13},{10,... | collective-permute-start | bytes 393224 | tf_op jit(solution)/shard_map/ppermute | solution.py:26
  155.9 33.0 %collective-permute-start.19 = (bf16[2,1,2,32,512]{4,3,2,1,0:T(8,128)(2,1)S(1)}, bf16[2,1,2,32,512]{4,3,2,1,0:T(8,128)(2,1)S(1)}, u32[]{:S(2)}, u32[]{:S(2)}) collective-permute-start(bf16[2,1,2,32,512]{4,3,2,1,0:T(8,128)(2,1)S(1)} %get-tuple-element.75), channel_id=1, source_target_pairs={{0,2},{1,3},{2,0},{3,1},{4,6},{5,7},{6,4},{7,5},{8,10},{9,11},{10,... | collective-permute-start | bytes 393224 | tf_op jit(solution)/shard_map/ppermute | solution.py:26
  187.1 16.9 %collective-permute-start.17 = (bf16[384,512]{1,0:T(8,128)(2,1)S(1)}, bf16[384,512]{1,0:T(8,128)(2,1)S(1)}, u32[]{:S(2)}, u32[]{:S(2)}) collective-permute-start(bf16[384,512]{1,0:T(8,128)(2,1)S(1)} %fusion.3), channel_id=1, source_target_pairs={{0,4},{1,5},{2,6},{3,7},{4,0},{5,1},{6,2},{7,3},{8,12},{9,13},{10,... | collective-permute-start | bytes 1179656 | tf_op jit(solution)/shard_map/ppermute | solution.py:26
  189.0 11.5 %collective-permute-start.20 = (bf16[2,2,1,32,512]{4,3,2,1,0:T(8,128)(2,1)S(1)}, bf16[2,2,1,32,512]{4,3,2,1,0:T(8,128)(2,1)S(1)}, u32[]{:S(2)}, u32[]{:S(2)}) collective-permute-start(bf16[2,2,1,32,512]{4,3,2,1,0:T(8,128)(2,1)S(1)} %get-tuple-element.73), channel_id=1, source_target_pairs={{0,1},{1,0},{2,3},{3,2},{4,5},{5,4},{6,7},{7,6},{8,9},{9,8},{10,11... | collective-permute-start | bytes 393224 | tf_op jit(solution)/shard_map/ppermute | solution.py:26
  214.0 13.1 %collective-permute-start.28 = (f32[8,32]{1,0:T(8,128)S(1)}, f32[8,32]{1,0:T(8,128)S(1)}, u32[]{:S(2)}, u32[]{:S(2)}) collective-permute-start(f32[8,32]{1,0:T(8,128)S(1)} %get-tuple-element.78), channel_id=1, source_target_pairs={{8,0},{16,8},{24,16},{32,24},{40,32},{48,40},{56,48},{64,56},{72,6... | collective-permute-start | bytes 3080 | tf_op jit(solution)/shard_map/ppermute | solution.py:34
  215.2 11.8 %collective-permute-start.27 = (f32[8,32]{1,0:T(8,128)S(1)}, f32[8,32]{1,0:T(8,128)S(1)}, u32[]{:S(2)}, u32[]{:S(2)}) collective-permute-start(f32[8,32]{1,0:T(8,128)S(1)} %get-tuple-element.79), channel_id=1, source_target_pairs={{0,8},{8,16},{16,24},{24,32},{32,40},{40,48},{48,56},{56,64},{64,7... | collective-permute-start | bytes 3080 | tf_op jit(solution)/shard_map/ppermute | solution.py:33
  218.7 8.3 %collective-permute-start.31 = (bf16[4,32,384]{2,1,0:T(8,128)(2,1)S(1)}, bf16[4,32,384]{2,1,0:T(8,128)(2,1)S(1)}, u32[]{:S(2)}, u32[]{:S(2)}) collective-permute-start(bf16[4,32,384]{2,1,0:T(8,128)(2,1)S(1)} %pad_maximum_fusion.7), channel_id=1, source_target_pairs={{0,4},{1,5},{2,6},{3,7},{4,0},{5,1},{6,2},{7,3},{8,12},{9,13},{10,... | collective-permute-start | bytes 294920 | tf_op jit(solution)/shard_map/ppermute | solution.py:26
  243.1 9.5 %collective-permute-start.37 = (bf16[32,4096]{1,0:T(8,128)(2,1)S(1)}, bf16[32,4096]{1,0:T(8,128)(2,1)S(1)}, u32[]{:S(2)}, u32[]{:S(2)}) collective-permute-start(bf16[32,4096]{1,0:T(8,128)(2,1)S(1)} %add_convert_fusion.4), channel_id=1, source_target_pairs={{0,16},{8,24},{16,0},{24,8},{32,48},{40,56},{48,32},{56,40},{64,80... | collective-permute-start | bytes 786440 | tf_op jit(solution)/shard_map/ppermute | solution.py:26
  246.7 11.5 %collective-permute-start.35 = (bf16[100,512]{1,0:T(8,128)(2,1)S(1)}, bf16[100,512]{1,0:T(8,128)(2,1)S(1)}, u32[]{:S(2)}, u32[]{:S(2)}) collective-permute-start(bf16[100,512]{1,0:T(8,128)(2,1)S(1)} %add_convert_fusion.5), channel_id=1, source_target_pairs={{0,64},{8,72},{16,80},{24,88},{32,96},{40,104},{48,112},{56,120},{... | collective-permute-start | bytes 307208 | tf_op jit(solution)/shard_map/ppermute | solution.py:26
  252.7 8.0 %collective-permute-start.38 = (bf16[32,4096]{1,0:T(8,128)(2,1)S(1)}, bf16[32,4096]{1,0:T(8,128)(2,1)S(1)}, u32[]{:S(2)}, u32[]{:S(2)}) collective-permute-start(bf16[32,4096]{1,0:T(8,128)(2,1)S(1)} %add_convert_fusion.3), channel_id=1, source_target_pairs={{0,32},{8,40},{16,48},{24,56},{32,0},{40,8},{48,16},{56,24},{64,96... | collective-permute-start | bytes 786440 | tf_op jit(solution)/shard_map/ppermute | solution.py:26
  253.5 20.5 %collective-permute-start.21 = (bf16[2,384,512]{2,1,0:T(8,128)(2,1)S(1)}, bf16[2,384,512]{2,1,0:T(8,128)(2,1)S(1)}, u32[]{:S(2)}, u32[]{:S(2)}) collective-permute-start(bf16[2,384,512]{2,1,0:T(8,128)(2,1)S(1)} %get-tuple-element.50), channel_id=1, source_target_pairs={{0,1},{1,0},{2,3},{3,2},{4,5},{5,4},{6,7},{7,6},{8,9},{9,8},{10,11... | collective-permute-start | bytes 2359304 | tf_op jit(solution)/shard_map/ppermute | solution.py:26
  255.2 33.3 %collective-permute-start.22 = (bf16[2,384,512]{2,1,0:T(8,128)(2,1)S(1)}, bf16[2,384,512]{2,1,0:T(8,128)(2,1)S(1)}, u32[]{:S(2)}, u32[]{:S(2)}) collective-permute-start(bf16[2,384,512]{2,1,0:T(8,128)(2,1)S(1)} %get-tuple-element.51), channel_id=1, source_target_pairs={{0,2},{1,3},{2,0},{3,1},{4,6},{5,7},{6,4},{7,5},{8,10},{9,11},{10,... | collective-permute-start | bytes 2359304 | tf_op jit(solution)/shard_map/ppermute | solution.py:26
  256.0 35.1 %collective-permute-start.23 = (bf16[2,384,512]{2,1,0:T(8,128)(2,1)S(1)}, bf16[2,384,512]{2,1,0:T(8,128)(2,1)S(1)}, u32[]{:S(2)}, u32[]{:S(2)}) collective-permute-start(bf16[2,384,512]{2,1,0:T(8,128)(2,1)S(1)} %get-tuple-element.52), channel_id=1, source_target_pairs={{0,3},{1,2},{2,1},{3,0},{4,7},{5,6},{6,5},{7,4},{8,11},{9,10},{10,... | collective-permute-start | bytes 2359304 | tf_op jit(solution)/shard_map/ppermute | solution.py:26
  260.7 32.6 %collective-permute-start.39 = (bf16[32,4096]{1,0:T(8,128)(2,1)S(1)}, bf16[32,4096]{1,0:T(8,128)(2,1)S(1)}, u32[]{:S(2)}, u32[]{:S(2)}) collective-permute-start(bf16[32,4096]{1,0:T(8,128)(2,1)S(1)} %add_convert_fusion.2), channel_id=1, source_target_pairs={{0,64},{8,72},{16,80},{24,88},{32,96},{40,104},{48,112},{56,120},{... | collective-permute-start | bytes 786440 | tf_op jit(solution)/shard_map/ppermute | solution.py:26
  291.3 9.4 %collective-permute-start.24 = (bf16[384,512]{1,0:T(8,128)(2,1)S(1)}, bf16[384,512]{1,0:T(8,128)(2,1)S(1)}, u32[]{:S(2)}, u32[]{:S(2)}) collective-permute-start(bf16[384,512]{1,0:T(8,128)(2,1)S(1)} %fusion.4), channel_id=1, source_target_pairs={{0,4},{1,5},{2,6},{3,7},{4,0},{5,1},{6,2},{7,3},{8,12},{9,13},{10,... | collective-permute-start | bytes 1179656 | tf_op jit(solution)/shard_map/ppermute | solution.py:26
  (50 other events, 302.8 us)
Sparse Core Ops, SparseCore 0:
  10.3 68.0 all-gather.2
  124.6 109.4 reduce-scatter.1

commit v3 on v2

--- a/solution.py
+++ b/solution.py
@@ -17,8 +17,19 @@
 TN = (((0,), (0,)), ((), ()))
 
 
-def params(megabytes):
+def params(megabytes=60):
     return pltpu.CompilerParams(vmem_limit_bytes=megabytes << 20)
+
+
+def after(value, *others):
+    return lax.optimization_barrier((value, *others))[0]
+
+
+def ordered(kernel, inputs, tokens):
+    def run(*refs):
+        kernel(*refs[:inputs], *refs[inputs + len(tokens) :])
+
+    return run, [pl.BlockSpec(memory_space=pl.ANY) for _ in tokens]
 
 
 def flip(value, axis, bit):
@@ -35,25 +46,29 @@
     return low, high
 
 
-def exchange(blocks):
+def exchange(blocks, bits=(4, 2, 1)):
     shape = blocks.shape
     cube = blocks.reshape((2, 2, 2) + shape[1:])
-    for place, bit in enumerate((4, 2, 1)):
+    for bit in bits:
+        place = {4: 0, 2: 1, 1: 2}[bit]
         keep = lax.index_in_dim(cube, 0, place, keepdims=True)
         send = lax.index_in_dim(cube, 1, place, keepdims=True)
         cube = jnp.concatenate([keep, flip(send, "tp", bit)], axis=place)
     return cube.reshape(shape)
 
 
-def gather_small(value):
+def gather_small(value, beside=()):
     blocks = value[None]
     for bit in (1, 2, 4):
-        blocks = jnp.concatenate([blocks, flip(blocks, "tp", bit)], axis=0)
+        other = flip(blocks, "tp", bit)
+        if bit == 4 and beside:
+            other = after(other, *beside)
+        blocks = jnp.concatenate([blocks, other], axis=0)
     return blocks
 
 
-def sum_over_seq(value):
-    for bit in (1, 2, 4, 8):
+def sum_over_seq(value, bits=(1, 8, 2, 4)):
+    for bit in bits:
         sent = value.astype(BF16)
         value = sent.astype(F32) + flip(sent, "seq", bit).astype(F32)
     return value
@@ -75,15 +90,21 @@
 
 def hidden_logits_kernel(order, *refs):
     pieces = refs[:10]
-    gen_ref, full_ref, edge_ref, flat_ref, tap_ref = refs[10:]
+    gen_ref, full_ref, edge_ref, flat_ref, tap_ref, sems = refs[10:]
     members, rows, width = full_ref.shape
     half = rows // 2
-    for at, ref in zip((0, 1, 3, 4, 5, 7), pieces[:6]):
-        full_ref[order[at]] = ref[...]
-    full_ref[order[2], 0:half] = pieces[6][...]
-    full_ref[order[2], half:] = pieces[7][...]
-    full_ref[order[6], 0:half] = pieces[8][...]
-    full_ref[order[6], half:] = pieces[9][...]
+    targets = [full_ref.at[order[at]] for at in (0, 1, 3, 4, 5, 7)]
+    for at in (2, 6):
+        targets.append(full_ref.at[order[at], 0:half])
+        targets.append(full_ref.at[order[at], half:rows])
+    copies = [
+        pltpu.make_async_copy(ref, target, sems.at[index])
+        for index, (ref, target) in enumerate(zip(pieces, targets))
+    ]
+    for copy in copies:
+        copy.start()
+    for copy in copies:
+        copy.wait()
     logits = jnp.zeros((gen_ref.shape[0], rows), F32)
     for piece in range(members):
         edge_ref[0, piece] = full_ref[piece, 0:PAD]
@@ -109,7 +130,7 @@
     rows, width = pieces[0].shape
     columns, depth = gen_rows.shape
     members = depth // width
-    whole = [pl.BlockSpec(p.shape, lambda i, o: (0, 0)) for p in pieces]
+    whole = [pl.BlockSpec(memory_space=pltpu.HBM) for _ in pieces]
     return pl.pallas_call(
         hidden_logits_kernel,
         grid_spec=pltpu.PrefetchScalarGridSpec(
@@ -122,6 +143,7 @@
                 pl.BlockSpec((ROWS, rows), lambda i, o: (0, 0)),
                 pl.BlockSpec((rows, ROWS), lambda i, o: (0, 0)),
             ],
+            scratch_shapes=[pltpu.SemaphoreType.DMA((len(pieces),))],
         ),
         out_shape=(
             jax.ShapeDtypeStruct((members, rows, width), BF16),
@@ -129,7 +151,7 @@
             jax.ShapeDtypeStruct((ROWS, rows), F32),
             jax.ShapeDtypeStruct((rows, ROWS), F32),
         ),
-        compiler_params=params(32),
+        compiler_params=params(),
         name="hidden_logits",
     )(order, *pieces, gen_rows)
 
@@ -139,7 +161,8 @@
     hidden_ref,
     low_ref,
     high_ref,
-    flat_ref,
+    flat_one_ref,
+    flat_two_ref,
     up_ref,
     grad_ref,
     act_ref,
@@ -148,34 +171,42 @@
     padded,
     pre,
 ):
-    _, rows, width = hidden_ref.shape
+    count, rows, width = hidden_ref.shape
     step = 64
     reach = 2 * step
     heads = 2
     head_width = width // heads
-    padded[0:PAD] = low_ref[0]
-    padded[PAD : PAD + rows] = hidden_ref[0]
-    padded[PAD + rows : 2 * PAD + rows] = high_ref[0]
-    padded[2 * PAD + rows :] = jnp.zeros((padded.shape[0] - 2 * PAD - rows, width), BF16)
-    flat = flat_ref[0]
-    taps = jnp.concatenate([flat, jnp.zeros((reach - ROWS, rows), F32)], axis=0).T
     lane = lax.broadcasted_iota(jnp.int32, (step, reach), 1)
-    for base in range(0, rows, step):
-        for head in range(heads):
-            lanes = slice(head * head_width, (head + 1) * head_width)
-            mine = (lane >= head * KW) & (lane < (head + 1) * KW)
-            own = jnp.where(mine, taps[base : base + step], 0.0)
-            own = pltpu.roll(own, (1 - head * KW) % reach, 1)
-            band = pltpu.roll(own, 0, 1, stride=1, stride_axis=0)
-            upper = band.astype(BF16)
-            lower = (band - upper.astype(F32)).astype(BF16)
-            window = padded[base : base + reach, lanes]
-            total = jnp.dot(upper, window, preferred_element_type=F32) + jnp.dot(
-                lower, window, preferred_element_type=F32
-            )
-            value = hidden_ref[0, base : base + step, lanes].astype(F32) + total
-            act_ref[0, base : base + step, lanes] = value.astype(BF16)
-    term = jnp.dot(act_ref[0], up_ref[...], preferred_element_type=F32)
+    term = None
+    for piece, flat_ref in enumerate((flat_one_ref, flat_two_ref)):
+        padded[piece, 0:PAD] = low_ref[piece]
+        padded[piece, PAD : PAD + rows] = hidden_ref[piece]
+        padded[piece, PAD + rows : 2 * PAD + rows] = high_ref[piece]
+        padded[piece, 2 * PAD + rows :] = jnp.zeros((step - 2 * PAD, width), BF16)
+        flat = flat_ref[0]
+        taps = jnp.concatenate([flat, jnp.zeros((reach - ROWS, rows), F32)], axis=0).T
+        for base in range(0, rows, step):
+            for head in range(heads):
+                lanes = slice(head * head_width, (head + 1) * head_width)
+                mine = (lane >= head * KW) & (lane < (head + 1) * KW)
+                own = jnp.where(mine, taps[base : base + step], 0.0)
+                own = pltpu.roll(own, (1 - head * KW) % reach, 1)
+                band = pltpu.roll(own, 0, 1, stride=1, stride_axis=0)
+                upper = band.astype(BF16)
+                lower = (band - upper.astype(F32)).astype(BF16)
+                window = padded[piece, base : base + reach, lanes]
+                both = jnp.dot(
+                    jnp.concatenate([upper, lower], axis=0), window, preferred_element_type=F32
+                )
+                value = hidden_ref[piece, base : base + step, lanes].astype(F32)
+                value = value + (both[:step] + both[step:])
+                act_ref[piece, base : base + step, lanes] = value.astype(BF16)
+        part = jnp.dot(
+            act_ref[piece],
+            up_ref[piece * width : (piece + 1) * width, :],
+            preferred_element_type=F32,
+        )
+        term = part if term is None else term + part
 
     @pl.when(pl.program_id(0) == 0)
     def _():
@@ -212,22 +243,23 @@
         conv_up_kernel,
         grid_spec=pltpu.PrefetchScalarGridSpec(
             num_scalar_prefetch=1,
-            grid=(members,),
+            grid=(members // 2,),
             in_specs=[
-                pl.BlockSpec((1, rows, width), lambda i, o: (i, 0, 0)),
-                pl.BlockSpec((1, PAD, width), lambda i, o: (i, 0, 0)),
-                pl.BlockSpec((1, PAD, width), lambda i, o: (i, 0, 0)),
-                pl.BlockSpec((1, ROWS, rows), lambda i, o: (o[i], 0, 0)),
-                pl.BlockSpec((width, units), lambda i, o: (i, 0)),
+                pl.BlockSpec((2, rows, width), lambda i, o: (i, 0, 0)),
+                pl.BlockSpec((2, PAD, width), lambda i, o: (i, 0, 0)),
+                pl.BlockSpec((2, PAD, width), lambda i, o: (i, 0, 0)),
+                pl.BlockSpec((1, ROWS, rows), lambda i, o: (o[2 * i], 0, 0)),
+                pl.BlockSpec((1, ROWS, rows), lambda i, o: (o[2 * i + 1], 0, 0)),
+                pl.BlockSpec((2 * width, units), lambda i, o: (i, 0)),
                 pl.BlockSpec((rows, units), lambda i, o: (0, 0)),
             ],
             out_specs=[
-                pl.BlockSpec((1, rows, width), lambda i, o: (i, 0, 0)),
+                pl.BlockSpec((2, rows, width), lambda i, o: (i, 0, 0)),
                 pl.BlockSpec((rows, units), lambda i, o: (0, 0)),
                 pl.BlockSpec((rows, units), lambda i, o: (0, 0)),
             ],
             scratch_shapes=[
-                pltpu.VMEM((rows + 64, width), BF16),
+                pltpu.VMEM((2, rows + 64, width), BF16),
                 pltpu.VMEM((rows, units), F32),
             ],
         ),
@@ -236,9 +268,9 @@
             jax.ShapeDtypeStruct((rows, units), BF16),
             jax.ShapeDtypeStruct((rows, units), BF16),
         ),
-        compiler_params=params(40),
+        compiler_params=params(),
         name="conv_up",
-    )(order, hidden_full, low, high, flat_full, up_weight, middle_grad)
+    )(order, hidden_full, low, high, flat_full, flat_full, up_weight, middle_grad)
 
 
 def grad_middle_kernel(cot_ref, down_ref, out_ref):
@@ -267,7 +299,7 @@
         ],
         out_specs=pl.BlockSpec((rows, block), lambda i: (0, i)),
         out_shape=jax.ShapeDtypeStruct((rows, units), F32),
-        compiler_params=params(40),
+        compiler_params=params(),
         name="grad_middle",
     )(cot_full, down_weight)
 
@@ -302,9 +334,46 @@
             out_specs=[pl.BlockSpec((1, rows, width), lambda k, o: (k // 4, 0, 0))] * 4,
         ),
         out_shape=[jax.ShapeDtypeStruct((2, rows, width), BF16)] * 4,
-        compiler_params=params(40),
+        compiler_params=params(),
         name=name,
     )(order, value, weight)
+
+
+def halves_kernel(order, value_ref, weight_ref, near_ref, far_ref):
+    result = jnp.dot(value_ref[...], weight_ref[...], preferred_element_type=F32).astype(BF16)
+
+    @pl.when(pl.program_id(0) < 4)
+    def _():
+        far_ref[0] = result
+
+    @pl.when(pl.program_id(0) >= 4)
+    def _():
+        near_ref[0] = result
+
+
+def halves(order, value, weight, tokens):
+    rows, units = value.shape
+    width = weight.shape[1] // 8
+    kernel, token_specs = ordered(halves_kernel, 3, tokens)
+    return pl.pallas_call(
+        kernel,
+        grid_spec=pltpu.PrefetchScalarGridSpec(
+            num_scalar_prefetch=1,
+            grid=(8,),
+            in_specs=[
+                pl.BlockSpec((rows, units), lambda k, o: (0, 0)),
+                pl.BlockSpec((units, width), lambda k, o: (0, o[(k + 4) % 8])),
+            ]
+            + token_specs,
+            out_specs=[
+                pl.BlockSpec((1, rows, width), lambda k, o: (jnp.maximum(k - 4, 0), 0, 0)),
+                pl.BlockSpec((1, rows, width), lambda k, o: (jnp.minimum(k, 3), 0, 0)),
+            ],
+        ),
+        out_shape=[jax.ShapeDtypeStruct((4, rows, width), BF16)] * 2,
+        compiler_params=params(),
+        name="ffn_out",
+    )(order, value, weight, *tokens)
 
 
 def weight_grads_kernel(act_ref, cot_ref, pre_grad_ref, middle_ref, out_ref):
@@ -334,7 +403,7 @@
         ],
         out_specs=pl.BlockSpec((per, 2 * chunk, units), lambda i: (i, 0, 0)),
         out_shape=jax.ShapeDtypeStruct((chunks, 2 * chunk, units), BF16),
-        compiler_params=params(40),
+        compiler_params=params(),
         name="weight_grads",
     )(act_full, cot_full, pre_grad, middle)
 
@@ -381,15 +450,17 @@
     logit_ref[...] = found_ref[...].T.astype(BF16)
 
 
-def kernel_grads(pairs, last, cotangent, hidden, low, high, taps):
+def kernel_grads(pairs, last, cotangent, hidden, low, high, taps, tokens):
     rows, width = hidden.shape
     flat = pl.BlockSpec((rows, width), lambda i: (0, 0))
     edge = pl.BlockSpec((PAD, width), lambda i: (0, 0))
-    return pl.pallas_call(
-        kernel_grad_kernel,
+    kernel, token_specs = ordered(kernel_grad_kernel, 10, tokens)
+    return pl.pallas_call(
+        kernel,
         grid=(1,),
         in_specs=[pl.BlockSpec((None, rows, width), lambda i: (0, 0, 0))] * 4
-        + [flat, flat, flat, edge, edge, pl.BlockSpec((rows, ROWS), lambda i: (0, 0))],
+        + [flat, flat, flat, edge, edge, pl.BlockSpec((rows, ROWS), lambda i: (0, 0))]
+        + token_specs,
         out_specs=[flat, pl.BlockSpec((ROWS, rows), lambda i: (0, 0))],
         out_shape=(
             jax.ShapeDtypeStruct((rows, width), F32),
@@ -399,9 +470,9 @@
             pltpu.VMEM((rows + 2 * PAD, width), F32),
             pltpu.VMEM((rows, ROWS), F32),
         ],
-        compiler_params=params(32),
+        compiler_params=params(24),
         name="kernel_grads",
-    )(*pairs, last, cotangent, hidden, low, high, taps)
+    )(*pairs, last, cotangent, hidden, low, high, taps, *tokens)
 
 
 def hidden_grad_kernel(
@@ -465,10 +536,18 @@
     )
 
 
-def hidden_grads(grad, glow, ghigh, taps, tlow, thigh, logit_full, gen_full, mask, code, codes):
-    rows, width = grad.shape
-    return pl.pallas_call(
-        hidden_grad_kernel,
+def hidden_grads(operands, codes, tokens):
+    rows, width = operands[0].shape
+    kernel, token_specs = ordered(hidden_grad_kernel, len(operands), tokens)
+    whole = [pl.BlockSpec(o.shape, lambda i: (0, 0)) for o in operands]
+    return pl.pallas_call(
+        kernel,
+        grid=(1,),
+        in_specs=whole + token_specs,
+        out_specs=[
+            pl.BlockSpec((rows, width), lambda i: (0, 0)),
+            pl.BlockSpec((codes, width), lambda i: (0, 0)),
+        ],
         out_shape=(
             jax.ShapeDtypeStruct((rows, width), F32),
             jax.ShapeDtypeStruct((codes, width), F32),
@@ -478,9 +557,38 @@
             pltpu.VMEM((rows + 2 * PAD, ROWS), F32),
             pltpu.VMEM((rows, width), F32),
         ],
-        compiler_params=params(32),
+        compiler_params=params(24),
         name="hidden_grads",
-    )(grad, glow, ghigh, taps, tlow, thigh, logit_full, gen_full, mask, code)
+    )(*operands, *tokens)
+
+
+def gen_blocks_kernel(order, gen_ref, token_ref, out_ref):
+    columns = gen_ref.shape[0]
+    members, _, width = out_ref.shape
+    out_ref[...] = jnp.zeros_like(out_ref)
+    for k in range(members):
+        at = pl.multiple_of(order[k] * width, width)
+        out_ref[k, 0:columns] = gen_ref[:, pl.ds(at, width)]
+
+
+def gen_blocks(order, gen_rows, width, token):
+    columns, depth = gen_rows.shape
+    members = depth // width
+    return pl.pallas_call(
+        gen_blocks_kernel,
+        grid_spec=pltpu.PrefetchScalarGridSpec(
+            num_scalar_prefetch=1,
+            grid=(1,),
+            in_specs=[
+                pl.BlockSpec((columns, depth), lambda i, o: (0, 0)),
+                pl.BlockSpec(memory_space=pl.ANY),
+            ],
+            out_specs=pl.BlockSpec((members, ROWS, width), lambda i, o: (0, 0, 0)),
+        ),
+        out_shape=jax.ShapeDtypeStruct((members, ROWS, width), BF16),
+        compiler_params=params(24),
+        name="gen_blocks",
+    )(order, gen_rows, token)
 
 
 def gen_grads_kernel(logit_ref, hidden_ref, out_ref):
@@ -497,19 +605,15 @@
     return pl.pallas_call(
         gen_grads_kernel,
         out_shape=jax.ShapeDtypeStruct((heads, members * width), F32),
-        compiler_params=params(32),
+        compiler_params=params(24),
         name="gen_grads",
     )(logit_grad, hidden_full)
 
 
-def after(value, *others):
-    return lax.optimization_barrier((value, *others))[0]
-
-
-def add_pairs(pairs, index):
-    total = pairs[0][index].astype(F32)
-    for pair in pairs[1:]:
-        total = total + pair[index].astype(F32)
+def add_up(values):
+    total = values[0].astype(F32)
+    for value in values[1:]:
+        total = total + value.astype(F32)
     return total
 
 
@@ -545,57 +649,63 @@
     count = lax.axis_size("seq")
     low_full = lax.ppermute(low_full, "seq", [(i, i + 1) for i in range(count - 1)])
     high_full = lax.ppermute(high_full, "seq", [(i + 1, i) for i in range(count - 1)])
-    flat_full = gather_small(flat)
     middle_grad = grad_middle(cot_full, down_weight)
+    flat_full = gather_small(flat, (middle_grad,))
     act_full, middle, pre_grad = conv_up(
         order, hidden_full, low_full, high_full, flat_full, up_weight, middle_grad
     )
 
     summed = weight_grads(act_full, cot_full, pre_grad, middle)
-    back_pairs = swap_pairs(spread(order, pre_grad, up_weight, True, "act_back"))
+    back_own = spread(order, pre_grad, up_weight, True, "act_back")
+    back_pairs = swap_pairs(back_own)
     summed = lax.psum_scatter(summed, "seq", scatter_dimension=0, tiled=False)
-    out_pairs = spread(order, middle, down_weight, False, "ffn_out")
-
     columns = gen_weight.shape[1]
-    gen_rows = jnp.pad(gen_weight.T, ((0, ROWS - columns), (0, 0)))
-    gen_own = jnp.stack(
-        [
-            lax.dynamic_slice(gen_rows, (jnp.int32(0), order[k] * width), (ROWS, width))
-            for k in range(members)
-        ]
-    )
-    gen_full = exchange(after(gen_own, pre_grad)).reshape(members * ROWS, width)
+    gen_full = gen_blocks(order, gen_weight.T, width, back_own[0])
+    out_near, out_far = halves(order, middle, down_weight, (back_pairs[1],))
+    out_far = flip(out_far, "tp", 4)
+
+    gen_full = exchange(gen_full).reshape(members * ROWS, width)
     tap_low, tap_high = halo(taps)
 
-    back_last = flip(add_pairs(back_pairs, 1).astype(BF16), "tp", 4)
+    back_last = flip(add_up([pair[1] for pair in back_pairs]).astype(BF16), "tp", 4)
     low = lax.dynamic_index_in_dim(low_full, me, 0, keepdims=False)
     high = lax.dynamic_index_in_dim(high_full, me, 0, keepdims=False)
     grad, logit_grad = kernel_grads(
-        back_pairs, back_last, after(cotangent, *out_pairs, gen_full), hidden, low, high, taps
+        back_pairs,
+        back_last,
+        cotangent,
+        hidden,
+        low,
+        high,
+        taps,
+        (out_far, gen_full, tap_low, tap_high),
     )
     grad_low, grad_high = halo(grad.astype(BF16))
     logit_full = gather_small(logit_grad).reshape(members * ROWS, rows)
+    gen_sum = sum_over_seq(gen_grads(logit_grad, hidden_full), (1, 8))
+    out_sums = [add_up([out_near[z], out_far[z]]) for z in range(members // 2)]
+    out_one, out_two, out_three = [flip(out_sums[z].astype(BF16), "tp", z) for z in (1, 2, 3)]
     embed_grad, table_part = hidden_grads(
-        grad,
-        grad_low,
-        grad_high,
-        taps,
-        tap_low,
-        tap_high,
-        logit_full,
-        gen_full,
-        span_mask[:, None],
-        sentinel_id[None, :],
+        (
+            grad,
+            grad_low,
+            grad_high,
+            taps,
+            tap_low,
+            tap_high,
+            logit_full,
+            gen_full,
+            span_mask[:, None],
+            sentinel_id[None, :],
+        ),
         codes,
+        (gen_sum, out_one, out_three),
     )
-    gen_sum = sum_over_seq(gen_grads(logit_grad, hidden_full))
+    gen_sum = sum_over_seq(gen_sum, (2, 4))
     gen_grad = gen_sum[:columns].T
     table_grad = sum_over_seq(table_part)
 
-    out_pairs = swap_pairs([after(pair, grad) for pair in out_pairs])
-    total = add_pairs(out_pairs, 0) + flip(
-        add_pairs(out_pairs, 1).astype(BF16), "tp", 4
-    ).astype(F32)
+    total = add_up([out_sums[0], out_one, out_two, out_three])
     act = lax.dynamic_index_in_dim(act_full, me, 0, keepdims=False)
     layer_output = (act.astype(F32) + total).astype(BF16)
 

time: 317 us -> 322 us (1.016)
  local copies, waits for them, and re-layouts: 34.9 us -> 7.41 us
  waiting for transfers between devices: 125 us -> 147 us
  Pallas kernels: 56.9 us -> 76.4 us
  starting transfers between devices: 66.9 us -> 61.4 us
  between operations: 19.6 us -> 14.5 us
    unnamed x88 -> x55, local copies, waits for them, and re-layouts: 31.9 us -> 3.53 us
    ppermute x34, waiting for transfers between devices: 124 us -> 146 us  [flip(): return lax.ppermute(value, axis, [(i, i ^ bit) for i in range(count)])]
    pallas_call x2 -> x4, Pallas kernels: 9.78 us -> 20.9 us  [the longest x1 10.6 us: halves(): pl.pallas_call(kernel, grid_spec=pltpu.PrefetchScalarGridSpec(num_scalar_...]
    pallas_call x1, Pallas kernels: 4.15 us -> 8.28 us  [grad_middle(): pl.pallas_call(grad_middle_kernel, grid=(units // block,), in_specs=[pl.B...]
    ppermute x34, starting transfers between devices: 53.3 us -> 49.5 us  [flip(): return lax.ppermute(value, axis, [(i, i ^ bit) for i in range(count)])]
    pallas_call x1, Pallas kernels: 1.92 us -> 5.37 us  [hidden_logits(): pl.pallas_call(hidden_logits_kernel, grid_spec=pltpu.PrefetchScalarGridSp...]
    pallas_call x2 -> x1, Pallas kernels: 13.7 us -> 11.1 us  [spread(): pl.pallas_call(functools.partial(spread_kernel, dims), grid_spec=pltpu.Pr...]
  transfers between devices with their start and end apart: 42 -> 42, of which waited for: 26 -> 24; matrix products, arithmetic and copies ran while one was open for 4% -> 5% of each run, Pallas kernels for 10% -> 14%
where the time goes in v3:
time: 322 us; the launch traced here: 320 us
  waiting for transfers between devices  147 us (46%)
  Pallas kernels  76.4 us (24%)
  starting transfers between devices  61.4 us (19%)
  between operations  14.5 us (5%)
  other arithmetic  11.8 us (4%)
  local copies, waits for them, and re-layouts  7.41 us (2%)
    ppermute x34, waiting for transfers between devices, flip(): return lax.ppermute(value, axis, [(i, i ^ bit) for i in range(count)])  146 us
    ppermute x34, starting transfers between devices, flip(): return lax.ppermute(value, axis, [(i, i ^ bit) for i in range(count)])  49.5 us
    pallas_call x1, Pallas kernels, conv_up(): pl.pallas_call(conv_up_kernel, grid_spec=pltpu.PrefetchScalarGridSpec(num...  15.4 us
    pallas_call x1, Pallas kernels, weight_grads(): pl.pallas_call(weight_grads_kernel, grid=(pieces,), in_specs=[pl.BlockSpe...  14.6 us
    pallas_call x1, Pallas kernels, spread(): pl.pallas_call(functools.partial(spread_kernel, dims), grid_spec=pltpu.Pr...  11.1 us
    pallas_call x1, Pallas kernels, halves(): pl.pallas_call(kernel, grid_spec=pltpu.PrefetchScalarGridSpec(num_scalar_...  10.6 us
    pallas_call x1, Pallas kernels, grad_middle(): pl.pallas_call(grad_middle_kernel, grid=(units // block,), in_specs=[pl.B...  8.28 us
  transfers between devices with their start and end apart: 42, of which 24 were waited for; matrix products, arithmetic and copies ran while one was open for 5% of the time, Pallas kernels for 14%

profile of v3, /device:TPU:0, one launch (start us, length us, event | category | flops | bytes accessed | tf_op | source)
XLA Modules:
  0.0 320.1 jit_solution(1767843352517666436)
XLA Ops:
  10.0 3.2 collective-permute-start.2
  13.2 4.0 %collective-permute-start.1 = (bf16[384,512]{1,0:T(8,128)(2,1)S(1)}, bf16[384,512]{1,0:T(8,128)(2,1)S(1)}, u32[]{:S(2)}, u32[]{:S(2)}) collective-permute-start(bf16[384,512]{1,0:T(8,128)(2,1)S(1)} %fusion.refs_0_.refs_6_), channel_id=1, source_target_pairs={{0,3},{1,2},{2,1},{3,0},{4,7},{5,6},{6,5},{7,4},{8,11},{9,10},{10,... | collective-permute-start | bytes 1179656 | tf_op jit(solution)/shard_map/ppermute | solution.py:37
  17.2 5.1 %collective-permute-done.2.refs_3_ = bf16[384,512]{1,0:T(8,128)(2,1)S(1)} collective-permute-done((bf16[384,512]{1,0:T(8,128)(2,1)S(1)}, bf16[384,512]{1,0:T(8,128)(2,1)S(1)}, u32[]{:S(2)}, u32[]{:S(2)}) %collective-permute-start.2) | collective-permute-done | bytes 393248 | tf_op jit(solution)/shard_map/ppermute | solution.py:37
  22.3 4.3 %collective-permute-start.4 = (bf16[384,512]{1,0:T(8,128)(2,1)S(1)}, bf16[384,512]{1,0:T(8,128)(2,1)S(1)}, u32[]{:S(2)}, u32[]{:S(2)}) collective-permute-start(bf16[384,512]{1,0:T(8,128)(2,1)S(1)} %collective-permute-done.2.refs_3_), channel_id=1, source_target_pairs={{0,3},{1,2},{2,1},{3,0},{4,7},{5,6},{6,5},{7,4},{8,11},{9,10},{10,... | collective-permute-start | bytes 1179656 | tf_op jit(solution)/shard_map/ppermute | solution.py:37
  32.3 9.8 %collective-permute-done.4.refs_5_ = bf16[384,512]{1,0:T(8,128)(2,1)S(1)} collective-permute-done((bf16[384,512]{1,0:T(8,128)(2,1)S(1)}, bf16[384,512]{1,0:T(8,128)(2,1)S(1)}, u32[]{:S(2)}, u32[]{:S(2)}) %collective-permute-start.4) | collective-permute-done | bytes 393248 | tf_op jit(solution)/shard_map/ppermute | solution.py:37
  47.4 4.2 %collective-permute-done.8.refs_9_ = bf16[192,512]{1,0:T(8,128)(2,1)S(1)} collective-permute-done((bf16[192,512]{1,0:T(8,128)(2,1)}, bf16[192,512]{1,0:T(8,128)(2,1)S(1)}, u32[]{:S(2)}, u32[]{:S(2)}) %collective-permute-start.8) | collective-permute-done | bytes 196640 | tf_op jit(solution)/shard_map/ppermute | solution.py:37
  53.6 5.4 %hidden_logits.1 = (bf16[8,384,512]{2,1,0:T(8,128)(2,1)}, bf16[2,8,8,512]{3,2,1,0:T(8,128)(2,1)}, f32[32,384]{1,0:T(8,128)}, f32[384,32]{1,0:T(8,128)}) custom-call(s32[8]{0:T(128)} %iota_xor_fusion.order.refs_0_, bf16[384,512]{1,0:T(8,128)(2,1)} %copy-done.6, bf16[384,512]{1,0:T(8,128)(2,1)} %copy-done.14, bf16[384,512]{1,0:T(8,128)(2,1)} %copy-done.13, ...), custom_call_target="tpu_custom_call" | custom-call | tf_op jit(solution)/shard_map/hidden_logits/pallas_call | solution.py:134
  59.7 4.7 %collective-permute-done.11 = f32[1,32,384]{2,1,0:T(8,128)S(1)} collective-permute-done((f32[1,32,384]{2,1,0:T(8,128)}, f32[1,32,384]{2,1,0:T(8,128)S(1)}, u32[]{:S(2)}, u32[]{:S(2)}) %collective-permute-start.11) | collective-permute-done | bytes 49184 | tf_op jit(solution)/shard_map/ppermute | solution.py:37
  65.2 3.1 collective-permute-start.12
  68.3 3.8 %collective-permute-done.12 = f32[2,32,384]{2,1,0:T(8,128)S(1)} collective-permute-done((f32[2,32,384]{2,1,0:T(8,128)S(1)}, f32[2,32,384]{2,1,0:T(8,128)S(1)}, u32[]{:S(2)}, u32[]{:S(2)}) %collective-permute-start.12) | collective-permute-done | bytes 98336 | tf_op jit(solution)/shard_map/ppermute | solution.py:37
  76.1 3.0 collective-permute-start.9
  79.2 8.3 %grad_middle.1.grad_ref = f32[384,1024]{1,0:T(8,128)} custom-call(bf16[8,384,512]{2,1,0:T(8,128)(2,1)} %bitcast.59, bf16[1024,4096]{1,0:T(8,128)(2,1)} %refs_2_.1), custom_call_target="tpu_custom_call" | custom-call | tf_op jit(solution)/shard_map/grad_middle/pallas_call | solution.py:293
  88.9 15.4 %conv_up.1 = (bf16[8,384,512]{2,1,0:T(8,128)(2,1)}, bf16[384,1024]{1,0:T(8,128)(2,1)}, bf16[384,1024]{1,0:T(8,128)(2,1)}) custom-call(s32[8]{0:T(128)} %iota_xor_fusion.order.refs_0_, bf16[8,384,512]{2,1,0:T(8,128)(2,1)} %get-tuple-element.24.hidden_ref, bf16[8,8,512]{2,1,0:T(8,128)(2,1)} %copy-done.24, bf16[8,8,512]{2,1,0:T(8,128)(2,1)} %copy-done.23, ...), custom_call_target="tpu_custom_call" | custom-call | tf_op jit(solution)/shard_map/conv_up/pallas_call | solution.py:242
  104.3 14.6 %weight_grads.1 = bf16[16,512,1024]{2,1,0:T(8,128)(2,1)} custom-call(bf16[8,384,512]{2,1,0:T(8,128)(2,1)} %get-tuple-element.28.act_ref, bf16[8,384,512]{2,1,0:T(8,128)(2,1)} %bitcast.60, bf16[384,1024]{1,0:T(8,128)(2,1)} %get-tuple-element.30.value_ref.pre_grad_ref, bf16[384,1024]{1,0:T(8,128)(2,1)} %get-tuple-element.29.refs_1_.middle_ref), custom_call_target="tpu_custom_call" | custom-call | tf_op jit(solution)/shard_map/weight_grads/pallas_call | solution.py:395
  118.9 11.1 %act_back.1 = (bf16[2,384,512]{2,1,0:T(8,128)(2,1)}, bf16[2,384,512]{2,1,0:T(8,128)(2,1)}, bf16[2,384,512]{2,1,0:T(8,128)(2,1)}, bf16[2,384,512]{2,1,0:T(8,128)(2,1)}) custom-call(s32[8]{0:T(128)} %iota_xor_fusion.order.refs_0_, bf16[384,1024]{1,0:T(8,128)(2,1)} %get-tuple-element.30.value_ref.pre_grad_ref, bf16[4096,1024]{1,0:T(8,128)(2,1)} %weight_ref.1), custom_call_target="tpu_custom_call" | custom-call | tf_op jit(solution)/shard_map/act_back/pallas_call | solution.py:328
  130.4 19.9 %collective-permute-done.14.refs_3_.refs_1_ = bf16[2,384,512]{2,1,0:T(8,128)(2,1)S(1)} collective-permute-done((bf16[2,384,512]{2,1,0:T(8,128)(2,1)}, bf16[2,384,512]{2,1,0:T(8,128)(2,1)S(1)}, u32[]{:S(2)}, u32[]{:S(2)}) %collective-permute-start.14) | collective-permute-done | bytes 786464 | tf_op jit(solution)/shard_map/ppermute | solution.py:37
  151.2 10.6 %ffn_out.1 = (bf16[4,384,512]{2,1,0:T(8,128)(2,1)}, bf16[4,384,512]{2,1,0:T(8,128)(2,1)}) custom-call(s32[8]{0:T(128)} %iota_xor_fusion.order.refs_0_, bf16[384,1024]{1,0:T(8,128)(2,1)} %get-tuple-element.29.refs_1_.middle_ref, bf16[1024,4096]{1,0:T(8,128)(2,1)} %refs_2_.1, bf16[2,384,512]{2,1,0:T(8,128)(2,1)} %copy-done.3), custom_call_target="tpu_custom_call" | custom-call | tf_op jit(solution)/shard_map/ffn_out/pallas_call | solution.py:358
  161.7 2.9 collective-permute-start.15
  164.6 4.0 %collective-permute-start.19 = (bf16[2,384,512]{2,1,0:T(8,128)(2,1)}, bf16[2,384,512]{2,1,0:T(8,128)(2,1)}, u32[]{:S(2)}, u32[]{:S(2)}) collective-permute-start(bf16[2,384,512]{2,1,0:T(8,128)(2,1)} %get-tuple-element.35), channel_id=1, source_target_pairs={{0,2},{1,3},{2,0},{3,1},{4,6},{5,7},{6,4},{7,5},{8,10},{9,11},{10,... | collective-permute-start | bytes 2359304 | tf_op jit(solution)/shard_map/ppermute | solution.py:37
  171.3 50.4 %collective-permute-done.22 = bf16[1,2,2,32,512]{4,3,2,1,0:T(8,128)(2,1)S(1)} collective-permute-done((bf16[1,2,2,32,512]{4,3,2,1,0:T(8,128)(2,1)S(1)}, bf16[1,2,2,32,512]{4,3,2,1,0:T(8,128)(2,1)S(1)}, u32[]{:S(2)}, u32[]{:S(2)}) %collective-permute-start.22) | collective-permute-done | bytes 131104 | tf_op jit(solution)/shard_map/ppermute | solution.py:37
  223.8 4.1 %collective-permute-start.23 = (bf16[2,1,2,32,512]{4,3,2,1,0:T(8,128)(2,1)S(1)}, bf16[2,1,2,32,512]{4,3,2,1,0:T(8,128)(2,1)S(1)}, u32[]{:S(2)}, u32[]{:S(2)}) collective-permute-start(bf16[2,1,2,32,512]{4,3,2,1,0:T(8,128)(2,1)S(1)} %get-tuple-element.66), channel_id=1, source_target_pairs={{0,2},{1,3},{2,0},{3,1},{4,6},{5,7},{6,4},{7,5},{8,10},{9,11},{10,... | collective-permute-start | bytes 393224 | tf_op jit(solution)/shard_map/ppermute | solution.py:37
  233.4 3.5 %collective-permute-done.24 = bf16[2,2,1,32,512]{4,3,2,1,0:T(8,128)(2,1)S(1)} collective-permute-done((bf16[2,2,1,32,512]{4,3,2,1,0:T(8,128)(2,1)S(1)}, bf16[2,2,1,32,512]{4,3,2,1,0:T(8,128)(2,1)S(1)}, u32[]{:S(2)}, u32[]{:S(2)}) %collective-permute-start.24) | collective-permute-done | bytes 131104 | tf_op jit(solution)/shard_map/ppermute | solution.py:37
  237.0 9.6 %collective-permute-done.21.refs_4_ = bf16[384,512]{1,0:T(8,128)(2,1)S(1)} collective-permute-done((bf16[384,512]{1,0:T(8,128)(2,1)S(1)}, bf16[384,512]{1,0:T(8,128)(2,1)S(1)}, u32[]{:S(2)}, u32[]{:S(2)}) %collective-permute-start.21) | collective-permute-done | bytes 393248 | tf_op jit(solution)/shard_map/ppermute | solution.py:37
  246.7 5.1 %kernel_grads.1 = (f32[384,512]{1,0:T(8,128)S(1)}, bf16[32,384]{1,0:T(8,128)(2,1)S(1)}) custom-call(bf16[2,384,512]{2,1,0:T(8,128)(2,1)S(1)} %copy-done.5, bf16[2,384,512]{2,1,0:T(8,128)(2,1)S(1)} %copy-done.4, bf16[2,384,512]{2,1,0:T(8,128)(2,1)} %collective-permute-done.19.refs_2_, bf16[2,384,512]{2,1,0:T(8,128)(2,1)} %collective-permute-done.20.refs_3_, ...), custom_call_target="tpu_custom_call" | custom-call | tf_op jit(solution)/shard_map/kernel_grads/pallas_call | solution.py:458
  257.2 3.0 collective-permute-start.27
  265.2 3.3 %collective-permute-done.31 = bf16[4,32,384]{2,1,0:T(8,128)(2,1)S(1)} collective-permute-done((bf16[4,32,384]{2,1,0:T(8,128)(2,1)S(1)}, bf16[4,32,384]{2,1,0:T(8,128)(2,1)S(1)}, u32[]{:S(2)}, u32[]{:S(2)}) %collective-permute-start.31) | collective-permute-done | bytes 98336 | tf_op jit(solution)/shard_map/ppermute | solution.py:37
  273.9 4.8 %collective-permute-done.18.refs_12_ = bf16[384,512]{1,0:T(8,128)(2,1)S(1)} collective-permute-done((bf16[384,512]{1,0:T(8,128)(2,1)S(1)}, bf16[384,512]{1,0:T(8,128)(2,1)S(1)}, u32[]{:S(2)}, u32[]{:S(2)}) %collective-permute-start.18) | collective-permute-done | bytes 393248 | tf_op jit(solution)/shard_map/ppermute | solution.py:37
  278.7 4.8 %hidden_grads.1 = (f32[384,512]{1,0:T(8,128)}, f32[100,512]{1,0:T(8,128)S(1)}) custom-call(f32[384,512]{1,0:T(8,128)S(1)} %get-tuple-element.38.refs_0_, bf16[8,512]{1,0:T(8,128)(2,1)S(1)} %collective-permute-done.27.refs_1_, bf16[8,512]{1,0:T(8,128)(2,1)S(1)} %collective-permute-done.28.refs_2_, f32[384,32]{1,0:T(8,128)S(1)} %copy-done.10, ...), custom_call_target="tpu_custom_call" | custom-call | tf_op jit(solution)/shard_map/hidden_grads/pallas_call | solution.py:543
  287.1 3.0 collective-permute-done.35
  290.2 4.2 %collective-permute-done.38 = bf16[32,4096]{1,0:T(8,128)(2,1)S(1)} collective-permute-done((bf16[32,4096]{1,0:T(8,128)(2,1)S(1)}, bf16[32,4096]{1,0:T(8,128)(2,1)S(1)}, u32[]{:S(2)}, u32[]{:S(2)}) %collective-permute-start.38) | collective-permute-done | bytes 262176 | tf_op jit(solution)/shard_map/ppermute | solution.py:37
  294.5 4.3 %collective-permute-start.39 = (bf16[32,4096]{1,0:T(8,128)(2,1)S(1)}, bf16[32,4096]{1,0:T(8,128)(2,1)S(1)}, u32[]{:S(2)}, u32[]{:S(2)}) collective-permute-start(bf16[32,4096]{1,0:T(8,128)(2,1)S(1)} %add_convert_fusion.4), channel_id=1, source_target_pairs={{0,32},{8,40},{16,48},{24,56},{32,0},{40,8},{48,16},{56,24},{64,96... | collective-permute-start | bytes 786440 | tf_op jit(solution)/shard_map/ppermute | solution.py:37
  302.7 5.3 %collective-permute-done.37 = bf16[100,512]{1,0:T(8,128)(2,1)S(1)} collective-permute-done((bf16[100,512]{1,0:T(8,128)(2,1)S(1)}, bf16[100,512]{1,0:T(8,128)(2,1)S(1)}, u32[]{:S(2)}, u32[]{:S(2)}) %collective-permute-start.37) | collective-permute-done | bytes 102432 | tf_op jit(solution)/shard_map/ppermute | solution.py:37
  (158 shorter events, 62.7 us)
Async XLA Ops:
  7.2 72.0 %all-gather.3.cloned.1.call-start = ((), (), s32[]{:S(2)}) async-start(), calls=%async_computation.2 | async-start | bytes 3538944 | tf_op jit(solution)/shard_map/all_gather | solution.py:645
  7.9 301.7 %reduce-scatter.2.cloned.1.call-start = ((), (), s32[]{:S(2)}) async-start(), calls=%async_computation.1 | async-start | bytes 17825792 | tf_op jit(solution)/shard_map/reduce_scatter | solution.py:661
  10.0 12.3 %collective-permute-start.2 = (bf16[384,512]{1,0:T(8,128)(2,1)S(1)}, bf16[384,512]{1,0:T(8,128)(2,1)S(1)}, u32[]{:S(2)}, u32[]{:S(2)}) collective-permute-start(bf16[384,512]{1,0:T(8,128)(2,1)S(1)} %fusion.refs_0_.refs_6_), channel_id=1, source_target_pairs={{0,4},{1,5},{2,6},{3,7},{4,0},{5,1},{6,2},{7,3},{8,12},{9,13},{10,... | collective-permute-start | bytes 1179656 | tf_op jit(solution)/shard_map/ppermute | solution.py:37
  13.2 15.2 %collective-permute-start.1 = (bf16[384,512]{1,0:T(8,128)(2,1)S(1)}, bf16[384,512]{1,0:T(8,128)(2,1)S(1)}, u32[]{:S(2)}, u32[]{:S(2)}) collective-permute-start(bf16[384,512]{1,0:T(8,128)(2,1)S(1)} %fusion.refs_0_.refs_6_), channel_id=1, source_target_pairs={{0,3},{1,2},{2,1},{3,0},{4,7},{5,6},{6,5},{7,4},{8,11},{9,10},{10,... | collective-permute-start | bytes 1179656 | tf_op jit(solution)/shard_map/ppermute | solution.py:37
  17.2 13.4 %collective-permute-start = (bf16[384,512]{1,0:T(8,128)(2,1)S(1)}, bf16[384,512]{1,0:T(8,128)(2,1)S(1)}, u32[]{:S(2)}, u32[]{:S(2)}) collective-permute-start(bf16[384,512]{1,0:T(8,128)(2,1)S(1)} %fusion.refs_0_.refs_6_), channel_id=1, source_target_pairs={{0,1},{1,0},{2,3},{3,2},{4,5},{5,4},{6,7},{7,6},{8,9},{9,8},{10,11... | collective-permute-start | bytes 1179656 | tf_op jit(solution)/shard_map/ppermute | solution.py:37
  22.3 19.7 %collective-permute-start.4 = (bf16[384,512]{1,0:T(8,128)(2,1)S(1)}, bf16[384,512]{1,0:T(8,128)(2,1)S(1)}, u32[]{:S(2)}, u32[]{:S(2)}) collective-permute-start(bf16[384,512]{1,0:T(8,128)(2,1)S(1)} %collective-permute-done.2.refs_3_), channel_id=1, source_target_pairs={{0,3},{1,2},{2,1},{3,0},{4,7},{5,6},{6,5},{7,4},{8,11},{9,10},{10,... | collective-permute-start | bytes 1179656 | tf_op jit(solution)/shard_map/ppermute | solution.py:37
  26.6 16.7 %collective-permute-start.3 = (bf16[384,512]{1,0:T(8,128)(2,1)S(1)}, bf16[384,512]{1,0:T(8,128)(2,1)S(1)}, u32[]{:S(2)}, u32[]{:S(2)}) collective-permute-start(bf16[384,512]{1,0:T(8,128)(2,1)S(1)} %collective-permute-done.2.refs_3_), channel_id=1, source_target_pairs={{0,1},{1,0},{2,3},{3,2},{4,5},{5,4},{6,7},{7,6},{8,9},{9,8},{10,11... | collective-permute-start | bytes 1179656 | tf_op jit(solution)/shard_map/ppermute | solution.py:37
  28.4 19.1 %collective-permute-start.6 = (bf16[192,512]{1,0:T(8,128)(2,1)S(1)}, bf16[192,512]{1,0:T(8,128)(2,1)S(1)}, u32[]{:S(2)}, u32[]{:S(2)}) collective-permute-start(bf16[192,512]{1,0:T(8,128)(2,1)S(1)} %slice.135), channel_id=1, source_target_pairs={{0,1},{1,0},{2,3},{3,2},{4,5},{5,4},{6,7},{7,6},{8,9},{9,8},{10,11... | collective-permute-start | bytes 589832 | tf_op jit(solution)/shard_map/ppermute | solution.py:37
  30.6 16.8 %collective-permute-start.5 = (bf16[192,512]{1,0:T(8,128)(2,1)S(1)}, bf16[192,512]{1,0:T(8,128)(2,1)S(1)}, u32[]{:S(2)}, u32[]{:S(2)}) collective-permute-start(bf16[192,512]{1,0:T(8,128)(2,1)S(1)} %slice.134), channel_id=1, source_target_pairs={{0,3},{1,2},{2,1},{3,0},{4,7},{5,6},{6,5},{7,4},{8,11},{9,10},{10,... | collective-permute-start | bytes 589832 | tf_op jit(solution)/shard_map/ppermute | solution.py:37
  42.8 8.8 %collective-permute-start.8 = (bf16[192,512]{1,0:T(8,128)(2,1)}, bf16[192,512]{1,0:T(8,128)(2,1)S(1)}, u32[]{:S(2)}, u32[]{:S(2)}) collective-permute-start(bf16[192,512]{1,0:T(8,128)(2,1)} %slice.137), channel_id=1, source_target_pairs={{0,1},{1,0},{2,3},{3,2},{4,5},{5,4},{6,7},{7,6},{8,9},{9,8},{10,11... | collective-permute-start | bytes 589832 | tf_op jit(solution)/shard_map/ppermute | solution.py:37
  43.9 9.0 %collective-permute-start.7 = (bf16[192,512]{1,0:T(8,128)(2,1)}, bf16[192,512]{1,0:T(8,128)(2,1)S(1)}, u32[]{:S(2)}, u32[]{:S(2)}) collective-permute-start(bf16[192,512]{1,0:T(8,128)(2,1)} %slice.136), channel_id=1, source_target_pairs={{0,3},{1,2},{2,1},{3,0},{4,7},{5,6},{6,5},{7,4},{8,11},{9,10},{10,... | collective-permute-start | bytes 589832 | tf_op jit(solution)/shard_map/ppermute | solution.py:37
  72.9 14.6 %collective-permute-start.13 = (f32[4,32,384]{2,1,0:T(8,128)S(1)}, f32[4,32,384]{2,1,0:T(8,128)S(1)}, u32[]{:S(2)}, u32[]{:S(2)}) collective-permute-start(f32[4,32,384]{2,1,0:T(8,128)S(1)} %pad_maximum_fusion.2), channel_id=1, source_target_pairs={{0,4},{1,5},{2,6},{3,7},{4,0},{5,1},{6,2},{7,3},{8,12},{9,13},{10,... | collective-permute-start | bytes 589832 | tf_op jit(solution)/shard_map/ppermute | solution.py:37
  74.8 13.4 %collective-permute-start.10 = (bf16[8,8,512]{2,1,0:T(8,128)(2,1)S(1)}, bf16[8,8,512]{2,1,0:T(8,128)(2,1)S(1)}, u32[]{:S(2)}, u32[]{:S(2)}) collective-permute-start(bf16[8,8,512]{2,1,0:T(8,128)(2,1)S(1)} %get-tuple-element.71), channel_id=1, source_target_pairs={{8,0},{16,8},{24,16},{32,24},{40,32},{48,40},{56,48},{64,56},{72,6... | collective-permute-start | bytes 196616 | tf_op jit(solution)/shard_map/ppermute | solution.py:651
  76.1 12.1 %collective-permute-start.9 = (bf16[8,8,512]{2,1,0:T(8,128)(2,1)S(1)}, bf16[8,8,512]{2,1,0:T(8,128)(2,1)S(1)}, u32[]{:S(2)}, u32[]{:S(2)}) collective-permute-start(bf16[8,8,512]{2,1,0:T(8,128)(2,1)S(1)} %get-tuple-element.72), channel_id=1, source_target_pairs={{0,8},{8,16},{16,24},{24,32},{32,40},{40,48},{48,56},{56,64},{64,7... | collective-permute-start | bytes 196616 | tf_op jit(solution)/shard_map/ppermute | solution.py:650
  130.1 20.2 %collective-permute-start.14 = (bf16[2,384,512]{2,1,0:T(8,128)(2,1)}, bf16[2,384,512]{2,1,0:T(8,128)(2,1)S(1)}, u32[]{:S(2)}, u32[]{:S(2)}) collective-permute-start(bf16[2,384,512]{2,1,0:T(8,128)(2,1)} %get-tuple-element.31), channel_id=1, source_target_pairs={{0,1},{1,0},{2,3},{3,2},{4,5},{5,4},{6,7},{7,6},{8,9},{9,8},{10,11... | collective-permute-start | bytes 2359304 | tf_op jit(solution)/shard_map/ppermute | solution.py:37
  161.7 84.9 %collective-permute-start.15 = (bf16[4,384,512]{2,1,0:T(8,128)(2,1)}, bf16[4,384,512]{2,1,0:T(8,128)(2,1)S(1)}, u32[]{:S(2)}, u32[]{:S(2)}) collective-permute-start(bf16[4,384,512]{2,1,0:T(8,128)(2,1)} %get-tuple-element.33), channel_id=1, source_target_pairs={{0,4},{1,5},{2,6},{3,7},{4,0},{5,1},{6,2},{7,3},{8,12},{9,13},{10,... | collective-permute-start | bytes 4718600 | tf_op jit(solution)/shard_map/ppermute | solution.py:37
  164.6 59.1 %collective-permute-start.19 = (bf16[2,384,512]{2,1,0:T(8,128)(2,1)}, bf16[2,384,512]{2,1,0:T(8,128)(2,1)}, u32[]{:S(2)}, u32[]{:S(2)}) collective-permute-start(bf16[2,384,512]{2,1,0:T(8,128)(2,1)} %get-tuple-element.35), channel_id=1, source_target_pairs={{0,2},{1,3},{2,0},{3,1},{4,6},{5,7},{6,4},{7,5},{8,10},{9,11},{10,... | collective-permute-start | bytes 2359304 | tf_op jit(solution)/shard_map/ppermute | solution.py:37
  168.6 59.2 %collective-permute-start.20 = (bf16[2,384,512]{2,1,0:T(8,128)(2,1)}, bf16[2,384,512]{2,1,0:T(8,128)(2,1)}, u32[]{:S(2)}, u32[]{:S(2)}) collective-permute-start(bf16[2,384,512]{2,1,0:T(8,128)(2,1)} %get-tuple-element.36), channel_id=1, source_target_pairs={{0,3},{1,2},{2,1},{3,0},{4,7},{5,6},{6,5},{7,4},{8,11},{9,10},{10,... | collective-permute-start | bytes 2359304 | tf_op jit(solution)/shard_map/ppermute | solution.py:37
  169.2 52.5 %collective-permute-start.22 = (bf16[1,2,2,32,512]{4,3,2,1,0:T(8,128)(2,1)S(1)}, bf16[1,2,2,32,512]{4,3,2,1,0:T(8,128)(2,1)S(1)}, u32[]{:S(2)}, u32[]{:S(2)}) collective-permute-start(bf16[1,2,2,32,512]{4,3,2,1,0:T(8,128)(2,1)S(1)} %bitcast.66), channel_id=1, source_target_pairs={{0,4},{1,5},{2,6},{3,7},{4,0},{5,1},{6,2},{7,3},{8,12},{9,13},{10,... | collective-permute-start | bytes 393224 | tf_op jit(solution)/shard_map/ppermute | solution.py:37
  170.0 67.0 %collective-permute-start.26 = (f32[8,32]{1,0:T(8,128)S(1)}, f32[8,32]{1,0:T(8,128)S(1)}, u32[]{:S(2)}, u32[]{:S(2)}) collective-permute-start(f32[8,32]{1,0:T(8,128)S(1)} %get-tuple-element.69), channel_id=1, source_target_pairs={{8,0},{16,8},{24,16},{32,24},{40,32},{48,40},{56,48},{64,56},{72,6... | collective-permute-start | bytes 3080 | tf_op jit(solution)/shard_map/ppermute | solution.py:45
  221.7 15.3 %collective-permute-start.25 = (f32[8,32]{1,0:T(8,128)S(1)}, f32[8,32]{1,0:T(8,128)S(1)}, u32[]{:S(2)}, u32[]{:S(2)}) collective-permute-start(f32[8,32]{1,0:T(8,128)S(1)} %get-tuple-element.70), channel_id=1, source_target_pairs={{0,8},{8,16},{16,24},{24,32},{32,40},{40,48},{48,56},{56,64},{64,7... | collective-permute-start | bytes 3080 | tf_op jit(solution)/shard_map/ppermute | solution.py:44
  229.2 17.4 %collective-permute-start.21 = (bf16[384,512]{1,0:T(8,128)(2,1)S(1)}, bf16[384,512]{1,0:T(8,128)(2,1)S(1)}, u32[]{:S(2)}, u32[]{:S(2)}) collective-permute-start(bf16[384,512]{1,0:T(8,128)(2,1)S(1)} %fusion.8), channel_id=1, source_target_pairs={{0,4},{1,5},{2,6},{3,7},{4,0},{5,1},{6,2},{7,3},{8,12},{9,13},{10,... | collective-permute-start | bytes 1179656 | tf_op jit(solution)/shard_map/ppermute | solution.py:37
  252.8 10.8 %collective-permute-start.32 = (bf16[32,4096]{1,0:T(8,128)(2,1)S(1)}, bf16[32,4096]{1,0:T(8,128)(2,1)S(1)}, u32[]{:S(2)}, u32[]{:S(2)}) collective-permute-start(bf16[32,4096]{1,0:T(8,128)(2,1)S(1)} %convert_element_type.200), channel_id=1, source_target_pairs={{0,8},{8,0},{16,24},{24,16},{32,40},{40,32},{48,56},{56,48},{64,72... | collective-permute-start | bytes 786440 | tf_op jit(solution)/shard_map/ppermute | solution.py:37
  255.9 15.6 %collective-permute-start.28 = (bf16[8,512]{1,0:T(8,128)(2,1)S(1)}, bf16[8,512]{1,0:T(8,128)(2,1)S(1)}, u32[]{:S(2)}, u32[]{:S(2)}) collective-permute-start(bf16[8,512]{1,0:T(8,128)(2,1)S(1)} %get-tuple-element.61), channel_id=1, source_target_pairs={{8,0},{16,8},{24,16},{32,24},{40,32},{48,40},{56,48},{64,56},{72,6... | collective-permute-start | bytes 24584 | tf_op jit(solution)/shard_map/ppermute | solution.py:45
  257.2 14.3 %collective-permute-start.27 = (bf16[8,512]{1,0:T(8,128)(2,1)S(1)}, bf16[8,512]{1,0:T(8,128)(2,1)S(1)}, u32[]{:S(2)}, u32[]{:S(2)}) collective-permute-start(bf16[8,512]{1,0:T(8,128)(2,1)S(1)} %get-tuple-element.62), channel_id=1, source_target_pairs={{0,8},{8,16},{16,24},{24,32},{32,40},{40,48},{48,56},{56,64},{64,7... | collective-permute-start | bytes 24584 | tf_op jit(solution)/shard_map/ppermute | solution.py:44
  264.1 9.8 %collective-permute-start.16 = (bf16[384,512]{1,0:T(8,128)(2,1)S(1)}, bf16[384,512]{1,0:T(8,128)(2,1)S(1)}, u32[]{:S(2)}, u32[]{:S(2)}) collective-permute-start(bf16[384,512]{1,0:T(8,128)(2,1)S(1)} %get-tuple-element.54), channel_id=1, source_target_pairs={{0,1},{1,0},{2,3},{3,2},{4,5},{5,4},{6,7},{7,6},{8,9},{9,8},{10,11... | collective-permute-start | bytes 1179656 | tf_op jit(solution)/shard_map/ppermute | solution.py:37
  268.5 10.2 %collective-permute-start.18 = (bf16[384,512]{1,0:T(8,128)(2,1)S(1)}, bf16[384,512]{1,0:T(8,128)(2,1)S(1)}, u32[]{:S(2)}, u32[]{:S(2)}) collective-permute-start(bf16[384,512]{1,0:T(8,128)(2,1)S(1)} %get-tuple-element.55), channel_id=1, source_target_pairs={{0,3},{1,2},{2,1},{3,0},{4,7},{5,6},{6,5},{7,4},{8,11},{9,10},{10,... | collective-permute-start | bytes 1179656 | tf_op jit(solution)/shard_map/ppermute | solution.py:37
  285.2 9.2 %collective-permute-start.38 = (bf16[32,4096]{1,0:T(8,128)(2,1)S(1)}, bf16[32,4096]{1,0:T(8,128)(2,1)S(1)}, u32[]{:S(2)}, u32[]{:S(2)}) collective-permute-start(bf16[32,4096]{1,0:T(8,128)(2,1)S(1)} %get-tuple-element.59), channel_id=1, source_target_pairs={{0,16},{8,24},{16,0},{24,8},{32,48},{40,56},{48,32},{56,40},{64,80... | collective-permute-start | bytes 786440 | tf_op jit(solution)/shard_map/ppermute | solution.py:37
  285.2 15.5 %collective-permute-start.17 = (bf16[384,512]{1,0:T(8,128)(2,1)S(1)}, bf16[384,512]{1,0:T(8,128)(2,1)S(1)}, u32[]{:S(2)}, u32[]{:S(2)}) collective-permute-start(bf16[384,512]{1,0:T(8,128)(2,1)S(1)} %get-tuple-element.56), channel_id=1, source_target_pairs={{0,2},{1,3},{2,0},{3,1},{4,6},{5,7},{6,4},{7,5},{8,10},{9,11},{10,... | collective-permute-start | bytes 1179656 | tf_op jit(solution)/shard_map/ppermute | solution.py:37
  290.1 8.7 %collective-permute-start.36 = (bf16[100,512]{1,0:T(8,128)(2,1)S(1)}, bf16[100,512]{1,0:T(8,128)(2,1)S(1)}, u32[]{:S(2)}, u32[]{:S(2)}) collective-permute-start(bf16[100,512]{1,0:T(8,128)(2,1)S(1)} %add_convert_fusion.7), channel_id=1, source_target_pairs={{0,16},{8,24},{16,0},{24,8},{32,48},{40,56},{48,32},{56,40},{64,80... | collective-permute-start | bytes 307208 | tf_op jit(solution)/shard_map/ppermute | solution.py:37
  294.5 14.3 %collective-permute-start.39 = (bf16[32,4096]{1,0:T(8,128)(2,1)S(1)}, bf16[32,4096]{1,0:T(8,128)(2,1)S(1)}, u32[]{:S(2)}, u32[]{:S(2)}) collective-permute-start(bf16[32,4096]{1,0:T(8,128)(2,1)S(1)} %add_convert_fusion.4), channel_id=1, source_target_pairs={{0,32},{8,40},{16,48},{24,56},{32,0},{40,8},{48,16},{56,24},{64,96... | collective-permute-start | bytes 786440 | tf_op jit(solution)/shard_map/ppermute | solution.py:37
  298.8 9.2 %collective-permute-start.37 = (bf16[100,512]{1,0:T(8,128)(2,1)S(1)}, bf16[100,512]{1,0:T(8,128)(2,1)S(1)}, u32[]{:S(2)}, u32[]{:S(2)}) collective-permute-start(bf16[100,512]{1,0:T(8,128)(2,1)S(1)} %add_convert_fusion.6), channel_id=1, source_target_pairs={{0,32},{8,40},{16,48},{24,56},{32,0},{40,8},{48,16},{56,24},{64,96... | collective-permute-start | bytes 307208 | tf_op jit(solution)/shard_map/ppermute | solution.py:37
  (37 other events, 482.3 us)
Sparse Core Ops, SparseCore 0:
  10.3 66.9 all-gather.2
  119.1 147.5 reduce-scatter.1

commit v4 on v3

--- a/solution.py
+++ b/solution.py
@@ -90,7 +90,7 @@
 
 def hidden_logits_kernel(order, *refs):
     pieces = refs[:10]
-    gen_ref, full_ref, edge_ref, flat_ref, tap_ref, sems = refs[10:]
+    gen_ref, out_ref, edge_ref, flat_ref, tap_ref, full_ref, sems = refs[10:]
     members, rows, width = full_ref.shape
     half = rows // 2
     targets = [full_ref.at[order[at]] for at in (0, 1, 3, 4, 5, 7)]
@@ -105,6 +105,12 @@
         copy.start()
     for copy in copies:
         copy.wait()
+    backs = [
+        pltpu.make_async_copy(full_ref.at[piece], out_ref.at[piece], sems.at[len(pieces) + piece])
+        for piece in range(members)
+    ]
+    for copy in backs:
+        copy.start()
     logits = jnp.zeros((gen_ref.shape[0], rows), F32)
     for piece in range(members):
         edge_ref[0, piece] = full_ref[piece, 0:PAD]
@@ -124,6 +130,8 @@
     flat = jnp.concatenate([first, second, blank], axis=0)
     flat_ref[...] = flat
     tap_ref[...] = flat.T
+    for copy in backs:
+        copy.wait()
 
 
 def hidden_logits(order, pieces, gen_rows):
@@ -138,12 +146,15 @@
             grid=(1,),
             in_specs=whole + [pl.BlockSpec((columns, depth), lambda i, o: (0, 0))],
             out_specs=[
-                pl.BlockSpec((members, rows, width), lambda i, o: (0, 0, 0)),
+                pl.BlockSpec(memory_space=pltpu.HBM),
                 pl.BlockSpec((2, members, PAD, width), lambda i, o: (0, 0, 0, 0)),
                 pl.BlockSpec((ROWS, rows), lambda i, o: (0, 0)),
                 pl.BlockSpec((rows, ROWS), lambda i, o: (0, 0)),
             ],
-            scratch_shapes=[pltpu.SemaphoreType.DMA((len(pieces),))],
+            scratch_shapes=[
+                pltpu.VMEM((members, rows, width), BF16),
+                pltpu.SemaphoreType.DMA((len(pieces) + members,)),
+            ],
         ),
         out_shape=(
             jax.ShapeDtypeStruct((members, rows, width), BF16),
@@ -273,15 +284,15 @@
     )(order, hidden_full, low, high, flat_full, flat_full, up_weight, middle_grad)
 
 
-def grad_middle_kernel(cot_ref, down_ref, out_ref):
+def grad_middle_kernel(cot_ref, *refs):
+    out_ref = refs[-1]
     width = cot_ref.shape[2]
     total = jnp.zeros(out_ref.shape, F32)
     for piece in range(cot_ref.shape[0]):
+        ref = refs[piece // 2]
+        lanes = slice(piece % 2 * width, (piece % 2 + 1) * width)
         total = total + lax.dot_general(
-            cot_ref[piece],
-            down_ref[:, piece * width : (piece + 1) * width],
-            NT,
-            preferred_element_type=F32,
+            cot_ref[piece], ref[:, lanes], NT, preferred_element_type=F32
         )
     out_ref[...] = total
 
@@ -290,24 +301,32 @@
     pieces, rows, width = cot_full.shape
     units = down_weight.shape[0]
     block = 256
+    parts = pieces // 2
     return pl.pallas_call(
         grad_middle_kernel,
         grid=(units // block,),
-        in_specs=[
-            pl.BlockSpec((pieces, rows, width), lambda i: (0, 0, 0)),
-            pl.BlockSpec((block, pieces * width), lambda i: (i, 0)),
-        ],
+        in_specs=[pl.BlockSpec((pieces, rows, width), lambda i: (0, 0, 0))]
+        + [pl.BlockSpec((block, 2 * width), lambda i, q=q: (i, q)) for q in range(parts)],
         out_specs=pl.BlockSpec((rows, block), lambda i: (0, i)),
         out_shape=jax.ShapeDtypeStruct((rows, units), F32),
         compiler_params=params(),
         name="grad_middle",
-    )(cot_full, down_weight)
-
-
-def spread_kernel(dims, order, value_ref, weight_ref, *out_refs):
-    result = lax.dot_general(
-        value_ref[...], weight_ref[...], dims, preferred_element_type=F32
-    ).astype(BF16)
+    )(cot_full, *[down_weight] * parts)
+
+
+def spread_kernel(transposed, order, value_ref, one_ref, two_ref, *out_refs):
+    value = value_ref[...]
+    if transposed:
+        parts = [
+            lax.dot_general(value, ref[...], NT, preferred_element_type=F32)
+            for ref in (one_ref, two_ref)
+        ]
+        result = jnp.concatenate(parts, axis=1).astype(BF16)
+    else:
+        half = one_ref.shape[0]
+        result = jnp.dot(value[:, :half], one_ref[...], preferred_element_type=F32)
+        result = result + jnp.dot(value[:, half:], two_ref[...], preferred_element_type=F32)
+        result = result.astype(BF16)
     for index, ref in enumerate(out_refs):
 
         @pl.when(lax.rem(pl.program_id(0), 4) == index)
@@ -315,75 +334,76 @@
             ref[0] = result
 
 
-def spread(order, value, weight, transposed, name):
+def spread(order, value, weight, transposed, name, tokens=()):
     rows, units = value.shape
     if transposed:
         width = weight.shape[0] // 8
-        spec = pl.BlockSpec((width, units), lambda k, o: (o[k], 0))
-        dims = NT
+        block = (width // 2, units)
+        specs = [
+            pl.BlockSpec(block, lambda k, o: (2 * o[k], 0)),
+            pl.BlockSpec(block, lambda k, o: (2 * o[k] + 1, 0)),
+        ]
     else:
         width = weight.shape[1] // 8
-        spec = pl.BlockSpec((units, width), lambda k, o: (0, o[k]))
-        dims = (((1,), (0,)), ((), ()))
-    return pl.pallas_call(
-        functools.partial(spread_kernel, dims),
-        grid_spec=pltpu.PrefetchScalarGridSpec(
-            num_scalar_prefetch=1,
-            grid=(8,),
-            in_specs=[pl.BlockSpec((rows, units), lambda k, o: (0, 0)), spec],
-            out_specs=[pl.BlockSpec((1, rows, width), lambda k, o: (k // 4, 0, 0))] * 4,
-        ),
-        out_shape=[jax.ShapeDtypeStruct((2, rows, width), BF16)] * 4,
-        compiler_params=params(),
-        name=name,
-    )(order, value, weight)
-
-
-def halves_kernel(order, value_ref, weight_ref, near_ref, far_ref):
-    result = jnp.dot(value_ref[...], weight_ref[...], preferred_element_type=F32).astype(BF16)
-
-    @pl.when(pl.program_id(0) < 4)
-    def _():
-        far_ref[0] = result
-
-    @pl.when(pl.program_id(0) >= 4)
-    def _():
-        near_ref[0] = result
-
-
-def halves(order, value, weight, tokens):
-    rows, units = value.shape
-    width = weight.shape[1] // 8
-    kernel, token_specs = ordered(halves_kernel, 3, tokens)
+        block = (units // 2, width)
+        specs = [
+            pl.BlockSpec(block, lambda k, o: (0, o[k])),
+            pl.BlockSpec(block, lambda k, o: (1, o[k])),
+        ]
+    kernel, token_specs = ordered(functools.partial(spread_kernel, transposed), 4, tokens)
     return pl.pallas_call(
         kernel,
         grid_spec=pltpu.PrefetchScalarGridSpec(
             num_scalar_prefetch=1,
             grid=(8,),
-            in_specs=[
-                pl.BlockSpec((rows, units), lambda k, o: (0, 0)),
-                pl.BlockSpec((units, width), lambda k, o: (0, o[(k + 4) % 8])),
-            ]
-            + token_specs,
-            out_specs=[
-                pl.BlockSpec((1, rows, width), lambda k, o: (jnp.maximum(k - 4, 0), 0, 0)),
-                pl.BlockSpec((1, rows, width), lambda k, o: (jnp.minimum(k, 3), 0, 0)),
-            ],
-        ),
-        out_shape=[jax.ShapeDtypeStruct((4, rows, width), BF16)] * 2,
+            in_specs=[pl.BlockSpec((rows, units), lambda k, o: (0, 0))] + specs + token_specs,
+            out_specs=[pl.BlockSpec((1, rows, width), lambda k, o: (k // 4, 0, 0))] * 4,
+        ),
+        out_shape=[jax.ShapeDtypeStruct((2, rows, width), BF16)] * 4,
         compiler_params=params(),
-        name="ffn_out",
-    )(order, value, weight, *tokens)
-
-
-def weight_grads_kernel(act_ref, cot_ref, pre_grad_ref, middle_ref, out_ref):
+        name=name,
+    )(order, value, weight, weight, *tokens)
+
+
+def weight_grads_kernel(act_ref, cot_ref, pre_grad_ref, middle_ref, out_ref, held, sems):
+    step = pl.program_id(0)
+    last = pl.num_programs(0) - 1
+    slot = lax.rem(step, 2)
+    per = held.shape[1]
+    chunk = held.shape[2] // 2
+
+    def copies(at, place):
+        return [
+            pltpu.make_async_copy(
+                held.at[place, index, part * chunk : (part + 1) * chunk],
+                out_ref.at[per * at + index, part * chunk : (part + 1) * chunk],
+                sems.at[place, 2 * index + part],
+            )
+            for index in range(per)
+            for part in range(2)
+        ]
+
     up = lax.dot_general(act_ref[0], pre_grad_ref[...], TN, preferred_element_type=F32)
     down = lax.dot_general(cot_ref[0], middle_ref[...], TN, preferred_element_type=F32)
-    chunk = out_ref.shape[1] // 2
-    for index in range(out_ref.shape[0]):
+
+    @pl.when(step >= 2)
+    def _():
+        for copy in copies(step - 2, slot):
+            copy.wait()
+
+    for index in range(per):
         rows = slice(index * chunk, (index + 1) * chunk)
-        out_ref[index, 0:chunk] = up[rows].astype(BF16)
-        out_ref[index, chunk:] = down[rows].astype(BF16)
+        held[slot, index, 0:chunk] = up[rows].astype(BF16)
+        held[slot, index, chunk:] = down[rows].astype(BF16)
+    for copy in copies(step, slot):
+        copy.start()
+
+    @pl.when(step == last)
+    def _():
+        for copy in copies(step - 1, 1 - slot):
+            copy.wait()
+        for copy in copies(step, slot):
+            copy.wait()
 
 
 def weight_grads(act_full, cot_full, pre_grad, middle):
@@ -401,8 +421,12 @@
             pl.BlockSpec((rows, units), lambda i: (0, 0)),
             pl.BlockSpec((rows, units), lambda i: (0, 0)),
         ],
-        out_specs=pl.BlockSpec((per, 2 * chunk, units), lambda i: (i, 0, 0)),
+        out_specs=pl.BlockSpec(memory_space=pltpu.HBM),
         out_shape=jax.ShapeDtypeStruct((chunks, 2 * chunk, units), BF16),
+        scratch_shapes=[
+            pltpu.VMEM((2, per, 2 * chunk, units), BF16),
+            pltpu.SemaphoreType.DMA((2, 2 * per)),
+        ],
         compiler_params=params(),
         name="weight_grads",
     )(act_full, cot_full, pre_grad, middle)
@@ -656,17 +680,18 @@
     )
 
     summed = weight_grads(act_full, cot_full, pre_grad, middle)
-    back_own = spread(order, pre_grad, up_weight, True, "act_back")
+    back_own = spread(order, pre_grad, up_weight, True, "act_back", (summed,))
     back_pairs = swap_pairs(back_own)
     summed = lax.psum_scatter(summed, "seq", scatter_dimension=0, tiled=False)
+
     columns = gen_weight.shape[1]
     gen_full = gen_blocks(order, gen_weight.T, width, back_own[0])
-    out_near, out_far = halves(order, middle, down_weight, (back_pairs[1],))
-    out_far = flip(out_far, "tp", 4)
-
-    gen_full = exchange(gen_full).reshape(members * ROWS, width)
+    gen_full = exchange(gen_full, (4,))
+    out_pairs = swap_pairs(spread(order, middle, down_weight, False, "ffn_out", (gen_full,)))
+    gen_full = exchange(gen_full, (2, 1)).reshape(members * ROWS, width)
     tap_low, tap_high = halo(taps)
 
+    out_last = flip(add_up([pair[1] for pair in out_pairs]).astype(BF16), "tp", 4)
     back_last = flip(add_up([pair[1] for pair in back_pairs]).astype(BF16), "tp", 4)
     low = lax.dynamic_index_in_dim(low_full, me, 0, keepdims=False)
     high = lax.dynamic_index_in_dim(high_full, me, 0, keepdims=False)
@@ -678,13 +703,11 @@
         low,
         high,
         taps,
-        (out_far, gen_full, tap_low, tap_high),
+        (gen_full, tap_low, tap_high),
     )
     grad_low, grad_high = halo(grad.astype(BF16))
     logit_full = gather_small(logit_grad).reshape(members * ROWS, rows)
     gen_sum = sum_over_seq(gen_grads(logit_grad, hidden_full), (1, 8))
-    out_sums = [add_up([out_near[z], out_far[z]]) for z in range(members // 2)]
-    out_one, out_two, out_three = [flip(out_sums[z].astype(BF16), "tp", z) for z in (1, 2, 3)]
     embed_grad, table_part = hidden_grads(
         (
             grad,
@@ -699,13 +722,13 @@
             sentinel_id[None, :],
         ),
         codes,
-        (gen_sum, out_one, out_three),
+        (gen_sum, out_last),
     )
     gen_sum = sum_over_seq(gen_sum, (2, 4))
     gen_grad = gen_sum[:columns].T
     table_grad = sum_over_seq(table_part)
 
-    total = add_up([out_sums[0], out_one, out_two, out_three])
+    total = add_up([pair[0] for pair in out_pairs] + [out_last])
     act = lax.dynamic_index_in_dim(act_full, me, 0, keepdims=False)
     layer_output = (act.astype(F32) + total).astype(BF16)
 

time: 322 us -> 284 us (0.88)
  waiting for transfers between devices: 147 us -> 108 us
    ppermute x34, waiting for transfers between devices: 146 us -> 105 us  [flip(): return lax.ppermute(value, axis, [(i, i ^ bit) for i in range(count)])]
  transfers between devices with their start and end apart: 42 -> 42, of which waited for: 24 -> 22; matrix products, arithmetic and copies ran while one was open for 5% -> 5% of each run, Pallas kernels for 14% -> 17%
where the time goes in v4:
time: 284 us; the launch traced here: 283 us
  waiting for transfers between devices  108 us (38%)
  Pallas kernels  78 us (27%)
  starting transfers between devices  60.7 us (21%)
  between operations  14.6 us (5%)
  other arithmetic  11.9 us (4%)
  local copies, waits for them, and re-layouts  8.45 us (3%)
    ppermute x34, waiting for transfers between devices, flip(): return lax.ppermute(value, axis, [(i, i ^ bit) for i in range(count)])  105 us
    ppermute x34, starting transfers between devices, flip(): return lax.ppermute(value, axis, [(i, i ^ bit) for i in range(count)])  50.8 us
    pallas_call x2, Pallas kernels, spread(): pl.pallas_call(kernel, grid_spec=pltpu.PrefetchScalarGridSpec(num_scalar_...  22.4 us
    pallas_call x1, Pallas kernels, weight_grads(): pl.pallas_call(weight_grads_kernel, grid=(pieces,), in_specs=[pl.BlockSpe...  15.7 us
    pallas_call x1, Pallas kernels, conv_up(): pl.pallas_call(conv_up_kernel, grid_spec=pltpu.PrefetchScalarGridSpec(num...  15.4 us
    pallas_call x1, Pallas kernels, grad_middle(): pl.pallas_call(grad_middle_kernel, grid=(units // block,), in_specs=[pl.B...  8.59 us
    pallas_call x1, Pallas kernels, hidden_logits(): pl.pallas_call(hidden_logits_kernel, grid_spec=pltpu.PrefetchScalarGridSp...  6.06 us
  transfers between devices with their start and end apart: 42, of which 22 were waited for; matrix products, arithmetic and copies ran while one was open for 5% of the time, Pallas kernels for 17%

profile of v4, /device:TPU:0, one launch (start us, length us, event | category | flops | bytes accessed | tf_op | source)
XLA Modules:
  0.0 282.7 jit_solution(16953034091076012701)
XLA Ops:
  10.0 3.2 %collective-permute-start.2 = (bf16[384,512]{1,0:T(8,128)(2,1)S(1)}, bf16[384,512]{1,0:T(8,128)(2,1)S(1)}, u32[]{:S(2)}, u32[]{:S(2)}) collective-permute-start(bf16[384,512]{1,0:T(8,128)(2,1)S(1)} %fusion.refs_0_.refs_6_), channel_id=1, source_target_pairs={{0,4},{1,5},{2,6},{3,7},{4,0},{5,1},{6,2},{7,3},{8,12},{9,13},{10,... | collective-permute-start | bytes 1179656 | tf_op jit(solution)/shard_map/ppermute | solution.py:37
  17.6 4.7 %collective-permute-done.2.refs_3_ = bf16[384,512]{1,0:T(8,128)(2,1)S(1)} collective-permute-done((bf16[384,512]{1,0:T(8,128)(2,1)S(1)}, bf16[384,512]{1,0:T(8,128)(2,1)S(1)}, u32[]{:S(2)}, u32[]{:S(2)}) %collective-permute-start.2) | collective-permute-done | bytes 393248 | tf_op jit(solution)/shard_map/ppermute | solution.py:37
  30.0 10.7 %collective-permute-done.3.refs_4_ = bf16[384,512]{1,0:T(8,128)(2,1)S(1)} collective-permute-done((bf16[384,512]{1,0:T(8,128)(2,1)S(1)}, bf16[384,512]{1,0:T(8,128)(2,1)S(1)}, u32[]{:S(2)}, u32[]{:S(2)}) %collective-permute-start.3) | collective-permute-done | bytes 393248 | tf_op jit(solution)/shard_map/ppermute | solution.py:37
  46.8 3.3 %collective-permute-done.7.refs_8_ = bf16[192,512]{1,0:T(8,128)(2,1)S(1)} collective-permute-done((bf16[192,512]{1,0:T(8,128)(2,1)}, bf16[192,512]{1,0:T(8,128)(2,1)S(1)}, u32[]{:S(2)}, u32[]{:S(2)}) %collective-permute-start.7) | collective-permute-done | bytes 196640 | tf_op jit(solution)/shard_map/ppermute | solution.py:37
  52.6 6.1 %hidden_logits.1 = (bf16[8,384,512]{2,1,0:T(8,128)(2,1)}, bf16[2,8,8,512]{3,2,1,0:T(8,128)(2,1)}, f32[32,384]{1,0:T(8,128)}, f32[384,32]{1,0:T(8,128)}) custom-call(s32[8]{0:T(128)} %iota_xor_fusion.order.refs_0_, bf16[384,512]{1,0:T(8,128)(2,1)} %copy-done.5, bf16[384,512]{1,0:T(8,128)(2,1)} %copy-done.11, bf16[384,512]{1,0:T(8,128)(2,1)} %copy-done.12, ...), custom_call_target="tpu_custom_call" | custom-call | tf_op jit(solution)/shard_map/hidden_logits/pallas_call | solution.py:142
  59.1 4.2 %collective-permute-done.11 = f32[1,32,384]{2,1,0:T(8,128)S(1)} collective-permute-done((f32[1,32,384]{2,1,0:T(8,128)}, f32[1,32,384]{2,1,0:T(8,128)S(1)}, u32[]{:S(2)}, u32[]{:S(2)}) %collective-permute-start.11) | collective-permute-done | bytes 49184 | tf_op jit(solution)/shard_map/ppermute | solution.py:37
  64.9 5.8 %collective-permute-done.12 = f32[2,32,384]{2,1,0:T(8,128)S(1)} collective-permute-done((f32[2,32,384]{2,1,0:T(8,128)S(1)}, f32[2,32,384]{2,1,0:T(8,128)S(1)}, u32[]{:S(2)}, u32[]{:S(2)}) %collective-permute-start.12) | collective-permute-done | bytes 98336 | tf_op jit(solution)/shard_map/ppermute | solution.py:37
  71.6 2.9 %collective-permute-start.13 = (f32[4,32,384]{2,1,0:T(8,128)S(1)}, f32[4,32,384]{2,1,0:T(8,128)S(1)}, u32[]{:S(2)}, u32[]{:S(2)}) collective-permute-start(f32[4,32,384]{2,1,0:T(8,128)S(1)} %pad_maximum_fusion.3), channel_id=1, source_target_pairs={{0,4},{1,5},{2,6},{3,7},{4,0},{5,1},{6,2},{7,3},{8,12},{9,13},{10,... | collective-permute-start | bytes 589832 | tf_op jit(solution)/shard_map/ppermute | solution.py:37
  76.6 3.0 %collective-permute-start.9 = (bf16[8,8,512]{2,1,0:T(8,128)(2,1)S(1)}, bf16[8,8,512]{2,1,0:T(8,128)(2,1)S(1)}, u32[]{:S(2)}, u32[]{:S(2)}) collective-permute-start(bf16[8,8,512]{2,1,0:T(8,128)(2,1)S(1)} %get-tuple-element.73), channel_id=1, source_target_pairs={{0,8},{8,16},{16,24},{24,32},{32,40},{40,48},{48,56},{56,64},{64,7... | collective-permute-start | bytes 196616 | tf_op jit(solution)/shard_map/ppermute | solution.py:674
  79.7 8.6 %grad_middle.1.grad_ref = f32[384,1024]{1,0:T(8,128)} custom-call(bf16[8,384,512]{2,1,0:T(8,128)(2,1)} %bitcast.52, bf16[1024,4096]{1,0:T(8,128)(2,1)} %refs_3_.5, bf16[1024,4096]{1,0:T(8,128)(2,1)} %refs_3_.5, bf16[1024,4096]{1,0:T(8,128)(2,1)} %refs_3_.5, bf16[1024,4096]{1,0:T(8,128)(2,1)} %refs_3_.5), custom_call_target="tpu_custom_call" | custom-call | tf_op jit(solution)/shard_map/grad_middle/pallas_call | solution.py:305
  89.7 15.4 %conv_up.1 = (bf16[8,384,512]{2,1,0:T(8,128)(2,1)}, bf16[384,1024]{1,0:T(8,128)(2,1)}, bf16[384,1024]{1,0:T(8,128)(2,1)}) custom-call(s32[8]{0:T(128)} %iota_xor_fusion.order.refs_0_, bf16[8,384,512]{2,1,0:T(8,128)(2,1)} %get-tuple-element.26.hidden_ref, bf16[8,8,512]{2,1,0:T(8,128)(2,1)} %copy-done.23, bf16[8,8,512]{2,1,0:T(8,128)(2,1)} %copy-done.22, ...), custom_call_target="tpu_custom_call" | custom-call | tf_op jit(solution)/shard_map/conv_up/pallas_call | solution.py:253
  105.2 15.7 %weight_grads.1.refs_4_ = bf16[16,512,1024]{2,1,0:T(8,128)(2,1)} custom-call(bf16[8,384,512]{2,1,0:T(8,128)(2,1)} %get-tuple-element.30.act_ref, bf16[8,384,512]{2,1,0:T(8,128)(2,1)} %bitcast.53, bf16[384,1024]{1,0:T(8,128)(2,1)} %get-tuple-element.32.pre_grad_ref.refs_1_, bf16[384,1024]{1,0:T(8,128)(2,1)} %get-tuple-element.31.middle_ref.refs_1_), custom_call_target="tpu_custom_call" | custom-call | tf_op jit(solution)/shard_map/weight_grads/pallas_call | solution.py:415
  120.9 11.4 %act_back.1 = (bf16[2,384,512]{2,1,0:T(8,128)(2,1)}, bf16[2,384,512]{2,1,0:T(8,128)(2,1)}, bf16[2,384,512]{2,1,0:T(8,128)(2,1)}, bf16[2,384,512]{2,1,0:T(8,128)(2,1)}) custom-call(s32[8]{0:T(128)} %iota_xor_fusion.order.refs_0_, bf16[384,1024]{1,0:T(8,128)(2,1)} %get-tuple-element.32.pre_grad_ref.refs_1_, bf16[4096,1024]{1,0:T(8,128)(2,1)} %refs_3_.4, ...), custom_call_target="tpu_custom_call" | custom-call | tf_op jit(solution)/shard_map/act_back/pallas_call | solution.py:354
  132.8 4.2 %collective-permute-start.21 = (bf16[2,384,512]{2,1,0:T(8,128)(2,1)}, bf16[2,384,512]{2,1,0:T(8,128)(2,1)S(1)}, u32[]{:S(2)}, u32[]{:S(2)}) collective-permute-start(bf16[2,384,512]{2,1,0:T(8,128)(2,1)} %get-tuple-element.40), channel_id=1, source_target_pairs={{0,3},{1,2},{2,1},{3,0},{4,7},{5,6},{6,5},{7,4},{8,11},{9,10},{10,... | collective-permute-start | bytes 2359304 | tf_op jit(solution)/shard_map/ppermute | solution.py:37
  141.5 6.4 %collective-permute-done.14 = bf16[1,2,2,32,512]{4,3,2,1,0:T(8,128)(2,1)S(1)} collective-permute-done((bf16[1,2,2,32,512]{4,3,2,1,0:T(8,128)(2,1)S(1)}, bf16[1,2,2,32,512]{4,3,2,1,0:T(8,128)(2,1)S(1)}, u32[]{:S(2)}, u32[]{:S(2)}) %collective-permute-start.14) | collective-permute-done | bytes 131104 | tf_op jit(solution)/shard_map/ppermute | solution.py:37
  149.2 11.1 %ffn_out.1 = (bf16[2,384,512]{2,1,0:T(8,128)(2,1)}, bf16[2,384,512]{2,1,0:T(8,128)(2,1)}, bf16[2,384,512]{2,1,0:T(8,128)(2,1)}, bf16[2,384,512]{2,1,0:T(8,128)(2,1)}) custom-call(s32[8]{0:T(128)} %iota_xor_fusion.order.refs_0_, bf16[384,1024]{1,0:T(8,128)(2,1)} %get-tuple-element.31.middle_ref.refs_1_, bf16[1024,4096]{1,0:T(8,128)(2,1)} %refs_3_.5, ...), custom_call_target="tpu_custom_call" | custom-call | tf_op jit(solution)/shard_map/ffn_out/pallas_call | solution.py:354
  161.4 6.8 %collective-permute-done.20.refs_2_ = bf16[2,384,512]{2,1,0:T(8,128)(2,1)S(1)} collective-permute-done((bf16[2,384,512]{2,1,0:T(8,128)(2,1)}, bf16[2,384,512]{2,1,0:T(8,128)(2,1)S(1)}, u32[]{:S(2)}, u32[]{:S(2)}) %collective-permute-start.20) | collective-permute-done | bytes 786464 | tf_op jit(solution)/shard_map/ppermute | solution.py:37
  168.2 2.8 %collective-permute-start.16 = (bf16[2,384,512]{2,1,0:T(8,128)(2,1)}, bf16[2,384,512]{2,1,0:T(8,128)(2,1)S(1)}, u32[]{:S(2)}, u32[]{:S(2)}) collective-permute-start(bf16[2,384,512]{2,1,0:T(8,128)(2,1)} %get-tuple-element.36), channel_id=1, source_target_pairs={{0,2},{1,3},{2,0},{3,1},{4,6},{5,7},{6,4},{7,5},{8,10},{9,11},{10,... | collective-permute-start | bytes 2359304 | tf_op jit(solution)/shard_map/ppermute | solution.py:37
  171.0 4.1 %collective-permute-done.21.refs_3_ = bf16[2,384,512]{2,1,0:T(8,128)(2,1)S(1)} collective-permute-done((bf16[2,384,512]{2,1,0:T(8,128)(2,1)}, bf16[2,384,512]{2,1,0:T(8,128)(2,1)S(1)}, u32[]{:S(2)}, u32[]{:S(2)}) %collective-permute-start.21) | collective-permute-done | bytes 786464 | tf_op jit(solution)/shard_map/ppermute | solution.py:37
  175.1 3.0 %collective-permute-start.17 = (bf16[2,384,512]{2,1,0:T(8,128)(2,1)}, bf16[2,384,512]{2,1,0:T(8,128)(2,1)S(1)}, u32[]{:S(2)}, u32[]{:S(2)}) collective-permute-start(bf16[2,384,512]{2,1,0:T(8,128)(2,1)} %get-tuple-element.37), channel_id=1, source_target_pairs={{0,3},{1,2},{2,1},{3,0},{4,7},{5,6},{6,5},{7,4},{8,11},{9,10},{10,... | collective-permute-start | bytes 2359304 | tf_op jit(solution)/shard_map/ppermute | solution.py:37
  180.7 28.3 %collective-permute-done.24 = bf16[2,2,1,32,512]{4,3,2,1,0:T(8,128)(2,1)S(1)} collective-permute-done((bf16[2,2,1,32,512]{4,3,2,1,0:T(8,128)(2,1)S(1)}, bf16[2,2,1,32,512]{4,3,2,1,0:T(8,128)(2,1)S(1)}, u32[]{:S(2)}, u32[]{:S(2)}) %collective-permute-start.24) | collective-permute-done | bytes 131104 | tf_op jit(solution)/shard_map/ppermute | solution.py:37
  212.1 3.8 %kernel_grads.1 = (f32[384,512]{1,0:T(8,128)S(1)}, bf16[32,384]{1,0:T(8,128)(2,1)S(1)}) custom-call(bf16[2,384,512]{2,1,0:T(8,128)(2,1)S(1)} %copy-done.4, bf16[2,384,512]{2,1,0:T(8,128)(2,1)S(1)} %collective-permute-done.19.refs_1_, bf16[2,384,512]{2,1,0:T(8,128)(2,1)S(1)} %collective-permute-done.20.refs_2_, ...), custom_call_target="tpu_custom_call" | custom-call | tf_op jit(solution)/shard_map/kernel_grads/pallas_call | solution.py:482
  216.8 2.8 collective-permute-start.32
  220.2 3.0 %collective-permute-start.18 = (bf16[384,512]{1,0:T(8,128)(2,1)S(1)}, bf16[384,512]{1,0:T(8,128)(2,1)S(1)}, u32[]{:S(2)}, u32[]{:S(2)}) collective-permute-start(bf16[384,512]{1,0:T(8,128)(2,1)S(1)} %fusion.3), channel_id=1, source_target_pairs={{0,4},{1,5},{2,6},{3,7},{4,0},{5,1},{6,2},{7,3},{8,12},{9,13},{10,... | collective-permute-start | bytes 1179656 | tf_op jit(solution)/shard_map/ppermute | solution.py:37
  226.7 3.9 %collective-permute-start.33 = (bf16[32,4096]{1,0:T(8,128)(2,1)S(1)}, bf16[32,4096]{1,0:T(8,128)(2,1)S(1)}, u32[]{:S(2)}, u32[]{:S(2)}) collective-permute-start(bf16[32,4096]{1,0:T(8,128)(2,1)S(1)} %add_convert_fusion.3), channel_id=1, source_target_pairs={{0,64},{8,72},{16,80},{24,88},{32,96},{40,104},{48,112},{56,120},{... | collective-permute-start | bytes 786440 | tf_op jit(solution)/shard_map/ppermute | solution.py:37
  233.1 4.8 %collective-permute-done.31 = bf16[4,32,384]{2,1,0:T(8,128)(2,1)S(1)} collective-permute-done((bf16[4,32,384]{2,1,0:T(8,128)(2,1)S(1)}, bf16[4,32,384]{2,1,0:T(8,128)(2,1)S(1)}, u32[]{:S(2)}, u32[]{:S(2)}) %collective-permute-start.31) | collective-permute-done | bytes 98336 | tf_op jit(solution)/shard_map/ppermute | solution.py:37
  237.9 3.7 %collective-permute-done.33 = bf16[32,4096]{1,0:T(8,128)(2,1)S(1)} collective-permute-done((bf16[32,4096]{1,0:T(8,128)(2,1)S(1)}, bf16[32,4096]{1,0:T(8,128)(2,1)S(1)}, u32[]{:S(2)}, u32[]{:S(2)}) %collective-permute-start.33) | collective-permute-done | bytes 262176 | tf_op jit(solution)/shard_map/ppermute | solution.py:37
  241.8 4.8 %hidden_grads.1 = (f32[384,512]{1,0:T(8,128)}, f32[100,512]{1,0:T(8,128)S(1)}) custom-call(f32[384,512]{1,0:T(8,128)S(1)} %get-tuple-element.42.refs_0_, bf16[8,512]{1,0:T(8,128)(2,1)S(1)} %collective-permute-done.27.refs_1_, bf16[8,512]{1,0:T(8,128)(2,1)S(1)} %collective-permute-done.28.refs_2_, f32[384,32]{1,0:T(8,128)S(1)} %copy-done.9, ...), custom_call_target="tpu_custom_call" | custom-call | tf_op jit(solution)/shard_map/hidden_grads/pallas_call | solution.py:567
  248.0 3.5 %collective-permute-start.35 = (bf16[100,512]{1,0:T(8,128)(2,1)S(1)}, bf16[100,512]{1,0:T(8,128)(2,1)S(1)}, u32[]{:S(2)}, u32[]{:S(2)}) collective-permute-start(bf16[100,512]{1,0:T(8,128)(2,1)S(1)} %add_convert_fusion.6), channel_id=1, source_target_pairs={{0,64},{8,72},{16,80},{24,88},{32,96},{40,104},{48,112},{56,120},{... | collective-permute-start | bytes 307208 | tf_op jit(solution)/shard_map/ppermute | solution.py:37
  251.4 3.3 %collective-permute-done.35 = bf16[100,512]{1,0:T(8,128)(2,1)S(1)} collective-permute-done((bf16[100,512]{1,0:T(8,128)(2,1)S(1)}, bf16[100,512]{1,0:T(8,128)(2,1)S(1)}, u32[]{:S(2)}, u32[]{:S(2)}) %collective-permute-start.35) | collective-permute-done | bytes 102432 | tf_op jit(solution)/shard_map/ppermute | solution.py:37
  254.9 5.8 %collective-permute-done.38 = bf16[32,4096]{1,0:T(8,128)(2,1)S(1)} collective-permute-done((bf16[32,4096]{1,0:T(8,128)(2,1)S(1)}, bf16[32,4096]{1,0:T(8,128)(2,1)S(1)}, u32[]{:S(2)}, u32[]{:S(2)}) %collective-permute-start.38) | collective-permute-done | bytes 262176 | tf_op jit(solution)/shard_map/ppermute | solution.py:37
  266.5 4.2 %collective-permute-done.37 = bf16[100,512]{1,0:T(8,128)(2,1)S(1)} collective-permute-done((bf16[100,512]{1,0:T(8,128)(2,1)S(1)}, bf16[100,512]{1,0:T(8,128)(2,1)S(1)}, u32[]{:S(2)}, u32[]{:S(2)}) %collective-permute-start.37) | collective-permute-done | bytes 102432 | tf_op jit(solution)/shard_map/ppermute | solution.py:37
  (157 shorter events, 63.2 us)
Async XLA Ops:
  7.2 72.5 %all-gather.3.cloned.1.call-start = ((), (), s32[]{:S(2)}) async-start(), calls=%async_computation.2 | async-start | bytes 3538944 | tf_op jit(solution)/shard_map/all_gather | solution.py:669
  7.9 264.3 %reduce-scatter.2.cloned.1.call-start = ((), (), s32[]{:S(2)}) async-start(), calls=%async_computation.1 | async-start | bytes 17825792 | tf_op jit(solution)/shard_map/reduce_scatter | solution.py:685
  10.0 12.3 %collective-permute-start.2 = (bf16[384,512]{1,0:T(8,128)(2,1)S(1)}, bf16[384,512]{1,0:T(8,128)(2,1)S(1)}, u32[]{:S(2)}, u32[]{:S(2)}) collective-permute-start(bf16[384,512]{1,0:T(8,128)(2,1)S(1)} %fusion.refs_0_.refs_6_), channel_id=1, source_target_pairs={{0,4},{1,5},{2,6},{3,7},{4,0},{5,1},{6,2},{7,3},{8,12},{9,13},{10,... | collective-permute-start | bytes 1179656 | tf_op jit(solution)/shard_map/ppermute | solution.py:37
  13.2 13.8 %collective-permute-start = (bf16[384,512]{1,0:T(8,128)(2,1)S(1)}, bf16[384,512]{1,0:T(8,128)(2,1)S(1)}, u32[]{:S(2)}, u32[]{:S(2)}) collective-permute-start(bf16[384,512]{1,0:T(8,128)(2,1)S(1)} %fusion.refs_0_.refs_6_), channel_id=1, source_target_pairs={{0,1},{1,0},{2,3},{3,2},{4,5},{5,4},{6,7},{7,6},{8,9},{9,8},{10,11... | collective-permute-start | bytes 1179656 | tf_op jit(solution)/shard_map/ppermute | solution.py:37
  15.1 13.5 %collective-permute-start.1 = (bf16[384,512]{1,0:T(8,128)(2,1)S(1)}, bf16[384,512]{1,0:T(8,128)(2,1)S(1)}, u32[]{:S(2)}, u32[]{:S(2)}) collective-permute-start(bf16[384,512]{1,0:T(8,128)(2,1)S(1)} %fusion.refs_0_.refs_6_), channel_id=1, source_target_pairs={{0,3},{1,2},{2,1},{3,0},{4,7},{5,6},{6,5},{7,4},{8,11},{9,10},{10,... | collective-permute-start | bytes 1179656 | tf_op jit(solution)/shard_map/ppermute | solution.py:37
  22.3 18.4 %collective-permute-start.3 = (bf16[384,512]{1,0:T(8,128)(2,1)S(1)}, bf16[384,512]{1,0:T(8,128)(2,1)S(1)}, u32[]{:S(2)}, u32[]{:S(2)}) collective-permute-start(bf16[384,512]{1,0:T(8,128)(2,1)S(1)} %collective-permute-done.2.refs_3_), channel_id=1, source_target_pairs={{0,1},{1,0},{2,3},{3,2},{4,5},{5,4},{6,7},{7,6},{8,9},{9,8},{10,11... | collective-permute-start | bytes 1179656 | tf_op jit(solution)/shard_map/ppermute | solution.py:37
  24.4 19.7 %collective-permute-start.4 = (bf16[384,512]{1,0:T(8,128)(2,1)S(1)}, bf16[384,512]{1,0:T(8,128)(2,1)S(1)}, u32[]{:S(2)}, u32[]{:S(2)}) collective-permute-start(bf16[384,512]{1,0:T(8,128)(2,1)S(1)} %collective-permute-done.2.refs_3_), channel_id=1, source_target_pairs={{0,3},{1,2},{2,1},{3,0},{4,7},{5,6},{6,5},{7,4},{8,11},{9,10},{10,... | collective-permute-start | bytes 1179656 | tf_op jit(solution)/shard_map/ppermute | solution.py:37
  27.0 19.8 %collective-permute-start.5 = (bf16[192,512]{1,0:T(8,128)(2,1)S(1)}, bf16[192,512]{1,0:T(8,128)(2,1)S(1)}, u32[]{:S(2)}, u32[]{:S(2)}) collective-permute-start(bf16[192,512]{1,0:T(8,128)(2,1)S(1)} %slice.134), channel_id=1, source_target_pairs={{0,3},{1,2},{2,1},{3,0},{4,7},{5,6},{6,5},{7,4},{8,11},{9,10},{10,... | collective-permute-start | bytes 589832 | tf_op jit(solution)/shard_map/ppermute | solution.py:37
  29.3 17.5 %collective-permute-start.6 = (bf16[192,512]{1,0:T(8,128)(2,1)}, bf16[192,512]{1,0:T(8,128)(2,1)S(1)}, u32[]{:S(2)}, u32[]{:S(2)}) collective-permute-start(bf16[192,512]{1,0:T(8,128)(2,1)} %slice.135), channel_id=1, source_target_pairs={{0,1},{1,0},{2,3},{3,2},{4,5},{5,4},{6,7},{7,6},{8,9},{9,8},{10,11... | collective-permute-start | bytes 589832 | tf_op jit(solution)/shard_map/ppermute | solution.py:37
  41.4 8.7 %collective-permute-start.7 = (bf16[192,512]{1,0:T(8,128)(2,1)}, bf16[192,512]{1,0:T(8,128)(2,1)S(1)}, u32[]{:S(2)}, u32[]{:S(2)}) collective-permute-start(bf16[192,512]{1,0:T(8,128)(2,1)} %slice.136), channel_id=1, source_target_pairs={{0,3},{1,2},{2,1},{3,0},{4,7},{5,6},{6,5},{7,4},{8,11},{9,10},{10,... | collective-permute-start | bytes 589832 | tf_op jit(solution)/shard_map/ppermute | solution.py:37
  71.6 16.7 %collective-permute-start.13 = (f32[4,32,384]{2,1,0:T(8,128)S(1)}, f32[4,32,384]{2,1,0:T(8,128)S(1)}, u32[]{:S(2)}, u32[]{:S(2)}) collective-permute-start(f32[4,32,384]{2,1,0:T(8,128)S(1)} %pad_maximum_fusion.3), channel_id=1, source_target_pairs={{0,4},{1,5},{2,6},{3,7},{4,0},{5,1},{6,2},{7,3},{8,12},{9,13},{10,... | collective-permute-start | bytes 589832 | tf_op jit(solution)/shard_map/ppermute | solution.py:37
  75.3 13.8 %collective-permute-start.10 = (bf16[8,8,512]{2,1,0:T(8,128)(2,1)S(1)}, bf16[8,8,512]{2,1,0:T(8,128)(2,1)S(1)}, u32[]{:S(2)}, u32[]{:S(2)}) collective-permute-start(bf16[8,8,512]{2,1,0:T(8,128)(2,1)S(1)} %get-tuple-element.72), channel_id=1, source_target_pairs={{8,0},{16,8},{24,16},{32,24},{40,32},{48,40},{56,48},{64,56},{72,6... | collective-permute-start | bytes 196616 | tf_op jit(solution)/shard_map/ppermute | solution.py:675
  76.6 12.5 %collective-permute-start.9 = (bf16[8,8,512]{2,1,0:T(8,128)(2,1)S(1)}, bf16[8,8,512]{2,1,0:T(8,128)(2,1)S(1)}, u32[]{:S(2)}, u32[]{:S(2)}) collective-permute-start(bf16[8,8,512]{2,1,0:T(8,128)(2,1)S(1)} %get-tuple-element.73), channel_id=1, source_target_pairs={{0,8},{8,16},{16,24},{24,32},{32,40},{40,48},{48,56},{56,64},{64,7... | collective-permute-start | bytes 196616 | tf_op jit(solution)/shard_map/ppermute | solution.py:674
  132.3 28.0 %collective-permute-start.19 = (bf16[2,384,512]{2,1,0:T(8,128)(2,1)}, bf16[2,384,512]{2,1,0:T(8,128)(2,1)S(1)}, u32[]{:S(2)}, u32[]{:S(2)}) collective-permute-start(bf16[2,384,512]{2,1,0:T(8,128)(2,1)} %get-tuple-element.38), channel_id=1, source_target_pairs={{0,1},{1,0},{2,3},{3,2},{4,5},{5,4},{6,7},{7,6},{8,9},{9,8},{10,11... | collective-permute-start | bytes 2359304 | tf_op jit(solution)/shard_map/ppermute | solution.py:37
  132.3 35.9 %collective-permute-start.20 = (bf16[2,384,512]{2,1,0:T(8,128)(2,1)}, bf16[2,384,512]{2,1,0:T(8,128)(2,1)S(1)}, u32[]{:S(2)}, u32[]{:S(2)}) collective-permute-start(bf16[2,384,512]{2,1,0:T(8,128)(2,1)} %get-tuple-element.39), channel_id=1, source_target_pairs={{0,2},{1,3},{2,0},{3,1},{4,6},{5,7},{6,4},{7,5},{8,10},{9,11},{10,... | collective-permute-start | bytes 2359304 | tf_op jit(solution)/shard_map/ppermute | solution.py:37
  132.8 42.4 %collective-permute-start.21 = (bf16[2,384,512]{2,1,0:T(8,128)(2,1)}, bf16[2,384,512]{2,1,0:T(8,128)(2,1)S(1)}, u32[]{:S(2)}, u32[]{:S(2)}) collective-permute-start(bf16[2,384,512]{2,1,0:T(8,128)(2,1)} %get-tuple-element.40), channel_id=1, source_target_pairs={{0,3},{1,2},{2,1},{3,0},{4,7},{5,6},{6,5},{7,4},{8,11},{9,10},{10,... | collective-permute-start | bytes 2359304 | tf_op jit(solution)/shard_map/ppermute | solution.py:37
  138.8 9.1 %collective-permute-start.14 = (bf16[1,2,2,32,512]{4,3,2,1,0:T(8,128)(2,1)S(1)}, bf16[1,2,2,32,512]{4,3,2,1,0:T(8,128)(2,1)S(1)}, u32[]{:S(2)}, u32[]{:S(2)}) collective-permute-start(bf16[1,2,2,32,512]{4,3,2,1,0:T(8,128)(2,1)S(1)} %bitcast.61), channel_id=1, source_target_pairs={{0,4},{1,5},{2,6},{3,7},{4,0},{5,1},{6,2},{7,3},{8,12},{9,13},{10,... | collective-permute-start | bytes 393224 | tf_op jit(solution)/shard_map/ppermute | solution.py:37
  139.7 39.4 %collective-permute-start.25 = (f32[8,32]{1,0:T(8,128)S(1)}, f32[8,32]{1,0:T(8,128)S(1)}, u32[]{:S(2)}, u32[]{:S(2)}) collective-permute-start(f32[8,32]{1,0:T(8,128)S(1)} %get-tuple-element.71), channel_id=1, source_target_pairs={{0,8},{8,16},{16,24},{24,32},{32,40},{40,48},{48,56},{56,64},{64,7... | collective-permute-start | bytes 3080 | tf_op jit(solution)/shard_map/ppermute | solution.py:44
  148.5 29.8 %collective-permute-start.23 = (bf16[2,1,2,32,512]{4,3,2,1,0:T(8,128)(2,1)}, bf16[2,1,2,32,512]{4,3,2,1,0:T(8,128)(2,1)S(1)}, u32[]{:S(2)}, u32[]{:S(2)}) collective-permute-start(bf16[2,1,2,32,512]{4,3,2,1,0:T(8,128)(2,1)} %get-tuple-element.67), channel_id=1, source_target_pairs={{0,2},{1,3},{2,0},{3,1},{4,6},{5,7},{6,4},{7,5},{8,10},{9,11},{10,... | collective-permute-start | bytes 393224 | tf_op jit(solution)/shard_map/ppermute | solution.py:37
  160.3 59.6 %collective-permute-start.15 = (bf16[2,384,512]{2,1,0:T(8,128)(2,1)}, bf16[2,384,512]{2,1,0:T(8,128)(2,1)S(1)}, u32[]{:S(2)}, u32[]{:S(2)}) collective-permute-start(bf16[2,384,512]{2,1,0:T(8,128)(2,1)} %get-tuple-element.35), channel_id=1, source_target_pairs={{0,1},{1,0},{2,3},{3,2},{4,5},{5,4},{6,7},{7,6},{8,9},{9,8},{10,11... | collective-permute-start | bytes 2359304 | tf_op jit(solution)/shard_map/ppermute | solution.py:37
  168.2 51.8 %collective-permute-start.16 = (bf16[2,384,512]{2,1,0:T(8,128)(2,1)}, bf16[2,384,512]{2,1,0:T(8,128)(2,1)S(1)}, u32[]{:S(2)}, u32[]{:S(2)}) collective-permute-start(bf16[2,384,512]{2,1,0:T(8,128)(2,1)} %get-tuple-element.36), channel_id=1, source_target_pairs={{0,2},{1,3},{2,0},{3,1},{4,6},{5,7},{6,4},{7,5},{8,10},{9,11},{10,... | collective-permute-start | bytes 2359304 | tf_op jit(solution)/shard_map/ppermute | solution.py:37
  175.1 44.8 %collective-permute-start.17 = (bf16[2,384,512]{2,1,0:T(8,128)(2,1)}, bf16[2,384,512]{2,1,0:T(8,128)(2,1)S(1)}, u32[]{:S(2)}, u32[]{:S(2)}) collective-permute-start(bf16[2,384,512]{2,1,0:T(8,128)(2,1)} %get-tuple-element.37), channel_id=1, source_target_pairs={{0,3},{1,2},{2,1},{3,0},{4,7},{5,6},{6,5},{7,4},{8,11},{9,10},{10,... | collective-permute-start | bytes 2359304 | tf_op jit(solution)/shard_map/ppermute | solution.py:37
  178.3 33.7 %collective-permute-start.22 = (bf16[384,512]{1,0:T(8,128)(2,1)S(1)}, bf16[384,512]{1,0:T(8,128)(2,1)S(1)}, u32[]{:S(2)}, u32[]{:S(2)}) collective-permute-start(bf16[384,512]{1,0:T(8,128)(2,1)S(1)} %fusion.4), channel_id=1, source_target_pairs={{0,4},{1,5},{2,6},{3,7},{4,0},{5,1},{6,2},{7,3},{8,12},{9,13},{10,... | collective-permute-start | bytes 1179656 | tf_op jit(solution)/shard_map/ppermute | solution.py:37
  179.2 29.9 %collective-permute-start.24 = (bf16[2,2,1,32,512]{4,3,2,1,0:T(8,128)(2,1)S(1)}, bf16[2,2,1,32,512]{4,3,2,1,0:T(8,128)(2,1)S(1)}, u32[]{:S(2)}, u32[]{:S(2)}) collective-permute-start(bf16[2,2,1,32,512]{4,3,2,1,0:T(8,128)(2,1)S(1)} %get-tuple-element.65), channel_id=1, source_target_pairs={{0,1},{1,0},{2,3},{3,2},{4,5},{5,4},{6,7},{7,6},{8,9},{9,8},{10,11... | collective-permute-start | bytes 393224 | tf_op jit(solution)/shard_map/ppermute | solution.py:37
  216.8 9.8 %collective-permute-start.32 = (bf16[32,4096]{1,0:T(8,128)(2,1)S(1)}, bf16[32,4096]{1,0:T(8,128)(2,1)S(1)}, u32[]{:S(2)}, u32[]{:S(2)}) collective-permute-start(bf16[32,4096]{1,0:T(8,128)(2,1)S(1)} %convert_element_type.169), channel_id=1, source_target_pairs={{0,8},{8,0},{16,24},{24,16},{32,40},{40,32},{48,56},{56,48},{64,72... | collective-permute-start | bytes 786440 | tf_op jit(solution)/shard_map/ppermute | solution.py:37
  220.2 21.6 %collective-permute-start.18 = (bf16[384,512]{1,0:T(8,128)(2,1)S(1)}, bf16[384,512]{1,0:T(8,128)(2,1)S(1)}, u32[]{:S(2)}, u32[]{:S(2)}) collective-permute-start(bf16[384,512]{1,0:T(8,128)(2,1)S(1)} %fusion.3), channel_id=1, source_target_pairs={{0,4},{1,5},{2,6},{3,7},{4,0},{5,1},{6,2},{7,3},{8,12},{9,13},{10,... | collective-permute-start | bytes 1179656 | tf_op jit(solution)/shard_map/ppermute | solution.py:37
  225.5 12.4 %collective-permute-start.31 = (bf16[4,32,384]{2,1,0:T(8,128)(2,1)S(1)}, bf16[4,32,384]{2,1,0:T(8,128)(2,1)S(1)}, u32[]{:S(2)}, u32[]{:S(2)}) collective-permute-start(bf16[4,32,384]{2,1,0:T(8,128)(2,1)S(1)} %pad_maximum_fusion.7), channel_id=1, source_target_pairs={{0,4},{1,5},{2,6},{3,7},{4,0},{5,1},{6,2},{7,3},{8,12},{9,13},{10,... | collective-permute-start | bytes 294920 | tf_op jit(solution)/shard_map/ppermute | solution.py:37
  226.7 15.0 %collective-permute-start.33 = (bf16[32,4096]{1,0:T(8,128)(2,1)S(1)}, bf16[32,4096]{1,0:T(8,128)(2,1)S(1)}, u32[]{:S(2)}, u32[]{:S(2)}) collective-permute-start(bf16[32,4096]{1,0:T(8,128)(2,1)S(1)} %add_convert_fusion.3), channel_id=1, source_target_pairs={{0,64},{8,72},{16,80},{24,88},{32,96},{40,104},{48,112},{56,120},{... | collective-permute-start | bytes 786440 | tf_op jit(solution)/shard_map/ppermute | solution.py:37
  230.6 11.2 %collective-permute-start.27 = (bf16[8,512]{1,0:T(8,128)(2,1)S(1)}, bf16[8,512]{1,0:T(8,128)(2,1)S(1)}, u32[]{:S(2)}, u32[]{:S(2)}) collective-permute-start(bf16[8,512]{1,0:T(8,128)(2,1)S(1)} %get-tuple-element.63), channel_id=1, source_target_pairs={{0,8},{8,16},{16,24},{24,32},{32,40},{40,48},{48,56},{56,64},{64,7... | collective-permute-start | bytes 24584 | tf_op jit(solution)/shard_map/ppermute | solution.py:44
  231.8 9.9 %collective-permute-start.28 = (bf16[8,512]{1,0:T(8,128)(2,1)S(1)}, bf16[8,512]{1,0:T(8,128)(2,1)S(1)}, u32[]{:S(2)}, u32[]{:S(2)}) collective-permute-start(bf16[8,512]{1,0:T(8,128)(2,1)S(1)} %get-tuple-element.62), channel_id=1, source_target_pairs={{8,0},{16,8},{24,16},{32,24},{40,32},{48,40},{56,48},{64,56},{72,6... | collective-permute-start | bytes 24584 | tf_op jit(solution)/shard_map/ppermute | solution.py:45
  251.4 9.2 %collective-permute-start.38 = (bf16[32,4096]{1,0:T(8,128)(2,1)S(1)}, bf16[32,4096]{1,0:T(8,128)(2,1)S(1)}, u32[]{:S(2)}, u32[]{:S(2)}) collective-permute-start(bf16[32,4096]{1,0:T(8,128)(2,1)S(1)} %get-tuple-element.60), channel_id=1, source_target_pairs={{0,16},{8,24},{16,0},{24,8},{32,48},{40,56},{48,32},{56,40},{64,80... | collective-permute-start | bytes 786440 | tf_op jit(solution)/shard_map/ppermute | solution.py:37
  260.7 10.7 %collective-permute-start.39 = (bf16[32,4096]{1,0:T(8,128)(2,1)S(1)}, bf16[32,4096]{1,0:T(8,128)(2,1)S(1)}, u32[]{:S(2)}, u32[]{:S(2)}) collective-permute-start(bf16[32,4096]{1,0:T(8,128)(2,1)S(1)} %add_convert_fusion.2), channel_id=1, source_target_pairs={{0,32},{8,40},{16,48},{24,56},{32,0},{40,8},{48,16},{56,24},{64,96... | collective-permute-start | bytes 786440 | tf_op jit(solution)/shard_map/ppermute | solution.py:37
  (36 other events, 525.1 us)
Sparse Core Ops, SparseCore 0:
  10.3 66.8 all-gather.2
  121.0 111.4 reduce-scatter.1

commit v5 on v4

--- a/solution.py
+++ b/solution.py
@@ -29,7 +29,7 @@
     def run(*refs):
         kernel(*refs[:inputs], *refs[inputs + len(tokens) :])
 
-    return run, [pl.BlockSpec(memory_space=pl.ANY) for _ in tokens]
+    return run, [pl.BlockSpec(memory_space=pltpu.HBM) for _ in tokens]
 
 
 def flip(value, axis, bit):
@@ -167,7 +167,7 @@
     )(order, *pieces, gen_rows)
 
 
-def conv_up_kernel(
+def layer_kernel(
     order,
     hidden_ref,
     low_ref,
@@ -176,64 +176,84 @@
     flat_two_ref,
     up_ref,
     grad_ref,
-    act_ref,
+    cot_ref,
+    summed_ref,
+    own_ref,
     middle_ref,
-    pre_grad_ref,
+    zero_ref,
+    one_ref,
+    two_ref,
+    three_ref,
     padded,
     pre,
+    pre_grad,
+    act,
+    up_kept,
+    held,
+    sems,
 ):
+    index = pl.program_id(0)
     count, rows, width = hidden_ref.shape
-    step = 64
-    reach = 2 * step
-    heads = 2
-    head_width = width // heads
-    lane = lax.broadcasted_iota(jnp.int32, (step, reach), 1)
-    term = None
-    for piece, flat_ref in enumerate((flat_one_ref, flat_two_ref)):
-        padded[piece, 0:PAD] = low_ref[piece]
-        padded[piece, PAD : PAD + rows] = hidden_ref[piece]
-        padded[piece, PAD + rows : 2 * PAD + rows] = high_ref[piece]
-        padded[piece, 2 * PAD + rows :] = jnp.zeros((step - 2 * PAD, width), BF16)
-        flat = flat_ref[0]
-        taps = jnp.concatenate([flat, jnp.zeros((reach - ROWS, rows), F32)], axis=0).T
-        for base in range(0, rows, step):
-            for head in range(heads):
-                lanes = slice(head * head_width, (head + 1) * head_width)
-                mine = (lane >= head * KW) & (lane < (head + 1) * KW)
-                own = jnp.where(mine, taps[base : base + step], 0.0)
-                own = pltpu.roll(own, (1 - head * KW) % reach, 1)
-                band = pltpu.roll(own, 0, 1, stride=1, stride_axis=0)
-                upper = band.astype(BF16)
-                lower = (band - upper.astype(F32)).astype(BF16)
-                window = padded[piece, base : base + reach, lanes]
-                both = jnp.dot(
-                    jnp.concatenate([upper, lower], axis=0), window, preferred_element_type=F32
-                )
-                value = hidden_ref[piece, base : base + step, lanes].astype(F32)
-                value = value + (both[:step] + both[step:])
-                act_ref[piece, base : base + step, lanes] = value.astype(BF16)
-        part = jnp.dot(
-            act_ref[piece],
-            up_ref[piece * width : (piece + 1) * width, :],
-            preferred_element_type=F32,
-        )
-        term = part if term is None else term + part
-
-    @pl.when(pl.program_id(0) == 0)
+    firsts = act.shape[0] // count
+
+    @pl.when(index < firsts)
     def _():
-        pre[...] = term
-
-    @pl.when(pl.program_id(0) > 0)
-    def _():
-        pre[...] += term
-
-    @pl.when(pl.program_id(0) == pl.num_programs(0) - 1)
+        step = 64
+        reach = 2 * step
+        heads = 2
+        head_width = width // heads
+        lane = lax.broadcasted_iota(jnp.int32, (step, reach), 1)
+        depth = up_ref.shape[0]
+        up_kept[pl.ds(pl.multiple_of(index * depth, depth), depth)] = up_ref[...]
+        term = None
+        for piece, flat_ref in enumerate((flat_one_ref, flat_two_ref)):
+            at = count * index + piece
+            padded[piece, 0:PAD] = low_ref[piece]
+            padded[piece, PAD : PAD + rows] = hidden_ref[piece]
+            padded[piece, PAD + rows : 2 * PAD + rows] = high_ref[piece]
+            padded[piece, 2 * PAD + rows :] = jnp.zeros((step - 2 * PAD, width), BF16)
+            flat = flat_ref[0]
+            taps = jnp.concatenate([flat, jnp.zeros((reach - ROWS, rows), F32)], axis=0).T
+            for base in range(0, rows, step):
+                for head in range(heads):
+                    lanes = slice(head * head_width, (head + 1) * head_width)
+                    mine = (lane >= head * KW) & (lane < (head + 1) * KW)
+                    own = jnp.where(mine, taps[base : base + step], 0.0)
+                    own = pltpu.roll(own, (1 - head * KW) % reach, 1)
+                    band = pltpu.roll(own, 0, 1, stride=1, stride_axis=0)
+                    upper = band.astype(BF16)
+                    lower = (band - upper.astype(F32)).astype(BF16)
+                    window = padded[piece, base : base + reach, lanes]
+                    both = jnp.dot(
+                        jnp.concatenate([upper, lower], axis=0),
+                        window,
+                        preferred_element_type=F32,
+                    )
+                    value = hidden_ref[piece, base : base + step, lanes].astype(F32)
+                    value = value + (both[:step] + both[step:])
+                    act[at, base : base + step, lanes] = value.astype(BF16)
+            part = jnp.dot(
+                act[at],
+                up_ref[piece * width : (piece + 1) * width, :],
+                preferred_element_type=F32,
+            )
+            term = part if term is None else term + part
+
+        @pl.when(index == 0)
+        def _():
+            pre[...] = term
+
+        @pl.when(index > 0)
+        def _():
+            pre[...] += term
+
+    @pl.when(index == firsts - 1)
     def _():
         scale = 0.7978845608028654
         chunk = 64
 
-        def run(index, carry):
-            at = pl.ds(pl.multiple_of(index * chunk, chunk), chunk)
+        def run(turn, carry):
+            at = pl.ds(pl.multiple_of(turn * chunk, chunk), chunk)
             value = pre[at, :]
             square = value * value
             bent = jnp.tanh(scale * (value + 0.044715 * (square * value)))
@@ -241,47 +261,130 @@
             slope = 0.5 * (1.0 + bent) + 0.5 * value * (1.0 - bent * bent) * (
                 scale * (1.0 + 3.0 * 0.044715 * square)
             )
-            pre_grad_ref[at, :] = (grad_ref[at, :] * slope).astype(BF16)
+            pre_grad[at, :] = (grad_ref[at, :] * slope).astype(BF16)
             return carry
 
         lax.fori_loop(0, rows // chunk, run, 0)
-
-
-def conv_up(order, hidden_full, low, high, flat_full, up_weight, middle_grad):
+        own_ref[...] = act[order[0]]
+
+    turn = index - firsts
+    last = act.shape[0] - 1
+    per = held.shape[1]
+    half = held.shape[2] // 2
+
+    def copies(at, slot):
+        return [
+            pltpu.make_async_copy(
+                held.at[slot, chunk, part * half : (part + 1) * half],
+                summed_ref.at[per * at + chunk, part * half : (part + 1) * half],
+                sems.at[slot, 2 * chunk + part],
+            )
+            for chunk in range(per)
+            for part in range(2)
+        ]
+
+    @pl.when(turn >= 0)
+    def _():
+        slot = lax.rem(turn, 2)
+        up = lax.dot_general(act[turn], pre_grad[...], TN, preferred_element_type=F32)
+        down = lax.dot_general(cot_ref[0], middle_ref[...], TN, preferred_element_type=F32)
+
+        @pl.when(turn >= 2)
+        def _():
+            for copy in copies(turn - 2, slot):
+                copy.wait()
+
+        for chunk in range(per):
+            lines = slice(chunk * half, (chunk + 1) * half)
+            held[slot, chunk, 0:half] = up[lines].astype(BF16)
+            held[slot, chunk, half:] = down[lines].astype(BF16)
+        for copy in copies(turn, slot):
+            copy.start()
+        at = pl.multiple_of(order[turn] * width, width)
+        result = lax.dot_general(
+            pre_grad[...], up_kept[pl.ds(at, width)], NT, preferred_element_type=F32
+        ).astype(BF16)
+        for z, ref in enumerate((zero_ref, one_ref, two_ref, three_ref)):
+
+            @pl.when(lax.rem(turn, 4) == z)
+            def _(ref=ref):
+                ref[0] = result
+
+        @pl.when(turn == last)
+        def _():
+            for copy in copies(turn - 1, 1 - slot):
+                copy.wait()
+            for copy in copies(turn, slot):
+                copy.wait()
+
+
+def layer(order, hidden_full, low, high, flat_full, up_weight, middle_grad, cot_full, tokens):
     members, rows, width = hidden_full.shape
     units = up_weight.shape[1]
+    firsts = members // 2
+    chunks = lax.axis_size("seq")
+    per = chunks // members
+    chunk = width // per
+    kernel, token_specs = ordered(layer_kernel, 9, tokens)
+
+    def pair(i):
+        return jnp.minimum(i, firsts - 1)
+
+    def turn(i):
+        return jnp.maximum(i - firsts, 0)
+
     return pl.pallas_call(
-        conv_up_kernel,
+        kernel,
         grid_spec=pltpu.PrefetchScalarGridSpec(
             num_scalar_prefetch=1,
-            grid=(members // 2,),
+            grid=(firsts + members,),
             in_specs=[
-                pl.BlockSpec((2, rows, width), lambda i, o: (i, 0, 0)),
-                pl.BlockSpec((2, PAD, width), lambda i, o: (i, 0, 0)),
-                pl.BlockSpec((2, PAD, width), lambda i, o: (i, 0, 0)),
-                pl.BlockSpec((1, ROWS, rows), lambda i, o: (o[2 * i], 0, 0)),
-                pl.BlockSpec((1, ROWS, rows), lambda i, o: (o[2 * i + 1], 0, 0)),
-                pl.BlockSpec((2 * width, units), lambda i, o: (i, 0)),
+                pl.BlockSpec((2, rows, width), lambda i, o: (pair(i), 0, 0)),
+                pl.BlockSpec((2, PAD, width), lambda i, o: (pair(i), 0, 0)),
+                pl.BlockSpec((2, PAD, width), lambda i, o: (pair(i), 0, 0)),
+                pl.BlockSpec((1, ROWS, rows), lambda i, o: (o[2 * pair(i)], 0, 0)),
+                pl.BlockSpec((1, ROWS, rows), lambda i, o: (o[2 * pair(i) + 1], 0, 0)),
+                pl.BlockSpec((2 * width, units), lambda i, o: (pair(i), 0)),
                 pl.BlockSpec((rows, units), lambda i, o: (0, 0)),
-            ],
+                pl.BlockSpec((1, rows, width), lambda i, o: (turn(i), 0, 0)),
+            ]
+            + token_specs,
             out_specs=[
-                pl.BlockSpec((2, rows, width), lambda i, o: (i, 0, 0)),
+                pl.BlockSpec(memory_space=pltpu.HBM),
+                pl.BlockSpec((rows, width), lambda i, o: (0, 0)),
                 pl.BlockSpec((rows, units), lambda i, o: (0, 0)),
-                pl.BlockSpec((rows, units), lambda i, o: (0, 0)),
-            ],
+            ]
+            + [pl.BlockSpec((1, rows, width), lambda i, o: (turn(i) // 4, 0, 0))] * 4,
             scratch_shapes=[
                 pltpu.VMEM((2, rows + 64, width), BF16),
                 pltpu.VMEM((rows, units), F32),
+                pltpu.VMEM((rows, units), BF16),
+                pltpu.VMEM((members, rows, width), BF16),
+                pltpu.VMEM((members * width, units), BF16),
+                pltpu.VMEM((2, per, 2 * chunk, units), BF16),
+                pltpu.SemaphoreType.DMA((2, 2 * per)),
             ],
         ),
-        out_shape=(
-            jax.ShapeDtypeStruct((members, rows, width), BF16),
+        out_shape=[
+            jax.ShapeDtypeStruct((chunks, 2 * chunk, units), BF16),
+            jax.ShapeDtypeStruct((rows, width), BF16),
             jax.ShapeDtypeStruct((rows, units), BF16),
-            jax.ShapeDtypeStruct((rows, units), BF16),
-        ),
+        ]
+        + [jax.ShapeDtypeStruct((2, rows, width), BF16)] * 4,
         compiler_params=params(),
-        name="conv_up",
-    )(order, hidden_full, low, high, flat_full, flat_full, up_weight, middle_grad)
+        name="layer",
+    )(
+        order,
+        hidden_full,
+        low,
+        high,
+        flat_full,
+        flat_full,
+        up_weight,
+        middle_grad,
+        cot_full,
+        *tokens,
+    )
 
 
 def grad_middle_kernel(cot_ref, *refs):
@@ -314,19 +417,8 @@
     )(cot_full, *[down_weight] * parts)
 
 
-def spread_kernel(transposed, order, value_ref, one_ref, two_ref, *out_refs):
-    value = value_ref[...]
-    if transposed:
-        parts = [
-            lax.dot_general(value, ref[...], NT, preferred_element_type=F32)
-            for ref in (one_ref, two_ref)
-        ]
-        result = jnp.concatenate(parts, axis=1).astype(BF16)
-    else:
-        half = one_ref.shape[0]
-        result = jnp.dot(value[:, :half], one_ref[...], preferred_element_type=F32)
-        result = result + jnp.dot(value[:, half:], two_ref[...], preferred_element_type=F32)
-        result = result.astype(BF16)
+def spread_kernel(order, value_ref, weight_ref, *out_refs):
+    result = jnp.dot(value_ref[...], weight_ref[...], preferred_element_type=F32).astype(BF16)
     for index, ref in enumerate(out_refs):
 
         @pl.when(lax.rem(pl.program_id(0), 4) == index)
@@ -334,102 +426,26 @@
             ref[0] = result
 
 
-def spread(order, value, weight, transposed, name, tokens=()):
+def spread(order, value, weight, tokens):
     rows, units = value.shape
-    if transposed:
-        width = weight.shape[0] // 8
-        block = (width // 2, units)
-        specs = [
-            pl.BlockSpec(block, lambda k, o: (2 * o[k], 0)),
-            pl.BlockSpec(block, lambda k, o: (2 * o[k] + 1, 0)),
-        ]
-    else:
-        width = weight.shape[1] // 8
-        block = (units // 2, width)
-        specs = [
-            pl.BlockSpec(block, lambda k, o: (0, o[k])),
-            pl.BlockSpec(block, lambda k, o: (1, o[k])),
-        ]
-    kernel, token_specs = ordered(functools.partial(spread_kernel, transposed), 4, tokens)
+    width = weight.shape[1] // 8
+    kernel, token_specs = ordered(spread_kernel, 3, tokens)
     return pl.pallas_call(
         kernel,
         grid_spec=pltpu.PrefetchScalarGridSpec(
             num_scalar_prefetch=1,
             grid=(8,),
-            in_specs=[pl.BlockSpec((rows, units), lambda k, o: (0, 0))] + specs + token_specs,
+            in_specs=[
+                pl.BlockSpec((rows, units), lambda k, o: (0, 0)),
+                pl.BlockSpec((units, width), lambda k, o: (0, o[k])),
+            ]
+            + token_specs,
             out_specs=[pl.BlockSpec((1, rows, width), lambda k, o: (k // 4, 0, 0))] * 4,
         ),
         out_shape=[jax.ShapeDtypeStruct((2, rows, width), BF16)] * 4,
         compiler_params=params(),
-        name=name,
-    )(order, value, weight, weight, *tokens)
-
-
-def weight_grads_kernel(act_ref, cot_ref, pre_grad_ref, middle_ref, out_ref, held, sems):
-    step = pl.program_id(0)
-    last = pl.num_programs(0) - 1
-    slot = lax.rem(step, 2)
-    per = held.shape[1]
-    chunk = held.shape[2] // 2
-
-    def copies(at, place):
-        return [
-            pltpu.make_async_copy(
-                held.at[place, index, part * chunk : (part + 1) * chunk],
-                out_ref.at[per * at + index, part * chunk : (part + 1) * chunk],
-                sems.at[place, 2 * index + part],
-            )
-            for index in range(per)
-            for part in range(2)
-        ]
-
-    up = lax.dot_general(act_ref[0], pre_grad_ref[...], TN, preferred_element_type=F32)
-    down = lax.dot_general(cot_ref[0], middle_ref[...], TN, preferred_element_type=F32)
-
-    @pl.when(step >= 2)
-    def _():
-        for copy in copies(step - 2, slot):
-            copy.wait()
-
-    for index in range(per):
-        rows = slice(index * chunk, (index + 1) * chunk)
-        held[slot, index, 0:chunk] = up[rows].astype(BF16)
-        held[slot, index, chunk:] = down[rows].astype(BF16)
-    for copy in copies(step, slot):
-        copy.start()
-
-    @pl.when(step == last)
-    def _():
-        for copy in copies(step - 1, 1 - slot):
-            copy.wait()
-        for copy in copies(step, slot):
-            copy.wait()
-
-
-def weight_grads(act_full, cot_full, pre_grad, middle):
-    pieces, rows, width = act_full.shape
-    units = middle.shape[1]
-    chunks = lax.axis_size("seq")
-    per = chunks // pieces
-    chunk = width // per
-    return pl.pallas_call(
-        weight_grads_kernel,
-        grid=(pieces,),
-        in_specs=[
-            pl.BlockSpec((1, rows, width), lambda i: (i, 0, 0)),
-            pl.BlockSpec((1, rows, width), lambda i: (i, 0, 0)),
-            pl.BlockSpec((rows, units), lambda i: (0, 0)),
-            pl.BlockSpec((rows, units), lambda i: (0, 0)),
-        ],
-        out_specs=pl.BlockSpec(memory_space=pltpu.HBM),
-        out_shape=jax.ShapeDtypeStruct((chunks, 2 * chunk, units), BF16),
-        scratch_shapes=[
-            pltpu.VMEM((2, per, 2 * chunk, units), BF16),
-            pltpu.SemaphoreType.DMA((2, 2 * per)),
-        ],
-        compiler_params=params(),
-        name="weight_grads",
-    )(act_full, cot_full, pre_grad, middle)
+        name="ffn_out",
+    )(order, value, weight, *tokens)
 
 
 def kernel_grad_kernel(*refs):
@@ -605,7 +621,7 @@
             grid=(1,),
             in_specs=[
                 pl.BlockSpec((columns, depth), lambda i, o: (0, 0)),
-                pl.BlockSpec(memory_space=pl.ANY),
+                pl.BlockSpec(memory_space=pltpu.HBM),
             ],
             out_specs=pl.BlockSpec((members, ROWS, width), lambda i, o: (0, 0, 0)),
         ),
@@ -675,21 +691,28 @@
     high_full = lax.ppermute(high_full, "seq", [(i + 1, i) for i in range(count - 1)])
     middle_grad = grad_middle(cot_full, down_weight)
     flat_full = gather_small(flat, (middle_grad,))
-    act_full, middle, pre_grad = conv_up(
-        order, hidden_full, low_full, high_full, flat_full, up_weight, middle_grad
+
+    columns = gen_weight.shape[1]
+    gen_full = gen_blocks(order, gen_weight.T, width, hidden_full)
+    gen_full = exchange(gen_full, (1, 2))
+
+    summed, act, middle, *back_own = layer(
+        order,
+        hidden_full,
+        low_full,
+        high_full,
+        flat_full,
+        up_weight,
+        middle_grad,
+        cot_full,
+        (gen_full,),
     )
-
-    summed = weight_grads(act_full, cot_full, pre_grad, middle)
-    back_own = spread(order, pre_grad, up_weight, True, "act_back", (summed,))
     back_pairs = swap_pairs(back_own)
     summed = lax.psum_scatter(summed, "seq", scatter_dimension=0, tiled=False)
-
-    columns = gen_weight.shape[1]
-    gen_full = gen_blocks(order, gen_weight.T, width, back_own[0])
-    gen_full = exchange(gen_full, (4,))
-    out_pairs = swap_pairs(spread(order, middle, down_weight, False, "ffn_out", (gen_full,)))
-    gen_full = exchange(gen_full, (2, 1)).reshape(members * ROWS, width)
     tap_low, tap_high = halo(taps)
+    out_own = spread(order, middle, down_weight, (tap_low,))
+    out_pairs = swap_pairs(out_own)
+    gen_full = exchange(gen_full, (4,)).reshape(members * ROWS, width)
 
     out_last = flip(add_up([pair[1] for pair in out_pairs]).astype(BF16), "tp", 4)
     back_last = flip(add_up([pair[1] for pair in back_pairs]).astype(BF16), "tp", 4)
@@ -703,11 +726,11 @@
         low,
         high,
         taps,
-        (gen_full, tap_low, tap_high),
+        (gen_full, tap_low, tap_high, out_own[0]),
     )
     grad_low, grad_high = halo(grad.astype(BF16))
     logit_full = gather_small(logit_grad).reshape(members * ROWS, rows)
-    gen_sum = sum_over_seq(gen_grads(logit_grad, hidden_full), (1, 8))
+    gen_sum = sum_over_seq(gen_grads(logit_grad, hidden_full), (1,))
     embed_grad, table_part = hidden_grads(
         (
             grad,
@@ -724,12 +747,11 @@
         codes,
         (gen_sum, out_last),
     )
-    gen_sum = sum_over_seq(gen_sum, (2, 4))
+    gen_sum = sum_over_seq(gen_sum, (8, 2, 4))
     gen_grad = gen_sum[:columns].T
     table_grad = sum_over_seq(table_part)
 
     total = add_up([pair[0] for pair in out_pairs] + [out_last])
-    act = lax.dynamic_index_in_dim(act_full, me, 0, keepdims=False)
     layer_output = (act.astype(F32) + total).astype(BF16)
 
     chunk = summed.shape[0] // 2

time: 284 us -> 286 us (level)
  local copies, waits for them, and re-layouts: 8.45 us -> 14.2 us
  Pallas kernels: 78 us -> 72.6 us
  starting transfers between devices: 60.7 us -> 64.8 us
  waiting for transfers between devices: 108 us -> 104 us
    pallas_call x2 -> x1, Pallas kernels: 22.4 us -> 11.3 us  [spread(): pl.pallas_call(kernel, grid_spec=pltpu.PrefetchScalarGridSpec(num_scalar_...]
    unnamed x53 -> x65, local copies, waits for them, and re-layouts: 3.78 us -> 9.64 us
    pallas_call x2 -> x1, Pallas kernels: 31.2 us -> 35.7 us  [layer(): pl.pallas_call(kernel, grid_spec=pltpu.PrefetchScalarGridSpec(num_scalar_...]
    ppermute x34, waiting for transfers between devices: 105 us -> 101 us  [flip(): return lax.ppermute(value, axis, [(i, i ^ bit) for i in range(count)])]
  transfers between devices with their start and end apart: 42 -> 42, of which waited for: 22 -> 22; matrix products, arithmetic and copies ran while one was open for 5% -> 6% of each run, Pallas kernels for 17% -> 13%
where the time goes in v5:
time: 286 us; the launch traced here: 285 us
  waiting for transfers between devices  104 us (36%)
  Pallas kernels  72.6 us (25%)
  starting transfers between devices  64.8 us (23%)
  between operations  14.6 us (5%)
  local copies, waits for them, and re-layouts  14.2 us (5%)
  other arithmetic  13.4 us (5%)
    ppermute x34, waiting for transfers between devices, flip(): return lax.ppermute(value, axis, [(i, i ^ bit) for i in range(count)])  101 us
    ppermute x34, starting transfers between devices, flip(): return lax.ppermute(value, axis, [(i, i ^ bit) for i in range(count)])  53.6 us
    pallas_call x1, Pallas kernels, layer(): pl.pallas_call(kernel, grid_spec=pltpu.PrefetchScalarGridSpec(num_scalar_...  35.7 us
    pallas_call x1, Pallas kernels, spread(): pl.pallas_call(kernel, grid_spec=pltpu.PrefetchScalarGridSpec(num_scalar_...  11.3 us
    unnamed x65, local copies, waits for them, and re-layouts  9.64 us
    pallas_call x1, Pallas kernels, grad_middle(): pl.pallas_call(grad_middle_kernel, grid=(units // block,), in_specs=[pl.B...  8.62 us
    pallas_call x1, Pallas kernels, hidden_logits(): pl.pallas_call(hidden_logits_kernel, grid_spec=pltpu.PrefetchScalarGridSp...  6 us
  transfers between devices with their start and end apart: 42, of which 22 were waited for; matrix products, arithmetic and copies ran while one was open for 6% of the time, Pallas kernels for 13%

profile of v5, /device:TPU:0, one launch (start us, length us, event | category | flops | bytes accessed | tf_op | source)
XLA Modules:
  0.0 285.3 jit_solution(13270078326728365341)
XLA Ops:
  10.0 3.2 %collective-permute-start.2 = (bf16[384,512]{1,0:T(8,128)(2,1)S(1)}, bf16[384,512]{1,0:T(8,128)(2,1)S(1)}, u32[]{:S(2)}, u32[]{:S(2)}) collective-permute-start(bf16[384,512]{1,0:T(8,128)(2,1)S(1)} %fusion.refs_0_.refs_6_), channel_id=1, source_target_pairs={{0,4},{1,5},{2,6},{3,7},{4,0},{5,1},{6,2},{7,3},{8,12},{9,13},{10,... | collective-permute-start | bytes 1179656 | tf_op jit(solution)/shard_map/ppermute | solution.py:37
  15.1 2.5 collective-permute-start.1
  17.6 4.7 %collective-permute-done.2.refs_3_ = bf16[384,512]{1,0:T(8,128)(2,1)S(1)} collective-permute-done((bf16[384,512]{1,0:T(8,128)(2,1)S(1)}, bf16[384,512]{1,0:T(8,128)(2,1)S(1)}, u32[]{:S(2)}, u32[]{:S(2)}) %collective-permute-start.2) | collective-permute-done | bytes 393248 | tf_op jit(solution)/shard_map/ppermute | solution.py:37
  24.4 2.5 collective-permute-start.4
  29.4 11.3 %collective-permute-done.3.refs_4_ = bf16[384,512]{1,0:T(8,128)(2,1)S(1)} collective-permute-done((bf16[384,512]{1,0:T(8,128)(2,1)S(1)}, bf16[384,512]{1,0:T(8,128)(2,1)S(1)}, u32[]{:S(2)}, u32[]{:S(2)}) %collective-permute-start.3) | collective-permute-done | bytes 393248 | tf_op jit(solution)/shard_map/ppermute | solution.py:37
  41.4 2.7 collective-permute-start.7
  46.8 3.3 %collective-permute-done.7.refs_8_ = bf16[192,512]{1,0:T(8,128)(2,1)S(1)} collective-permute-done((bf16[192,512]{1,0:T(8,128)(2,1)}, bf16[192,512]{1,0:T(8,128)(2,1)S(1)}, u32[]{:S(2)}, u32[]{:S(2)}) %collective-permute-start.7) | collective-permute-done | bytes 196640 | tf_op jit(solution)/shard_map/ppermute | solution.py:37
  52.6 6.0 %hidden_logits.1 = (bf16[8,384,512]{2,1,0:T(8,128)(2,1)}, bf16[2,8,8,512]{3,2,1,0:T(8,128)(2,1)}, f32[32,384]{1,0:T(8,128)}, f32[384,32]{1,0:T(8,128)}) custom-call(s32[8]{0:T(128)} %iota_xor_fusion.order.refs_0_, bf16[384,512]{1,0:T(8,128)(2,1)} %copy-done.4, bf16[384,512]{1,0:T(8,128)(2,1)} %copy-done.17, bf16[384,512]{1,0:T(8,128)(2,1)} %copy-done.18, ...), custom_call_target="tpu_custom_call" | custom-call | tf_op jit(solution)/shard_map/hidden_logits/pallas_call | solution.py:142
  70.3 2.8 collective-permute-start.15
  73.2 2.9 %collective-permute-done.12 = f32[2,32,384]{2,1,0:T(8,128)S(1)} collective-permute-done((f32[2,32,384]{2,1,0:T(8,128)S(1)}, f32[2,32,384]{2,1,0:T(8,128)S(1)}, u32[]{:S(2)}, u32[]{:S(2)}) %collective-permute-start.12) | collective-permute-done | bytes 98336 | tf_op jit(solution)/shard_map/ppermute | solution.py:37
  76.9 3.3 %collective-permute-start.13 = (f32[4,32,384]{2,1,0:T(8,128)S(1)}, f32[4,32,384]{2,1,0:T(8,128)S(1)}, u32[]{:S(2)}, u32[]{:S(2)}) collective-permute-start(f32[4,32,384]{2,1,0:T(8,128)S(1)} %pad_maximum_fusion.3), channel_id=1, source_target_pairs={{0,4},{1,5},{2,6},{3,7},{4,0},{5,1},{6,2},{7,3},{8,12},{9,13},{10,... | collective-permute-start | bytes 589832 | tf_op jit(solution)/shard_map/ppermute | solution.py:37
  82.4 3.0 %collective-permute-start.9 = (bf16[8,8,512]{2,1,0:T(8,128)(2,1)S(1)}, bf16[8,8,512]{2,1,0:T(8,128)(2,1)S(1)}, u32[]{:S(2)}, u32[]{:S(2)}) collective-permute-start(bf16[8,8,512]{2,1,0:T(8,128)(2,1)S(1)} %get-tuple-element.73), channel_id=1, source_target_pairs={{0,8},{8,16},{16,24},{24,32},{32,40},{40,48},{48,56},{56,64},{64,7... | collective-permute-start | bytes 196616 | tf_op jit(solution)/shard_map/ppermute | solution.py:690
  87.1 8.6 %grad_middle.1.refs_7_ = f32[384,1024]{1,0:T(8,128)} custom-call(bf16[8,384,512]{2,1,0:T(8,128)(2,1)} %bitcast.51, bf16[1024,4096]{1,0:T(8,128)(2,1)} %refs_2_.3, bf16[1024,4096]{1,0:T(8,128)(2,1)} %refs_2_.3, bf16[1024,4096]{1,0:T(8,128)(2,1)} %refs_2_.3, bf16[1024,4096]{1,0:T(8,128)(2,1)} %refs_2_.3), custom_call_target="tpu_custom_call" | custom-call | tf_op jit(solution)/shard_map/grad_middle/pallas_call | solution.py:408
  97.1 35.7 %layer.1 = (bf16[16,512,1024]{2,1,0:T(8,128)(2,1)}, bf16[384,512]{1,0:T(8,128)(2,1)}, bf16[384,1024]{1,0:T(8,128)(2,1)}, bf16[2,384,512]{2,1,0:T(8,128)(2,1)}, b...) custom-call(s32[8]{0:T(128)} %iota_xor_fusion.order.refs_0_, ...), custom_call_target="tpu_custom_call" | custom-call | tf_op jit(solution)/shard_map/layer/pallas_call | solution.py:336
  135.3 2.4 collective-permute-start.23
  138.3 2.6 collective-permute-start.16
  142.3 11.3 %ffn_out.1 = (bf16[2,384,512]{2,1,0:T(8,128)(2,1)}, bf16[2,384,512]{2,1,0:T(8,128)(2,1)}, bf16[2,384,512]{2,1,0:T(8,128)(2,1)}, bf16[2,384,512]{2,1,0:T(8,128)(2,1)}) custom-call(s32[8]{0:T(128)} %iota_xor_fusion.order.refs_0_, bf16[384,1024]{1,0:T(8,128)(2,1)} %get-tuple-element.31.refs_1_, bf16[1024,4096]{1,0:T(8,128)(2,1)} %refs_2_.3, f32[8,32]{1,0:T(8,128)} %copy-done.12), custom_call_target="tpu_custom_call" | custom-call | tf_op jit(solution)/shard_map/ffn_out/pallas_call | solution.py:433
  155.9 2.5 collective-permute-start.19
  158.4 12.3 %collective-permute-done.22.refs_2_ = bf16[2,384,512]{2,1,0:T(8,128)(2,1)} collective-permute-done((bf16[2,384,512]{2,1,0:T(8,128)(2,1)}, bf16[2,384,512]{2,1,0:T(8,128)(2,1)}, u32[]{:S(2)}, u32[]{:S(2)}) %collective-permute-start.22) | collective-permute-done | bytes 786464 | tf_op jit(solution)/shard_map/ppermute | solution.py:37
  170.6 3.4 %collective-permute-done.23.refs_3_ = bf16[2,384,512]{2,1,0:T(8,128)(2,1)} collective-permute-done((bf16[2,384,512]{2,1,0:T(8,128)(2,1)}, bf16[2,384,512]{2,1,0:T(8,128)(2,1)}, u32[]{:S(2)}, u32[]{:S(2)}) %collective-permute-start.23) | collective-permute-done | bytes 786464 | tf_op jit(solution)/shard_map/ppermute | solution.py:37
  178.0 2.4 collective-permute-start.25
  181.7 15.3 %collective-permute-done.25 = bf16[1,2,2,32,512]{4,3,2,1,0:T(8,128)(2,1)S(1)} collective-permute-done((bf16[1,2,2,32,512]{4,3,2,1,0:T(8,128)(2,1)S(1)}, bf16[1,2,2,32,512]{4,3,2,1,0:T(8,128)(2,1)S(1)}, u32[]{:S(2)}, u32[]{:S(2)}) %collective-permute-start.25) | collective-permute-done | bytes 131104 | tf_op jit(solution)/shard_map/ppermute | solution.py:37
  203.2 5.0 %kernel_grads.1 = (f32[384,512]{1,0:T(8,128)S(1)}, bf16[32,384]{1,0:T(8,128)(2,1)S(1)}) custom-call(bf16[2,384,512]{2,1,0:T(8,128)(2,1)S(1)} %copy-done.8, bf16[2,384,512]{2,1,0:T(8,128)(2,1)} %collective-permute-done.21.refs_1_, bf16[2,384,512]{2,1,0:T(8,128)(2,1)} %collective-permute-done.22.refs_2_, bf16[2,384,512]{2,1,0:T(8,128)(2,1)} %collective-permute-done.23.refs_3_, ...), custom_call_target="tpu_custom_call" | custom-call | tf_op jit(solution)/shard_map/kernel_grads/pallas_call | solution.py:498
  208.5 3.9 %collective-permute-done.29 = bf16[1,32,384]{2,1,0:T(8,128)(2,1)S(1)} collective-permute-done((bf16[1,32,384]{2,1,0:T(8,128)(2,1)S(1)}, bf16[1,32,384]{2,1,0:T(8,128)(2,1)S(1)}, u32[]{:S(2)}, u32[]{:S(2)}) %collective-permute-start.29) | collective-permute-done | bytes 24608 | tf_op jit(solution)/shard_map/ppermute | solution.py:37
  222.9 12.7 %collective-permute-done.31 = bf16[4,32,384]{2,1,0:T(8,128)(2,1)S(1)} collective-permute-done((bf16[4,32,384]{2,1,0:T(8,128)(2,1)S(1)}, bf16[4,32,384]{2,1,0:T(8,128)(2,1)S(1)}, u32[]{:S(2)}, u32[]{:S(2)}) %collective-permute-start.31) | collective-permute-done | bytes 98336 | tf_op jit(solution)/shard_map/ppermute | solution.py:37
  235.8 4.8 %hidden_grads.1 = (f32[384,512]{1,0:T(8,128)}, f32[100,512]{1,0:T(8,128)S(1)}) custom-call(f32[384,512]{1,0:T(8,128)S(1)} %get-tuple-element.41.refs_0_, bf16[8,512]{1,0:T(8,128)(2,1)S(1)} %collective-permute-done.27.refs_1_, bf16[8,512]{1,0:T(8,128)(2,1)S(1)} %collective-permute-done.28.refs_2_, f32[384,32]{1,0:T(8,128)S(1)} %copy-done.11, ...), custom_call_target="tpu_custom_call" | custom-call | tf_op jit(solution)/shard_map/hidden_grads/pallas_call | solution.py:583
  242.1 2.6 collective-permute-start.34
  244.8 4.9 %collective-permute-done.34 = bf16[100,512]{1,0:T(8,128)(2,1)S(1)} collective-permute-done((bf16[100,512]{1,0:T(8,128)(2,1)S(1)}, bf16[100,512]{1,0:T(8,128)(2,1)S(1)}, u32[]{:S(2)}, u32[]{:S(2)}) %collective-permute-start.34) | collective-permute-done | bytes 102432 | tf_op jit(solution)/shard_map/ppermute | solution.py:37
  249.8 6.7 %collective-permute-done.37 = bf16[32,4096]{1,0:T(8,128)(2,1)S(1)} collective-permute-done((bf16[32,4096]{1,0:T(8,128)(2,1)S(1)}, bf16[32,4096]{1,0:T(8,128)(2,1)S(1)}, u32[]{:S(2)}, u32[]{:S(2)}) %collective-permute-start.37) | collective-permute-done | bytes 262176 | tf_op jit(solution)/shard_map/ppermute | solution.py:37
  256.7 3.6 %collective-permute-start.36 = (bf16[100,512]{1,0:T(8,128)(2,1)S(1)}, bf16[100,512]{1,0:T(8,128)(2,1)S(1)}, u32[]{:S(2)}, u32[]{:S(2)}) collective-permute-start(bf16[100,512]{1,0:T(8,128)(2,1)S(1)} %add_convert_fusion.4), channel_id=1, source_target_pairs={{0,32},{8,40},{16,48},{24,56},{32,0},{40,8},{48,16},{56,24},{64,96... | collective-permute-start | bytes 307208 | tf_op jit(solution)/shard_map/ppermute | solution.py:37
  260.2 5.6 %collective-permute-done.38 = bf16[32,4096]{1,0:T(8,128)(2,1)S(1)} collective-permute-done((bf16[32,4096]{1,0:T(8,128)(2,1)S(1)}, bf16[32,4096]{1,0:T(8,128)(2,1)S(1)}, u32[]{:S(2)}, u32[]{:S(2)}) %collective-permute-start.38) | collective-permute-done | bytes 262176 | tf_op jit(solution)/shard_map/ppermute | solution.py:37
  269.2 4.8 %collective-permute-done.39 = bf16[32,4096]{1,0:T(8,128)(2,1)S(1)} collective-permute-done((bf16[32,4096]{1,0:T(8,128)(2,1)S(1)}, bf16[32,4096]{1,0:T(8,128)(2,1)S(1)}, u32[]{:S(2)}, u32[]{:S(2)}) %collective-permute-start.39) | collective-permute-done | bytes 262176 | tf_op jit(solution)/shard_map/ppermute | solution.py:37
  (167 shorter events, 71.6 us)
Async XLA Ops:
  7.2 79.9 %all-gather.3.cloned.1.call-start = ((), (), s32[]{:S(2)}) async-start(), calls=%async_computation.2 | async-start | bytes 3538944 | tf_op jit(solution)/shard_map/all_gather | solution.py:685
  7.9 266.9 %reduce-scatter.2.cloned.1.call-start = ((), (), s32[]{:S(2)}) async-start(), calls=%async_computation.1 | async-start | bytes 17825792 | tf_op jit(solution)/shard_map/reduce_scatter | solution.py:711
  10.0 12.3 %collective-permute-start.2 = (bf16[384,512]{1,0:T(8,128)(2,1)S(1)}, bf16[384,512]{1,0:T(8,128)(2,1)S(1)}, u32[]{:S(2)}, u32[]{:S(2)}) collective-permute-start(bf16[384,512]{1,0:T(8,128)(2,1)S(1)} %fusion.refs_0_.refs_6_), channel_id=1, source_target_pairs={{0,4},{1,5},{2,6},{3,7},{4,0},{5,1},{6,2},{7,3},{8,12},{9,13},{10,... | collective-permute-start | bytes 1179656 | tf_op jit(solution)/shard_map/ppermute | solution.py:37
  13.2 13.8 %collective-permute-start = (bf16[384,512]{1,0:T(8,128)(2,1)S(1)}, bf16[384,512]{1,0:T(8,128)(2,1)S(1)}, u32[]{:S(2)}, u32[]{:S(2)}) collective-permute-start(bf16[384,512]{1,0:T(8,128)(2,1)S(1)} %fusion.refs_0_.refs_6_), channel_id=1, source_target_pairs={{0,1},{1,0},{2,3},{3,2},{4,5},{5,4},{6,7},{7,6},{8,9},{9,8},{10,11... | collective-permute-start | bytes 1179656 | tf_op jit(solution)/shard_map/ppermute | solution.py:37
  15.1 13.5 %collective-permute-start.1 = (bf16[384,512]{1,0:T(8,128)(2,1)S(1)}, bf16[384,512]{1,0:T(8,128)(2,1)S(1)}, u32[]{:S(2)}, u32[]{:S(2)}) collective-permute-start(bf16[384,512]{1,0:T(8,128)(2,1)S(1)} %fusion.refs_0_.refs_6_), channel_id=1, source_target_pairs={{0,3},{1,2},{2,1},{3,0},{4,7},{5,6},{6,5},{7,4},{8,11},{9,10},{10,... | collective-permute-start | bytes 1179656 | tf_op jit(solution)/shard_map/ppermute | solution.py:37
  22.3 18.4 %collective-permute-start.3 = (bf16[384,512]{1,0:T(8,128)(2,1)S(1)}, bf16[384,512]{1,0:T(8,128)(2,1)S(1)}, u32[]{:S(2)}, u32[]{:S(2)}) collective-permute-start(bf16[384,512]{1,0:T(8,128)(2,1)S(1)} %collective-permute-done.2.refs_3_), channel_id=1, source_target_pairs={{0,1},{1,0},{2,3},{3,2},{4,5},{5,4},{6,7},{7,6},{8,9},{9,8},{10,11... | collective-permute-start | bytes 1179656 | tf_op jit(solution)/shard_map/ppermute | solution.py:37
  24.4 19.7 %collective-permute-start.4 = (bf16[384,512]{1,0:T(8,128)(2,1)S(1)}, bf16[384,512]{1,0:T(8,128)(2,1)S(1)}, u32[]{:S(2)}, u32[]{:S(2)}) collective-permute-start(bf16[384,512]{1,0:T(8,128)(2,1)S(1)} %collective-permute-done.2.refs_3_), channel_id=1, source_target_pairs={{0,3},{1,2},{2,1},{3,0},{4,7},{5,6},{6,5},{7,4},{8,11},{9,10},{10,... | collective-permute-start | bytes 1179656 | tf_op jit(solution)/shard_map/ppermute | solution.py:37
  27.0 19.8 %collective-permute-start.5 = (bf16[192,512]{1,0:T(8,128)(2,1)S(1)}, bf16[192,512]{1,0:T(8,128)(2,1)S(1)}, u32[]{:S(2)}, u32[]{:S(2)}) collective-permute-start(bf16[192,512]{1,0:T(8,128)(2,1)S(1)} %slice.126), channel_id=1, source_target_pairs={{0,3},{1,2},{2,1},{3,0},{4,7},{5,6},{6,5},{7,4},{8,11},{9,10},{10,... | collective-permute-start | bytes 589832 | tf_op jit(solution)/shard_map/ppermute | solution.py:37
  28.6 18.2 %collective-permute-start.6 = (bf16[192,512]{1,0:T(8,128)(2,1)S(1)}, bf16[192,512]{1,0:T(8,128)(2,1)S(1)}, u32[]{:S(2)}, u32[]{:S(2)}) collective-permute-start(bf16[192,512]{1,0:T(8,128)(2,1)S(1)} %slice.127), channel_id=1, source_target_pairs={{0,1},{1,0},{2,3},{3,2},{4,5},{5,4},{6,7},{7,6},{8,9},{9,8},{10,11... | collective-permute-start | bytes 589832 | tf_op jit(solution)/shard_map/ppermute | solution.py:37
  41.4 8.7 %collective-permute-start.7 = (bf16[192,512]{1,0:T(8,128)(2,1)}, bf16[192,512]{1,0:T(8,128)(2,1)S(1)}, u32[]{:S(2)}, u32[]{:S(2)}) collective-permute-start(bf16[192,512]{1,0:T(8,128)(2,1)} %slice.128), channel_id=1, source_target_pairs={{0,3},{1,2},{2,1},{3,0},{4,7},{5,6},{6,5},{7,4},{8,11},{9,10},{10,... | collective-permute-start | bytes 589832 | tf_op jit(solution)/shard_map/ppermute | solution.py:37
  67.9 8.2 %collective-permute-start.12 = (f32[2,32,384]{2,1,0:T(8,128)S(1)}, f32[2,32,384]{2,1,0:T(8,128)S(1)}, u32[]{:S(2)}, u32[]{:S(2)}) collective-permute-start(f32[2,32,384]{2,1,0:T(8,128)S(1)} %pad_maximum_fusion.6), channel_id=1, source_target_pairs={{0,2},{1,3},{2,0},{3,1},{4,6},{5,7},{6,4},{7,5},{8,10},{9,11},{10,... | collective-permute-start | bytes 294920 | tf_op jit(solution)/shard_map/ppermute | solution.py:37
  70.3 15.1 %collective-permute-start.15 = (bf16[2,1,2,32,512]{4,3,2,1,0:T(8,128)(2,1)S(1)}, bf16[2,1,2,32,512]{4,3,2,1,0:T(8,128)(2,1)}, u32[]{:S(2)}, u32[]{:S(2)}) collective-permute-start(bf16[2,1,2,32,512]{4,3,2,1,0:T(8,128)(2,1)S(1)} %get-tuple-element.67), channel_id=1, source_target_pairs={{0,2},{1,3},{2,0},{3,1},{4,6},{5,7},{6,4},{7,5},{8,10},{9,11},{10,... | collective-permute-start | bytes 393224 | tf_op jit(solution)/shard_map/ppermute | solution.py:37
  76.9 18.8 %collective-permute-start.13 = (f32[4,32,384]{2,1,0:T(8,128)S(1)}, f32[4,32,384]{2,1,0:T(8,128)S(1)}, u32[]{:S(2)}, u32[]{:S(2)}) collective-permute-start(f32[4,32,384]{2,1,0:T(8,128)S(1)} %pad_maximum_fusion.3), channel_id=1, source_target_pairs={{0,4},{1,5},{2,6},{3,7},{4,0},{5,1},{6,2},{7,3},{8,12},{9,13},{10,... | collective-permute-start | bytes 589832 | tf_op jit(solution)/shard_map/ppermute | solution.py:37
  81.1 15.4 %collective-permute-start.10 = (bf16[8,8,512]{2,1,0:T(8,128)(2,1)S(1)}, bf16[8,8,512]{2,1,0:T(8,128)(2,1)S(1)}, u32[]{:S(2)}, u32[]{:S(2)}) collective-permute-start(bf16[8,8,512]{2,1,0:T(8,128)(2,1)S(1)} %get-tuple-element.72), channel_id=1, source_target_pairs={{8,0},{16,8},{24,16},{32,24},{40,32},{48,40},{56,48},{64,56},{72,6... | collective-permute-start | bytes 196616 | tf_op jit(solution)/shard_map/ppermute | solution.py:691
  82.4 14.1 %collective-permute-start.9 = (bf16[8,8,512]{2,1,0:T(8,128)(2,1)S(1)}, bf16[8,8,512]{2,1,0:T(8,128)(2,1)S(1)}, u32[]{:S(2)}, u32[]{:S(2)}) collective-permute-start(bf16[8,8,512]{2,1,0:T(8,128)(2,1)S(1)} %get-tuple-element.73), channel_id=1, source_target_pairs={{0,8},{8,16},{16,24},{24,32},{32,40},{40,48},{48,56},{56,64},{64,7... | collective-permute-start | bytes 196616 | tf_op jit(solution)/shard_map/ppermute | solution.py:690
  132.9 23.0 %collective-permute-start.21 = (bf16[2,384,512]{2,1,0:T(8,128)(2,1)}, bf16[2,384,512]{2,1,0:T(8,128)(2,1)}, u32[]{:S(2)}, u32[]{:S(2)}) collective-permute-start(bf16[2,384,512]{2,1,0:T(8,128)(2,1)} %get-tuple-element.38), channel_id=1, source_target_pairs={{0,1},{1,0},{2,3},{3,2},{4,5},{5,4},{6,7},{7,6},{8,9},{9,8},{10,11... | collective-permute-start | bytes 2359304 | tf_op jit(solution)/shard_map/ppermute | solution.py:37
  133.9 36.8 %collective-permute-start.22 = (bf16[2,384,512]{2,1,0:T(8,128)(2,1)}, bf16[2,384,512]{2,1,0:T(8,128)(2,1)}, u32[]{:S(2)}, u32[]{:S(2)}) collective-permute-start(bf16[2,384,512]{2,1,0:T(8,128)(2,1)} %get-tuple-element.39), channel_id=1, source_target_pairs={{0,2},{1,3},{2,0},{3,1},{4,6},{5,7},{6,4},{7,5},{8,10},{9,11},{10,... | collective-permute-start | bytes 2359304 | tf_op jit(solution)/shard_map/ppermute | solution.py:37
  135.3 38.8 %collective-permute-start.23 = (bf16[2,384,512]{2,1,0:T(8,128)(2,1)}, bf16[2,384,512]{2,1,0:T(8,128)(2,1)}, u32[]{:S(2)}, u32[]{:S(2)}) collective-permute-start(bf16[2,384,512]{2,1,0:T(8,128)(2,1)} %get-tuple-element.40), channel_id=1, source_target_pairs={{0,3},{1,2},{2,1},{3,0},{4,7},{5,6},{6,5},{7,4},{8,11},{9,10},{10,... | collective-permute-start | bytes 2359304 | tf_op jit(solution)/shard_map/ppermute | solution.py:37
  153.6 60.8 %collective-permute-start.17 = (bf16[2,384,512]{2,1,0:T(8,128)(2,1)}, bf16[2,384,512]{2,1,0:T(8,128)(2,1)S(1)}, u32[]{:S(2)}, u32[]{:S(2)}) collective-permute-start(bf16[2,384,512]{2,1,0:T(8,128)(2,1)} %get-tuple-element.34), channel_id=1, source_target_pairs={{0,1},{1,0},{2,3},{3,2},{4,5},{5,4},{6,7},{7,6},{8,9},{9,8},{10,11... | collective-permute-start | bytes 2359304 | tf_op jit(solution)/shard_map/ppermute | solution.py:37
  153.7 60.7 %collective-permute-start.18 = (bf16[2,384,512]{2,1,0:T(8,128)(2,1)}, bf16[2,384,512]{2,1,0:T(8,128)(2,1)S(1)}, u32[]{:S(2)}, u32[]{:S(2)}) collective-permute-start(bf16[2,384,512]{2,1,0:T(8,128)(2,1)} %get-tuple-element.35), channel_id=1, source_target_pairs={{0,2},{1,3},{2,0},{3,1},{4,6},{5,7},{6,4},{7,5},{8,10},{9,11},{10,... | collective-permute-start | bytes 2359304 | tf_op jit(solution)/shard_map/ppermute | solution.py:37
  155.9 58.5 %collective-permute-start.19 = (bf16[2,384,512]{2,1,0:T(8,128)(2,1)}, bf16[2,384,512]{2,1,0:T(8,128)(2,1)S(1)}, u32[]{:S(2)}, u32[]{:S(2)}) collective-permute-start(bf16[2,384,512]{2,1,0:T(8,128)(2,1)} %get-tuple-element.36), channel_id=1, source_target_pairs={{0,3},{1,2},{2,1},{3,0},{4,7},{5,6},{6,5},{7,4},{8,11},{9,10},{10,... | collective-permute-start | bytes 2359304 | tf_op jit(solution)/shard_map/ppermute | solution.py:37
  175.7 24.6 %collective-permute-start.24 = (bf16[384,512]{1,0:T(8,128)(2,1)S(1)}, bf16[384,512]{1,0:T(8,128)(2,1)S(1)}, u32[]{:S(2)}, u32[]{:S(2)}) collective-permute-start(bf16[384,512]{1,0:T(8,128)(2,1)S(1)} %fusion.5), channel_id=1, source_target_pairs={{0,4},{1,5},{2,6},{3,7},{4,0},{5,1},{6,2},{7,3},{8,12},{9,13},{10,... | collective-permute-start | bytes 1179656 | tf_op jit(solution)/shard_map/ppermute | solution.py:37
  178.0 19.1 %collective-permute-start.25 = (bf16[1,2,2,32,512]{4,3,2,1,0:T(8,128)(2,1)S(1)}, bf16[1,2,2,32,512]{4,3,2,1,0:T(8,128)(2,1)S(1)}, u32[]{:S(2)}, u32[]{:S(2)}) collective-permute-start(bf16[1,2,2,32,512]{4,3,2,1,0:T(8,128)(2,1)S(1)} %get-tuple-element.65), channel_id=1, source_target_pairs={{0,4},{1,5},{2,6},{3,7},{4,0},{5,1},{6,2},{7,3},{8,12},{9,13},{10,... | collective-permute-start | bytes 393224 | tf_op jit(solution)/shard_map/ppermute | solution.py:37
  214.6 21.1 %collective-permute-start.20 = (bf16[384,512]{1,0:T(8,128)(2,1)S(1)}, bf16[384,512]{1,0:T(8,128)(2,1)S(1)}, u32[]{:S(2)}, u32[]{:S(2)}) collective-permute-start(bf16[384,512]{1,0:T(8,128)(2,1)S(1)} %fusion.4), channel_id=1, source_target_pairs={{0,4},{1,5},{2,6},{3,7},{4,0},{5,1},{6,2},{7,3},{8,12},{9,13},{10,... | collective-permute-start | bytes 1179656 | tf_op jit(solution)/shard_map/ppermute | solution.py:37
  215.7 20.0 %collective-permute-start.32 = (bf16[32,4096]{1,0:T(8,128)(2,1)S(1)}, bf16[32,4096]{1,0:T(8,128)(2,1)S(1)}, u32[]{:S(2)}, u32[]{:S(2)}) collective-permute-start(bf16[32,4096]{1,0:T(8,128)(2,1)S(1)} %convert_element_type.165), channel_id=1, source_target_pairs={{0,8},{8,0},{16,24},{24,16},{32,40},{40,32},{48,56},{56,48},{64,72... | collective-permute-start | bytes 786440 | tf_op jit(solution)/shard_map/ppermute | solution.py:37
  218.1 17.5 %collective-permute-start.31 = (bf16[4,32,384]{2,1,0:T(8,128)(2,1)S(1)}, bf16[4,32,384]{2,1,0:T(8,128)(2,1)S(1)}, u32[]{:S(2)}, u32[]{:S(2)}) collective-permute-start(bf16[4,32,384]{2,1,0:T(8,128)(2,1)S(1)} %pad_maximum_fusion.7), channel_id=1, source_target_pairs={{0,4},{1,5},{2,6},{3,7},{4,0},{5,1},{6,2},{7,3},{8,12},{9,13},{10,... | collective-permute-start | bytes 294920 | tf_op jit(solution)/shard_map/ppermute | solution.py:37
  220.0 15.8 %collective-permute-start.27 = (bf16[8,512]{1,0:T(8,128)(2,1)S(1)}, bf16[8,512]{1,0:T(8,128)(2,1)S(1)}, u32[]{:S(2)}, u32[]{:S(2)}) collective-permute-start(bf16[8,512]{1,0:T(8,128)(2,1)S(1)} %get-tuple-element.63), channel_id=1, source_target_pairs={{0,8},{8,16},{16,24},{24,32},{32,40},{40,48},{48,56},{56,64},{64,7... | collective-permute-start | bytes 24584 | tf_op jit(solution)/shard_map/ppermute | solution.py:44
  221.6 14.2 %collective-permute-start.28 = (bf16[8,512]{1,0:T(8,128)(2,1)S(1)}, bf16[8,512]{1,0:T(8,128)(2,1)S(1)}, u32[]{:S(2)}, u32[]{:S(2)}) collective-permute-start(bf16[8,512]{1,0:T(8,128)(2,1)S(1)} %get-tuple-element.62), channel_id=1, source_target_pairs={{8,0},{16,8},{24,16},{32,24},{40,32},{48,40},{56,48},{64,56},{72,6... | collective-permute-start | bytes 24584 | tf_op jit(solution)/shard_map/ppermute | solution.py:45
  244.7 11.8 %collective-permute-start.37 = (bf16[32,4096]{1,0:T(8,128)(2,1)S(1)}, bf16[32,4096]{1,0:T(8,128)(2,1)S(1)}, u32[]{:S(2)}, u32[]{:S(2)}) collective-permute-start(bf16[32,4096]{1,0:T(8,128)(2,1)S(1)} %get-tuple-element.60), channel_id=1, source_target_pairs={{0,64},{8,72},{16,80},{24,88},{32,96},{40,104},{48,112},{56,120},{... | collective-permute-start | bytes 786440 | tf_op jit(solution)/shard_map/ppermute | solution.py:37
  256.5 9.3 %collective-permute-start.38 = (bf16[32,4096]{1,0:T(8,128)(2,1)S(1)}, bf16[32,4096]{1,0:T(8,128)(2,1)S(1)}, u32[]{:S(2)}, u32[]{:S(2)}) collective-permute-start(bf16[32,4096]{1,0:T(8,128)(2,1)S(1)} %add_convert_fusion.3), channel_id=1, source_target_pairs={{0,16},{8,24},{16,0},{24,8},{32,48},{40,56},{48,32},{56,40},{64,80... | collective-permute-start | bytes 786440 | tf_op jit(solution)/shard_map/ppermute | solution.py:37
  256.7 11.8 %collective-permute-start.36 = (bf16[100,512]{1,0:T(8,128)(2,1)S(1)}, bf16[100,512]{1,0:T(8,128)(2,1)S(1)}, u32[]{:S(2)}, u32[]{:S(2)}) collective-permute-start(bf16[100,512]{1,0:T(8,128)(2,1)S(1)} %add_convert_fusion.4), channel_id=1, source_target_pairs={{0,32},{8,40},{16,48},{24,56},{32,0},{40,8},{48,16},{56,24},{64,96... | collective-permute-start | bytes 307208 | tf_op jit(solution)/shard_map/ppermute | solution.py:37
  265.8 8.1 %collective-permute-start.39 = (bf16[32,4096]{1,0:T(8,128)(2,1)S(1)}, bf16[32,4096]{1,0:T(8,128)(2,1)S(1)}, u32[]{:S(2)}, u32[]{:S(2)}) collective-permute-start(bf16[32,4096]{1,0:T(8,128)(2,1)S(1)} %add_convert_fusion.2), channel_id=1, source_target_pairs={{0,32},{8,40},{16,48},{24,56},{32,0},{40,8},{48,16},{56,24},{64,96... | collective-permute-start | bytes 786440 | tf_op jit(solution)/shard_map/ppermute | solution.py:37
  (42 other events, 779.4 us)
Sparse Core Ops, SparseCore 0:
  10.3 69.5 all-gather.2
  133.0 125.1 reduce-scatter.1

commit v6 on v5

--- a/solution.py
+++ b/solution.py
@@ -64,6 +64,14 @@
         if bit == 4 and beside:
             other = after(other, *beside)
         blocks = jnp.concatenate([blocks, other], axis=0)
+    return blocks
+
+
+def gather_far_first(value):
+    blocks = value[None]
+    for bit in (4, 2, 1):
+        both = jnp.stack([blocks, flip(blocks, "tp", bit)], axis=1)
+        blocks = both.reshape((-1,) + value.shape)
     return blocks
 
 
@@ -709,10 +717,11 @@
     )
     back_pairs = swap_pairs(back_own)
     summed = lax.psum_scatter(summed, "seq", scatter_dimension=0, tiled=False)
+    gen_full = exchange(gen_full, (4,))
     tap_low, tap_high = halo(taps)
-    out_own = spread(order, middle, down_weight, (tap_low,))
+    out_own = spread(order, middle, down_weight, (gen_full, tap_low, tap_high))
     out_pairs = swap_pairs(out_own)
-    gen_full = exchange(gen_full, (4,)).reshape(members * ROWS, width)
+    gen_full = gen_full.reshape(members * ROWS, width)
 
     out_last = flip(add_up([pair[1] for pair in out_pairs]).astype(BF16), "tp", 4)
     back_last = flip(add_up([pair[1] for pair in back_pairs]).astype(BF16), "tp", 4)
@@ -729,7 +738,7 @@
         (gen_full, tap_low, tap_high, out_own[0]),
     )
     grad_low, grad_high = halo(grad.astype(BF16))
-    logit_full = gather_small(logit_grad).reshape(members * ROWS, rows)
+    logit_full = gather_far_first(logit_grad).reshape(members * ROWS, rows)
     gen_sum = sum_over_seq(gen_grads(logit_grad, hidden_full), (1,))
     embed_grad, table_part = hidden_grads(
         (

time: 286 us -> 281 us (0.983)
  waiting for transfers between devices: 104 us -> 97.5 us
  starting transfers between devices: 64.8 us -> 58.4 us
  local copies, waits for them, and re-layouts: 14.2 us -> 18.7 us
    ppermute x34, starting transfers between devices: 53.6 us -> 47.1 us  [flip(): return lax.ppermute(value, axis, [(i, i ^ bit) for i in range(count)])]
    ppermute x34, waiting for transfers between devices: 101 us -> 95.7 us  [flip(): return lax.ppermute(value, axis, [(i, i ^ bit) for i in range(count)])]
    unnamed x65 -> x71, local copies, waits for them, and re-layouts: 9.64 us -> 13.3 us
  transfers between devices with their start and end apart: 42 -> 42, of which waited for: 22 -> 23; matrix products, arithmetic and copies ran while one was open for 6% -> 7% of each run, Pallas kernels for 13% -> 13%
where the time goes in v6:
time: 281 us; the launch traced here: 279 us
  waiting for transfers between devices  97.5 us (35%)
  Pallas kernels  73 us (26%)
  starting transfers between devices  58.4 us (21%)
  local copies, waits for them, and re-layouts  18.7 us (7%)
  other arithmetic  15.6 us (6%)
  between operations  14.5 us (5%)
    ppermute x34, waiting for transfers between devices, flip(): return lax.ppermute(value, axis, [(i, i ^ bit) for i in range(count)])  95.7 us
    ppermute x34, starting transfers between devices, flip(): return lax.ppermute(value, axis, [(i, i ^ bit) for i in range(count)])  47.1 us
    pallas_call x1, Pallas kernels, layer(): pl.pallas_call(kernel, grid_spec=pltpu.PrefetchScalarGridSpec(num_scalar_...  35.8 us
    unnamed x71, local copies, waits for them, and re-layouts  13.3 us
    pallas_call x1, Pallas kernels, spread(): pl.pallas_call(kernel, grid_spec=pltpu.PrefetchScalarGridSpec(num_scalar_...  11.4 us
    pallas_call x1, Pallas kernels, grad_middle(): pl.pallas_call(grad_middle_kernel, grid=(units // block,), in_specs=[pl.B...  8.64 us
    pallas_call x1, Pallas kernels, hidden_logits(): pl.pallas_call(hidden_logits_kernel, grid_spec=pltpu.PrefetchScalarGridSp...  6.02 us
  transfers between devices with their start and end apart: 42, of which 23 were waited for; matrix products, arithmetic and copies ran while one was open for 7% of the time, Pallas kernels for 13%

profile of v6, /device:TPU:0, one launch (start us, length us, event | category | flops | bytes accessed | tf_op | source)
XLA Modules:
  0.0 279.0 jit_solution(6386673527856059753)
XLA Ops:
  10.0 3.2 %collective-permute-start.2 = (bf16[384,512]{1,0:T(8,128)(2,1)S(1)}, bf16[384,512]{1,0:T(8,128)(2,1)S(1)}, u32[]{:S(2)}, u32[]{:S(2)}) collective-permute-start(bf16[384,512]{1,0:T(8,128)(2,1)S(1)} %fusion.refs_0_.refs_6_), channel_id=1, source_target_pairs={{0,4},{1,5},{2,6},{3,7},{4,0},{5,1},{6,2},{7,3},{8,12},{9,13},{10,... | collective-permute-start | bytes 1179656 | tf_op jit(solution)/shard_map/ppermute | solution.py:37
  15.1 2.5 collective-permute-start.1
  17.6 4.7 %collective-permute-done.2.refs_3_ = bf16[384,512]{1,0:T(8,128)(2,1)S(1)} collective-permute-done((bf16[384,512]{1,0:T(8,128)(2,1)S(1)}, bf16[384,512]{1,0:T(8,128)(2,1)S(1)}, u32[]{:S(2)}, u32[]{:S(2)}) %collective-permute-start.2) | collective-permute-done | bytes 393248 | tf_op jit(solution)/shard_map/ppermute | solution.py:37
  24.4 2.5 collective-permute-start.4
  30.0 10.7 %collective-permute-done.3.refs_4_ = bf16[384,512]{1,0:T(8,128)(2,1)S(1)} collective-permute-done((bf16[384,512]{1,0:T(8,128)(2,1)S(1)}, bf16[384,512]{1,0:T(8,128)(2,1)S(1)}, u32[]{:S(2)}, u32[]{:S(2)}) %collective-permute-start.3) | collective-permute-done | bytes 393248 | tf_op jit(solution)/shard_map/ppermute | solution.py:37
  41.4 2.7 collective-permute-start.7
  46.8 3.3 %collective-permute-done.7.refs_8_ = bf16[192,512]{1,0:T(8,128)(2,1)S(1)} collective-permute-done((bf16[192,512]{1,0:T(8,128)(2,1)}, bf16[192,512]{1,0:T(8,128)(2,1)S(1)}, u32[]{:S(2)}, u32[]{:S(2)}) %collective-permute-start.7) | collective-permute-done | bytes 196640 | tf_op jit(solution)/shard_map/ppermute | solution.py:37
  52.5 6.0 %hidden_logits.1 = (bf16[8,384,512]{2,1,0:T(8,128)(2,1)}, bf16[2,8,8,512]{3,2,1,0:T(8,128)(2,1)}, f32[32,384]{1,0:T(8,128)}, f32[384,32]{1,0:T(8,128)}) custom-call(s32[8]{0:T(128)} %iota_xor_fusion.order.refs_0_, bf16[384,512]{1,0:T(8,128)(2,1)} %copy-done.5, bf16[384,512]{1,0:T(8,128)(2,1)} %copy-done.20, bf16[384,512]{1,0:T(8,128)(2,1)} %copy-done.21, ...), custom_call_target="tpu_custom_call" | custom-call | tf_op jit(solution)/shard_map/hidden_logits/pallas_call | solution.py:150
  64.9 2.4 collective-permute-done.11
  70.4 2.8 %collective-permute-start.15 = (bf16[2,1,2,32,512]{4,3,2,1,0:T(8,128)(2,1)S(1)}, bf16[2,1,2,32,512]{4,3,2,1,0:T(8,128)(2,1)S(1)}, u32[]{:S(2)}, u32[]{:S(2)}) collective-permute-start(bf16[2,1,2,32,512]{4,3,2,1,0:T(8,128)(2,1)S(1)} %get-tuple-element.67), channel_id=1, source_target_pairs={{0,2},{1,3},{2,0},{3,1},{4,6},{5,7},{6,4},{7,5},{8,10},{9,11},{10,... | collective-permute-start | bytes 393224 | tf_op jit(solution)/shard_map/ppermute | solution.py:37
  73.2 2.9 %collective-permute-done.12 = f32[2,32,384]{2,1,0:T(8,128)S(1)} collective-permute-done((f32[2,32,384]{2,1,0:T(8,128)S(1)}, f32[2,32,384]{2,1,0:T(8,128)S(1)}, u32[]{:S(2)}, u32[]{:S(2)}) %collective-permute-start.12) | collective-permute-done | bytes 98336 | tf_op jit(solution)/shard_map/ppermute | solution.py:37
  77.0 3.5 %collective-permute-start.13 = (f32[4,32,384]{2,1,0:T(8,128)S(1)}, f32[4,32,384]{2,1,0:T(8,128)S(1)}, u32[]{:S(2)}, u32[]{:S(2)}) collective-permute-start(f32[4,32,384]{2,1,0:T(8,128)S(1)} %pad_maximum_fusion.3), channel_id=1, source_target_pairs={{0,4},{1,5},{2,6},{3,7},{4,0},{5,1},{6,2},{7,3},{8,12},{9,13},{10,... | collective-permute-start | bytes 589832 | tf_op jit(solution)/shard_map/ppermute | solution.py:37
  82.7 3.0 %collective-permute-start.9 = (bf16[8,8,512]{2,1,0:T(8,128)(2,1)S(1)}, bf16[8,8,512]{2,1,0:T(8,128)(2,1)S(1)}, u32[]{:S(2)}, u32[]{:S(2)}) collective-permute-start(bf16[8,8,512]{2,1,0:T(8,128)(2,1)S(1)} %get-tuple-element.73), channel_id=1, source_target_pairs={{0,8},{8,16},{16,24},{24,32},{32,40},{40,48},{48,56},{56,64},{64,7... | collective-permute-start | bytes 196616 | tf_op jit(solution)/shard_map/ppermute | solution.py:698
  86.5 8.6 %grad_middle.1.refs_7_ = f32[384,1024]{1,0:T(8,128)} custom-call(bf16[8,384,512]{2,1,0:T(8,128)(2,1)} %bitcast.61, bf16[1024,4096]{1,0:T(8,128)(2,1)} %refs_2_.3, bf16[1024,4096]{1,0:T(8,128)(2,1)} %refs_2_.3, bf16[1024,4096]{1,0:T(8,128)(2,1)} %refs_2_.3, bf16[1024,4096]{1,0:T(8,128)(2,1)} %refs_2_.3), custom_call_target="tpu_custom_call" | custom-call | tf_op jit(solution)/shard_map/grad_middle/pallas_call | solution.py:416
  96.6 35.8 %layer.1 = (bf16[16,512,1024]{2,1,0:T(8,128)(2,1)}, bf16[384,512]{1,0:T(8,128)(2,1)}, bf16[384,1024]{1,0:T(8,128)(2,1)}, bf16[2,384,512]{2,1,0:T(8,128)(2,1)}, b...) custom-call(s32[8]{0:T(128)} %iota_xor_fusion.order.refs_0_, ...), custom_call_target="tpu_custom_call" | custom-call | tf_op jit(solution)/shard_map/layer/pallas_call | solution.py:344
  134.5 2.7 collective-permute-start.25
  140.3 5.3 %collective-permute-done.16 = bf16[1,2,2,32,512]{4,3,2,1,0:T(8,128)(2,1)S(1)} collective-permute-done((bf16[1,2,2,32,512]{4,3,2,1,0:T(8,128)(2,1)S(1)}, bf16[1,2,2,32,512]{4,3,2,1,0:T(8,128)(2,1)S(1)}, u32[]{:S(2)}, u32[]{:S(2)}) %collective-permute-start.16) | collective-permute-done | bytes 131104 | tf_op jit(solution)/shard_map/ppermute | solution.py:37
  149.2 11.4 %ffn_out.1 = (bf16[2,384,512]{2,1,0:T(8,128)(2,1)}, bf16[2,384,512]{2,1,0:T(8,128)(2,1)}, bf16[2,384,512]{2,1,0:T(8,128)(2,1)}, bf16[2,384,512]{2,1,0:T(8,128)(2,1)}) custom-call(s32[8]{0:T(128)} %iota_xor_fusion.order.refs_0_, bf16[384,1024]{1,0:T(8,128)(2,1)} %get-tuple-element.31.refs_1_, bf16[1024,4096]{1,0:T(8,128)(2,1)} %refs_2_.3, ...), custom_call_target="tpu_custom_call" | custom-call | tf_op jit(solution)/shard_map/ffn_out/pallas_call | solution.py:441
  161.6 3.7 %collective-permute-start.21 = (bf16[2,384,512]{2,1,0:T(8,128)(2,1)}, bf16[2,384,512]{2,1,0:T(8,128)(2,1)}, u32[]{:S(2)}, u32[]{:S(2)}) collective-permute-start(bf16[2,384,512]{2,1,0:T(8,128)(2,1)} %get-tuple-element.36), channel_id=1, source_target_pairs={{0,3},{1,2},{2,1},{3,0},{4,7},{5,6},{6,5},{7,4},{8,11},{9,10},{10,... | collective-permute-start | bytes 2359304 | tf_op jit(solution)/shard_map/ppermute | solution.py:37
  165.3 4.4 %collective-permute-done.24.refs_2_ = bf16[2,384,512]{2,1,0:T(8,128)(2,1)} collective-permute-done((bf16[2,384,512]{2,1,0:T(8,128)(2,1)}, bf16[2,384,512]{2,1,0:T(8,128)(2,1)}, u32[]{:S(2)}, u32[]{:S(2)}) %collective-permute-start.24) | collective-permute-done | bytes 786464 | tf_op jit(solution)/shard_map/ppermute | solution.py:37
  169.7 3.5 %collective-permute-done.25.refs_3_ = bf16[2,384,512]{2,1,0:T(8,128)(2,1)} collective-permute-done((bf16[2,384,512]{2,1,0:T(8,128)(2,1)}, bf16[2,384,512]{2,1,0:T(8,128)(2,1)}, u32[]{:S(2)}, u32[]{:S(2)}) %collective-permute-start.25) | collective-permute-done | bytes 786464 | tf_op jit(solution)/shard_map/ppermute | solution.py:37
  178.3 14.7 %collective-permute-done.26.refs_4_ = bf16[384,512]{1,0:T(8,128)(2,1)} collective-permute-done((bf16[384,512]{1,0:T(8,128)(2,1)}, bf16[384,512]{1,0:T(8,128)(2,1)}, u32[]{:S(2)}, u32[]{:S(2)}) %collective-permute-start.26) | collective-permute-done | bytes 393248 | tf_op jit(solution)/shard_map/ppermute | solution.py:37
  199.6 5.2 %kernel_grads.1 = (f32[384,512]{1,0:T(8,128)S(1)}, bf16[32,384]{1,0:T(8,128)(2,1)S(1)}) custom-call(bf16[2,384,512]{2,1,0:T(8,128)(2,1)S(1)} %copy-done.9, bf16[2,384,512]{2,1,0:T(8,128)(2,1)} %collective-permute-done.23.refs_1_, bf16[2,384,512]{2,1,0:T(8,128)(2,1)} %collective-permute-done.24.refs_2_, bf16[2,384,512]{2,1,0:T(8,128)(2,1)} %collective-permute-done.25.refs_3_, ...), custom_call_target="tpu_custom_call" | custom-call | tf_op jit(solution)/shard_map/kernel_grads/pallas_call | solution.py:506
  206.2 4.4 %collective-permute-done.29 = bf16[1,32,384]{2,1,0:T(8,128)(2,1)S(1)} collective-permute-done((bf16[1,32,384]{2,1,0:T(8,128)(2,1)S(1)}, bf16[1,32,384]{2,1,0:T(8,128)(2,1)S(1)}, u32[]{:S(2)}, u32[]{:S(2)}) %collective-permute-start.29) | collective-permute-done | bytes 24608 | tf_op jit(solution)/shard_map/ppermute | solution.py:37
  221.1 8.0 %collective-permute-done.22.refs_11_ = bf16[384,512]{1,0:T(8,128)(2,1)S(1)} collective-permute-done((bf16[384,512]{1,0:T(8,128)(2,1)S(1)}, bf16[384,512]{1,0:T(8,128)(2,1)S(1)}, u32[]{:S(2)}, u32[]{:S(2)}) %collective-permute-start.22) | collective-permute-done | bytes 393248 | tf_op jit(solution)/shard_map/ppermute | solution.py:37
  229.2 4.8 %hidden_grads.1 = (f32[384,512]{1,0:T(8,128)}, f32[100,512]{1,0:T(8,128)S(1)}) custom-call(f32[384,512]{1,0:T(8,128)S(1)} %get-tuple-element.41.refs_0_, bf16[8,512]{1,0:T(8,128)(2,1)S(1)} %collective-permute-done.27.refs_1_, bf16[8,512]{1,0:T(8,128)(2,1)S(1)} %collective-permute-done.28.refs_2_, f32[384,32]{1,0:T(8,128)S(1)} %copy-done.12, ...), custom_call_target="tpu_custom_call" | custom-call | tf_op jit(solution)/shard_map/hidden_grads/pallas_call | solution.py:591
  237.5 4.9 %collective-permute-done.34 = bf16[100,512]{1,0:T(8,128)(2,1)S(1)} collective-permute-done((bf16[100,512]{1,0:T(8,128)(2,1)S(1)}, bf16[100,512]{1,0:T(8,128)(2,1)S(1)}, u32[]{:S(2)}, u32[]{:S(2)}) %collective-permute-start.34) | collective-permute-done | bytes 102432 | tf_op jit(solution)/shard_map/ppermute | solution.py:37
  242.5 8.0 %collective-permute-done.37 = bf16[32,4096]{1,0:T(8,128)(2,1)S(1)} collective-permute-done((bf16[32,4096]{1,0:T(8,128)(2,1)S(1)}, bf16[32,4096]{1,0:T(8,128)(2,1)S(1)}, u32[]{:S(2)}, u32[]{:S(2)}) %collective-permute-start.37) | collective-permute-done | bytes 262176 | tf_op jit(solution)/shard_map/ppermute | solution.py:37
  250.7 2.7 collective-permute-start.36
  253.4 6.1 %collective-permute-done.38 = bf16[32,4096]{1,0:T(8,128)(2,1)S(1)} collective-permute-done((bf16[32,4096]{1,0:T(8,128)(2,1)S(1)}, bf16[32,4096]{1,0:T(8,128)(2,1)S(1)}, u32[]{:S(2)}, u32[]{:S(2)}) %collective-permute-start.38) | collective-permute-done | bytes 262176 | tf_op jit(solution)/shard_map/ppermute | solution.py:37
  263.5 4.1 %collective-permute-done.39 = bf16[32,4096]{1,0:T(8,128)(2,1)S(1)} collective-permute-done((bf16[32,4096]{1,0:T(8,128)(2,1)S(1)}, bf16[32,4096]{1,0:T(8,128)(2,1)S(1)}, u32[]{:S(2)}, u32[]{:S(2)}) %collective-permute-start.39) | collective-permute-done | bytes 262176 | tf_op jit(solution)/shard_map/ppermute | solution.py:37
  268.4 2.4 convert_bitcast_fusion
  (175 shorter events, 73.6 us)
Async XLA Ops:
  7.2 79.3 %all-gather.3.cloned.1.call-start = ((), (), s32[]{:S(2)}) async-start(), calls=%async_computation.2 | async-start | bytes 3538944 | tf_op jit(solution)/shard_map/all_gather | solution.py:693
  7.9 260.5 %reduce-scatter.2.cloned.1.call-start = ((), (), s32[]{:S(2)}) async-start(), calls=%async_computation.1 | async-start | bytes 17825792 | tf_op jit(solution)/shard_map/reduce_scatter | solution.py:719
  10.0 12.3 %collective-permute-start.2 = (bf16[384,512]{1,0:T(8,128)(2,1)S(1)}, bf16[384,512]{1,0:T(8,128)(2,1)S(1)}, u32[]{:S(2)}, u32[]{:S(2)}) collective-permute-start(bf16[384,512]{1,0:T(8,128)(2,1)S(1)} %fusion.refs_0_.refs_6_), channel_id=1, source_target_pairs={{0,4},{1,5},{2,6},{3,7},{4,0},{5,1},{6,2},{7,3},{8,12},{9,13},{10,... | collective-permute-start | bytes 1179656 | tf_op jit(solution)/shard_map/ppermute | solution.py:37
  13.2 13.8 %collective-permute-start = (bf16[384,512]{1,0:T(8,128)(2,1)S(1)}, bf16[384,512]{1,0:T(8,128)(2,1)S(1)}, u32[]{:S(2)}, u32[]{:S(2)}) collective-permute-start(bf16[384,512]{1,0:T(8,128)(2,1)S(1)} %fusion.refs_0_.refs_6_), channel_id=1, source_target_pairs={{0,1},{1,0},{2,3},{3,2},{4,5},{5,4},{6,7},{7,6},{8,9},{9,8},{10,11... | collective-permute-start | bytes 1179656 | tf_op jit(solution)/shard_map/ppermute | solution.py:37
  15.1 13.5 %collective-permute-start.1 = (bf16[384,512]{1,0:T(8,128)(2,1)S(1)}, bf16[384,512]{1,0:T(8,128)(2,1)S(1)}, u32[]{:S(2)}, u32[]{:S(2)}) collective-permute-start(bf16[384,512]{1,0:T(8,128)(2,1)S(1)} %fusion.refs_0_.refs_6_), channel_id=1, source_target_pairs={{0,3},{1,2},{2,1},{3,0},{4,7},{5,6},{6,5},{7,4},{8,11},{9,10},{10,... | collective-permute-start | bytes 1179656 | tf_op jit(solution)/shard_map/ppermute | solution.py:37
  22.3 18.4 %collective-permute-start.3 = (bf16[384,512]{1,0:T(8,128)(2,1)S(1)}, bf16[384,512]{1,0:T(8,128)(2,1)S(1)}, u32[]{:S(2)}, u32[]{:S(2)}) collective-permute-start(bf16[384,512]{1,0:T(8,128)(2,1)S(1)} %collective-permute-done.2.refs_3_), channel_id=1, source_target_pairs={{0,1},{1,0},{2,3},{3,2},{4,5},{5,4},{6,7},{7,6},{8,9},{9,8},{10,11... | collective-permute-start | bytes 1179656 | tf_op jit(solution)/shard_map/ppermute | solution.py:37
  24.4 19.7 %collective-permute-start.4 = (bf16[384,512]{1,0:T(8,128)(2,1)S(1)}, bf16[384,512]{1,0:T(8,128)(2,1)S(1)}, u32[]{:S(2)}, u32[]{:S(2)}) collective-permute-start(bf16[384,512]{1,0:T(8,128)(2,1)S(1)} %collective-permute-done.2.refs_3_), channel_id=1, source_target_pairs={{0,3},{1,2},{2,1},{3,0},{4,7},{5,6},{6,5},{7,4},{8,11},{9,10},{10,... | collective-permute-start | bytes 1179656 | tf_op jit(solution)/shard_map/ppermute | solution.py:37
  27.0 19.8 %collective-permute-start.5 = (bf16[192,512]{1,0:T(8,128)(2,1)S(1)}, bf16[192,512]{1,0:T(8,128)(2,1)S(1)}, u32[]{:S(2)}, u32[]{:S(2)}) collective-permute-start(bf16[192,512]{1,0:T(8,128)(2,1)S(1)} %slice.126), channel_id=1, source_target_pairs={{0,3},{1,2},{2,1},{3,0},{4,7},{5,6},{6,5},{7,4},{8,11},{9,10},{10,... | collective-permute-start | bytes 589832 | tf_op jit(solution)/shard_map/ppermute | solution.py:37
  29.3 17.5 %collective-permute-start.6 = (bf16[192,512]{1,0:T(8,128)(2,1)}, bf16[192,512]{1,0:T(8,128)(2,1)S(1)}, u32[]{:S(2)}, u32[]{:S(2)}) collective-permute-start(bf16[192,512]{1,0:T(8,128)(2,1)} %slice.127), channel_id=1, source_target_pairs={{0,1},{1,0},{2,3},{3,2},{4,5},{5,4},{6,7},{7,6},{8,9},{9,8},{10,11... | collective-permute-start | bytes 589832 | tf_op jit(solution)/shard_map/ppermute | solution.py:37
  41.4 8.7 %collective-permute-start.7 = (bf16[192,512]{1,0:T(8,128)(2,1)}, bf16[192,512]{1,0:T(8,128)(2,1)S(1)}, u32[]{:S(2)}, u32[]{:S(2)}) collective-permute-start(bf16[192,512]{1,0:T(8,128)(2,1)} %slice.128), channel_id=1, source_target_pairs={{0,3},{1,2},{2,1},{3,0},{4,7},{5,6},{6,5},{7,4},{8,11},{9,10},{10,... | collective-permute-start | bytes 589832 | tf_op jit(solution)/shard_map/ppermute | solution.py:37
  68.0 8.1 %collective-permute-start.12 = (f32[2,32,384]{2,1,0:T(8,128)S(1)}, f32[2,32,384]{2,1,0:T(8,128)S(1)}, u32[]{:S(2)}, u32[]{:S(2)}) collective-permute-start(f32[2,32,384]{2,1,0:T(8,128)S(1)} %pad_maximum_fusion.6), channel_id=1, source_target_pairs={{0,2},{1,3},{2,0},{3,1},{4,6},{5,7},{6,4},{7,5},{8,10},{9,11},{10,... | collective-permute-start | bytes 294920 | tf_op jit(solution)/shard_map/ppermute | solution.py:37
  70.4 15.3 %collective-permute-start.15 = (bf16[2,1,2,32,512]{4,3,2,1,0:T(8,128)(2,1)S(1)}, bf16[2,1,2,32,512]{4,3,2,1,0:T(8,128)(2,1)S(1)}, u32[]{:S(2)}, u32[]{:S(2)}) collective-permute-start(bf16[2,1,2,32,512]{4,3,2,1,0:T(8,128)(2,1)S(1)} %get-tuple-element.67), channel_id=1, source_target_pairs={{0,2},{1,3},{2,0},{3,1},{4,6},{5,7},{6,4},{7,5},{8,10},{9,11},{10,... | collective-permute-start | bytes 393224 | tf_op jit(solution)/shard_map/ppermute | solution.py:37
  77.0 18.1 %collective-permute-start.13 = (f32[4,32,384]{2,1,0:T(8,128)S(1)}, f32[4,32,384]{2,1,0:T(8,128)S(1)}, u32[]{:S(2)}, u32[]{:S(2)}) collective-permute-start(f32[4,32,384]{2,1,0:T(8,128)S(1)} %pad_maximum_fusion.3), channel_id=1, source_target_pairs={{0,4},{1,5},{2,6},{3,7},{4,0},{5,1},{6,2},{7,3},{8,12},{9,13},{10,... | collective-permute-start | bytes 589832 | tf_op jit(solution)/shard_map/ppermute | solution.py:37
  81.4 14.5 %collective-permute-start.10 = (bf16[8,8,512]{2,1,0:T(8,128)(2,1)S(1)}, bf16[8,8,512]{2,1,0:T(8,128)(2,1)S(1)}, u32[]{:S(2)}, u32[]{:S(2)}) collective-permute-start(bf16[8,8,512]{2,1,0:T(8,128)(2,1)S(1)} %get-tuple-element.72), channel_id=1, source_target_pairs={{8,0},{16,8},{24,16},{32,24},{40,32},{48,40},{56,48},{64,56},{72,6... | collective-permute-start | bytes 196616 | tf_op jit(solution)/shard_map/ppermute | solution.py:699
  82.7 13.2 %collective-permute-start.9 = (bf16[8,8,512]{2,1,0:T(8,128)(2,1)S(1)}, bf16[8,8,512]{2,1,0:T(8,128)(2,1)S(1)}, u32[]{:S(2)}, u32[]{:S(2)}) collective-permute-start(bf16[8,8,512]{2,1,0:T(8,128)(2,1)S(1)} %get-tuple-element.73), channel_id=1, source_target_pairs={{0,8},{8,16},{16,24},{24,32},{32,40},{40,48},{48,56},{56,64},{64,7... | collective-permute-start | bytes 196616 | tf_op jit(solution)/shard_map/ppermute | solution.py:698
  132.4 29.3 %collective-permute-start.23 = (bf16[2,384,512]{2,1,0:T(8,128)(2,1)}, bf16[2,384,512]{2,1,0:T(8,128)(2,1)}, u32[]{:S(2)}, u32[]{:S(2)}) collective-permute-start(bf16[2,384,512]{2,1,0:T(8,128)(2,1)} %get-tuple-element.38), channel_id=1, source_target_pairs={{0,1},{1,0},{2,3},{3,2},{4,5},{5,4},{6,7},{7,6},{8,9},{9,8},{10,11... | collective-permute-start | bytes 2359304 | tf_op jit(solution)/shard_map/ppermute | solution.py:37
  133.0 36.8 %collective-permute-start.24 = (bf16[2,384,512]{2,1,0:T(8,128)(2,1)}, bf16[2,384,512]{2,1,0:T(8,128)(2,1)}, u32[]{:S(2)}, u32[]{:S(2)}) collective-permute-start(bf16[2,384,512]{2,1,0:T(8,128)(2,1)} %get-tuple-element.39), channel_id=1, source_target_pairs={{0,2},{1,3},{2,0},{3,1},{4,6},{5,7},{6,4},{7,5},{8,10},{9,11},{10,... | collective-permute-start | bytes 2359304 | tf_op jit(solution)/shard_map/ppermute | solution.py:37
  134.5 38.8 %collective-permute-start.25 = (bf16[2,384,512]{2,1,0:T(8,128)(2,1)}, bf16[2,384,512]{2,1,0:T(8,128)(2,1)}, u32[]{:S(2)}, u32[]{:S(2)}) collective-permute-start(bf16[2,384,512]{2,1,0:T(8,128)(2,1)} %get-tuple-element.40), channel_id=1, source_target_pairs={{0,3},{1,2},{2,1},{3,0},{4,7},{5,6},{6,5},{7,4},{8,11},{9,10},{10,... | collective-permute-start | bytes 2359304 | tf_op jit(solution)/shard_map/ppermute | solution.py:37
  137.2 8.4 %collective-permute-start.16 = (bf16[1,2,2,32,512]{4,3,2,1,0:T(8,128)(2,1)S(1)}, bf16[1,2,2,32,512]{4,3,2,1,0:T(8,128)(2,1)S(1)}, u32[]{:S(2)}, u32[]{:S(2)}) collective-permute-start(bf16[1,2,2,32,512]{4,3,2,1,0:T(8,128)(2,1)S(1)} %get-tuple-element.65), channel_id=1, source_target_pairs={{0,4},{1,5},{2,6},{3,7},{4,0},{5,1},{6,2},{7,3},{8,12},{9,13},{10,... | collective-permute-start | bytes 393224 | tf_op jit(solution)/shard_map/ppermute | solution.py:37
  138.0 9.6 %collective-permute-start.17 = (f32[8,32]{1,0:T(8,128)S(1)}, f32[8,32]{1,0:T(8,128)S(1)}, u32[]{:S(2)}, u32[]{:S(2)}) collective-permute-start(f32[8,32]{1,0:T(8,128)S(1)} %get-tuple-element.71), channel_id=1, source_target_pairs={{0,8},{8,16},{16,24},{24,32},{32,40},{40,48},{48,56},{56,64},{64,7... | collective-permute-start | bytes 3080 | tf_op jit(solution)/shard_map/ppermute | solution.py:44
  160.6 50.9 %collective-permute-start.19 = (bf16[2,384,512]{2,1,0:T(8,128)(2,1)}, bf16[2,384,512]{2,1,0:T(8,128)(2,1)}, u32[]{:S(2)}, u32[]{:S(2)}) collective-permute-start(bf16[2,384,512]{2,1,0:T(8,128)(2,1)} %get-tuple-element.34), channel_id=1, source_target_pairs={{0,1},{1,0},{2,3},{3,2},{4,5},{5,4},{6,7},{7,6},{8,9},{9,8},{10,11... | collective-permute-start | bytes 2359304 | tf_op jit(solution)/shard_map/ppermute | solution.py:37
  160.6 50.9 %collective-permute-start.20 = (bf16[2,384,512]{2,1,0:T(8,128)(2,1)}, bf16[2,384,512]{2,1,0:T(8,128)(2,1)}, u32[]{:S(2)}, u32[]{:S(2)}) collective-permute-start(bf16[2,384,512]{2,1,0:T(8,128)(2,1)} %get-tuple-element.35), channel_id=1, source_target_pairs={{0,2},{1,3},{2,0},{3,1},{4,6},{5,7},{6,4},{7,5},{8,10},{9,11},{10,... | collective-permute-start | bytes 2359304 | tf_op jit(solution)/shard_map/ppermute | solution.py:37
  161.6 49.8 %collective-permute-start.21 = (bf16[2,384,512]{2,1,0:T(8,128)(2,1)}, bf16[2,384,512]{2,1,0:T(8,128)(2,1)}, u32[]{:S(2)}, u32[]{:S(2)}) collective-permute-start(bf16[2,384,512]{2,1,0:T(8,128)(2,1)} %get-tuple-element.36), channel_id=1, source_target_pairs={{0,3},{1,2},{2,1},{3,0},{4,7},{5,6},{6,5},{7,4},{8,11},{9,10},{10,... | collective-permute-start | bytes 2359304 | tf_op jit(solution)/shard_map/ppermute | solution.py:37
  175.6 17.4 %collective-permute-start.26 = (bf16[384,512]{1,0:T(8,128)(2,1)}, bf16[384,512]{1,0:T(8,128)(2,1)}, u32[]{:S(2)}, u32[]{:S(2)}) collective-permute-start(bf16[384,512]{1,0:T(8,128)(2,1)} %fusion.5), channel_id=1, source_target_pairs={{0,4},{1,5},{2,6},{3,7},{4,0},{5,1},{6,2},{7,3},{8,12},{9,13},{10,... | collective-permute-start | bytes 1179656 | tf_op jit(solution)/shard_map/ppermute | solution.py:37
  213.0 16.2 %collective-permute-start.22 = (bf16[384,512]{1,0:T(8,128)(2,1)S(1)}, bf16[384,512]{1,0:T(8,128)(2,1)S(1)}, u32[]{:S(2)}, u32[]{:S(2)}) collective-permute-start(bf16[384,512]{1,0:T(8,128)(2,1)S(1)} %fusion.4), channel_id=1, source_target_pairs={{0,4},{1,5},{2,6},{3,7},{4,0},{5,1},{6,2},{7,3},{8,12},{9,13},{10,... | collective-permute-start | bytes 1179656 | tf_op jit(solution)/shard_map/ppermute | solution.py:37
  216.8 12.4 %collective-permute-start.27 = (bf16[8,512]{1,0:T(8,128)(2,1)S(1)}, bf16[8,512]{1,0:T(8,128)(2,1)S(1)}, u32[]{:S(2)}, u32[]{:S(2)}) collective-permute-start(bf16[8,512]{1,0:T(8,128)(2,1)S(1)} %get-tuple-element.63), channel_id=1, source_target_pairs={{0,8},{8,16},{16,24},{24,32},{32,40},{40,48},{48,56},{56,64},{64,7... | collective-permute-start | bytes 24584 | tf_op jit(solution)/shard_map/ppermute | solution.py:44
  218.9 10.3 %collective-permute-start.28 = (bf16[8,512]{1,0:T(8,128)(2,1)S(1)}, bf16[8,512]{1,0:T(8,128)(2,1)S(1)}, u32[]{:S(2)}, u32[]{:S(2)}) collective-permute-start(bf16[8,512]{1,0:T(8,128)(2,1)S(1)} %get-tuple-element.62), channel_id=1, source_target_pairs={{8,0},{16,8},{24,16},{32,24},{40,32},{48,40},{56,48},{64,56},{72,6... | collective-permute-start | bytes 24584 | tf_op jit(solution)/shard_map/ppermute | solution.py:45
  236.4 14.1 %collective-permute-start.37 = (bf16[32,4096]{1,0:T(8,128)(2,1)S(1)}, bf16[32,4096]{1,0:T(8,128)(2,1)S(1)}, u32[]{:S(2)}, u32[]{:S(2)}) collective-permute-start(bf16[32,4096]{1,0:T(8,128)(2,1)S(1)} %get-tuple-element.60), channel_id=1, source_target_pairs={{0,64},{8,72},{16,80},{24,88},{32,96},{40,104},{48,112},{56,120},{... | collective-permute-start | bytes 786440 | tf_op jit(solution)/shard_map/ppermute | solution.py:37
  242.4 8.2 %collective-permute-start.35 = (bf16[100,512]{1,0:T(8,128)(2,1)S(1)}, bf16[100,512]{1,0:T(8,128)(2,1)S(1)}, u32[]{:S(2)}, u32[]{:S(2)}) collective-permute-start(bf16[100,512]{1,0:T(8,128)(2,1)S(1)} %add_convert_fusion.5), channel_id=1, source_target_pairs={{0,16},{8,24},{16,0},{24,8},{32,48},{40,56},{48,32},{56,40},{64,80... | collective-permute-start | bytes 307208 | tf_op jit(solution)/shard_map/ppermute | solution.py:37
  250.6 9.0 %collective-permute-start.38 = (bf16[32,4096]{1,0:T(8,128)(2,1)S(1)}, bf16[32,4096]{1,0:T(8,128)(2,1)S(1)}, u32[]{:S(2)}, u32[]{:S(2)}) collective-permute-start(bf16[32,4096]{1,0:T(8,128)(2,1)S(1)} %add_convert_fusion.3), channel_id=1, source_target_pairs={{0,16},{8,24},{16,0},{24,8},{32,48},{40,56},{48,32},{56,40},{64,80... | collective-permute-start | bytes 786440 | tf_op jit(solution)/shard_map/ppermute | solution.py:37
  250.7 12.1 %collective-permute-start.36 = (bf16[100,512]{1,0:T(8,128)(2,1)S(1)}, bf16[100,512]{1,0:T(8,128)(2,1)S(1)}, u32[]{:S(2)}, u32[]{:S(2)}) collective-permute-start(bf16[100,512]{1,0:T(8,128)(2,1)S(1)} %add_convert_fusion.4), channel_id=1, source_target_pairs={{0,32},{8,40},{16,48},{24,56},{32,0},{40,8},{48,16},{56,24},{64,96... | collective-permute-start | bytes 307208 | tf_op jit(solution)/shard_map/ppermute | solution.py:37
  259.6 8.0 %collective-permute-start.39 = (bf16[32,4096]{1,0:T(8,128)(2,1)S(1)}, bf16[32,4096]{1,0:T(8,128)(2,1)S(1)}, u32[]{:S(2)}, u32[]{:S(2)}) collective-permute-start(bf16[32,4096]{1,0:T(8,128)(2,1)S(1)} %add_convert_fusion.2), channel_id=1, source_target_pairs={{0,32},{8,40},{16,48},{24,56},{32,0},{40,8},{48,16},{56,24},{64,96... | collective-permute-start | bytes 786440 | tf_op jit(solution)/shard_map/ppermute | solution.py:37
  (45 other events, 720.8 us)
Sparse Core Ops, SparseCore 0:
  10.3 69.6 all-gather.2
  132.5 122.0 reduce-scatter.1

commit v7 on v6

--- a/solution.py
+++ b/solution.py
@@ -739,7 +739,7 @@
     )
     grad_low, grad_high = halo(grad.astype(BF16))
     logit_full = gather_far_first(logit_grad).reshape(members * ROWS, rows)
-    gen_sum = sum_over_seq(gen_grads(logit_grad, hidden_full), (1,))
+    gen_sum = sum_over_seq(gen_grads(logit_grad, hidden_full), (1, 2))
     embed_grad, table_part = hidden_grads(
         (
             grad,
@@ -756,7 +756,7 @@
         codes,
         (gen_sum, out_last),
     )
-    gen_sum = sum_over_seq(gen_sum, (8, 2, 4))
+    gen_sum = sum_over_seq(gen_sum, (8, 4))
     gen_grad = gen_sum[:columns].T
     table_grad = sum_over_seq(table_part)
 

time: 281 us -> 276 us (0.982)
  waiting for transfers between devices: 97.5 us -> 93.8 us
    ppermute x34, waiting for transfers between devices: 95.7 us -> 92.1 us  [flip(): return lax.ppermute(value, axis, [(i, i ^ bit) for i in range(count)])]
  transfers between devices with their start and end apart: 42 -> 42, of which waited for: 23 -> 23; matrix products, arithmetic and copies ran while one was open for 7% -> 7% of each run, Pallas kernels for 13% -> 14%
where the time goes in v7:
time: 276 us; the launch traced here: 274 us
  waiting for transfers between devices  93.8 us (34%)
  Pallas kernels  73 us (26%)
  starting transfers between devices  57.2 us (21%)
  local copies, waits for them, and re-layouts  18.7 us (7%)
  other arithmetic  15.7 us (6%)
  between operations  14.5 us (5%)
    ppermute x34, waiting for transfers between devices, flip(): return lax.ppermute(value, axis, [(i, i ^ bit) for i in range(count)])  92.1 us
    ppermute x34, starting transfers between devices, flip(): return lax.ppermute(value, axis, [(i, i ^ bit) for i in range(count)])  46.7 us
    pallas_call x1, Pallas kernels, layer(): pl.pallas_call(kernel, grid_spec=pltpu.PrefetchScalarGridSpec(num_scalar_...  35.8 us
    unnamed x71, local copies, waits for them, and re-layouts  13.3 us
    pallas_call x1, Pallas kernels, spread(): pl.pallas_call(kernel, grid_spec=pltpu.PrefetchScalarGridSpec(num_scalar_...  11.4 us
    pallas_call x1, Pallas kernels, grad_middle(): pl.pallas_call(grad_middle_kernel, grid=(units // block,), in_specs=[pl.B...  8.64 us
    pallas_call x1, Pallas kernels, hidden_logits(): pl.pallas_call(hidden_logits_kernel, grid_spec=pltpu.PrefetchScalarGridSp...  6.02 us
  transfers between devices with their start and end apart: 42, of which 23 were waited for; matrix products, arithmetic and copies ran while one was open for 7% of the time, Pallas kernels for 14%

profile of v7, /device:TPU:0, one launch (start us, length us, event | category | flops | bytes accessed | tf_op | source)
XLA Modules:
  0.0 274.1 jit_solution(13926556283316920780)
XLA Ops:
  10.0 3.2 %collective-permute-start.2 = (bf16[384,512]{1,0:T(8,128)(2,1)S(1)}, bf16[384,512]{1,0:T(8,128)(2,1)S(1)}, u32[]{:S(2)}, u32[]{:S(2)}) collective-permute-start(bf16[384,512]{1,0:T(8,128)(2,1)S(1)} %fusion.refs_0_.refs_6_), channel_id=1, source_target_pairs={{0,4},{1,5},{2,6},{3,7},{4,0},{5,1},{6,2},{7,3},{8,12},{9,13},{10,... | collective-permute-start | bytes 1179656 | tf_op jit(solution)/shard_map/ppermute | solution.py:37
  15.1 2.5 collective-permute-start.1
  17.6 4.7 %collective-permute-done.2.refs_3_ = bf16[384,512]{1,0:T(8,128)(2,1)S(1)} collective-permute-done((bf16[384,512]{1,0:T(8,128)(2,1)S(1)}, bf16[384,512]{1,0:T(8,128)(2,1)S(1)}, u32[]{:S(2)}, u32[]{:S(2)}) %collective-permute-start.2) | collective-permute-done | bytes 393248 | tf_op jit(solution)/shard_map/ppermute | solution.py:37
  24.4 2.5 collective-permute-start.4
  30.0 10.7 %collective-permute-done.3.refs_4_ = bf16[384,512]{1,0:T(8,128)(2,1)S(1)} collective-permute-done((bf16[384,512]{1,0:T(8,128)(2,1)S(1)}, bf16[384,512]{1,0:T(8,128)(2,1)S(1)}, u32[]{:S(2)}, u32[]{:S(2)}) %collective-permute-start.3) | collective-permute-done | bytes 393248 | tf_op jit(solution)/shard_map/ppermute | solution.py:37
  41.4 2.7 collective-permute-start.7
  46.8 3.3 %collective-permute-done.7.refs_8_ = bf16[192,512]{1,0:T(8,128)(2,1)S(1)} collective-permute-done((bf16[192,512]{1,0:T(8,128)(2,1)}, bf16[192,512]{1,0:T(8,128)(2,1)S(1)}, u32[]{:S(2)}, u32[]{:S(2)}) %collective-permute-start.7) | collective-permute-done | bytes 196640 | tf_op jit(solution)/shard_map/ppermute | solution.py:37
  52.5 6.0 %hidden_logits.1 = (bf16[8,384,512]{2,1,0:T(8,128)(2,1)}, bf16[2,8,8,512]{3,2,1,0:T(8,128)(2,1)}, f32[32,384]{1,0:T(8,128)}, f32[384,32]{1,0:T(8,128)}) custom-call(s32[8]{0:T(128)} %iota_xor_fusion.order.refs_0_, bf16[384,512]{1,0:T(8,128)(2,1)} %copy-done.5, bf16[384,512]{1,0:T(8,128)(2,1)} %copy-done.20, bf16[384,512]{1,0:T(8,128)(2,1)} %copy-done.21, ...), custom_call_target="tpu_custom_call" | custom-call | tf_op jit(solution)/shard_map/hidden_logits/pallas_call | solution.py:150
  64.9 2.4 collective-permute-done.11
  70.4 2.8 %collective-permute-start.15 = (bf16[2,1,2,32,512]{4,3,2,1,0:T(8,128)(2,1)S(1)}, bf16[2,1,2,32,512]{4,3,2,1,0:T(8,128)(2,1)S(1)}, u32[]{:S(2)}, u32[]{:S(2)}) collective-permute-start(bf16[2,1,2,32,512]{4,3,2,1,0:T(8,128)(2,1)S(1)} %get-tuple-element.67), channel_id=1, source_target_pairs={{0,2},{1,3},{2,0},{3,1},{4,6},{5,7},{6,4},{7,5},{8,10},{9,11},{10,... | collective-permute-start | bytes 393224 | tf_op jit(solution)/shard_map/ppermute | solution.py:37
  73.2 2.9 %collective-permute-done.12 = f32[2,32,384]{2,1,0:T(8,128)S(1)} collective-permute-done((f32[2,32,384]{2,1,0:T(8,128)S(1)}, f32[2,32,384]{2,1,0:T(8,128)S(1)}, u32[]{:S(2)}, u32[]{:S(2)}) %collective-permute-start.12) | collective-permute-done | bytes 98336 | tf_op jit(solution)/shard_map/ppermute | solution.py:37
  77.0 3.5 %collective-permute-start.13 = (f32[4,32,384]{2,1,0:T(8,128)S(1)}, f32[4,32,384]{2,1,0:T(8,128)S(1)}, u32[]{:S(2)}, u32[]{:S(2)}) collective-permute-start(f32[4,32,384]{2,1,0:T(8,128)S(1)} %pad_maximum_fusion.3), channel_id=1, source_target_pairs={{0,4},{1,5},{2,6},{3,7},{4,0},{5,1},{6,2},{7,3},{8,12},{9,13},{10,... | collective-permute-start | bytes 589832 | tf_op jit(solution)/shard_map/ppermute | solution.py:37
  82.7 3.0 %collective-permute-start.9 = (bf16[8,8,512]{2,1,0:T(8,128)(2,1)S(1)}, bf16[8,8,512]{2,1,0:T(8,128)(2,1)S(1)}, u32[]{:S(2)}, u32[]{:S(2)}) collective-permute-start(bf16[8,8,512]{2,1,0:T(8,128)(2,1)S(1)} %get-tuple-element.73), channel_id=1, source_target_pairs={{0,8},{8,16},{16,24},{24,32},{32,40},{40,48},{48,56},{56,64},{64,7... | collective-permute-start | bytes 196616 | tf_op jit(solution)/shard_map/ppermute | solution.py:698
  86.5 8.6 %grad_middle.1.refs_7_ = f32[384,1024]{1,0:T(8,128)} custom-call(bf16[8,384,512]{2,1,0:T(8,128)(2,1)} %bitcast.61, bf16[1024,4096]{1,0:T(8,128)(2,1)} %refs_2_.3, bf16[1024,4096]{1,0:T(8,128)(2,1)} %refs_2_.3, bf16[1024,4096]{1,0:T(8,128)(2,1)} %refs_2_.3, bf16[1024,4096]{1,0:T(8,128)(2,1)} %refs_2_.3), custom_call_target="tpu_custom_call" | custom-call | tf_op jit(solution)/shard_map/grad_middle/pallas_call | solution.py:416
  96.6 35.8 %layer.1 = (bf16[16,512,1024]{2,1,0:T(8,128)(2,1)}, bf16[384,512]{1,0:T(8,128)(2,1)}, bf16[384,1024]{1,0:T(8,128)(2,1)}, bf16[2,384,512]{2,1,0:T(8,128)(2,1)}, b...) custom-call(s32[8]{0:T(128)} %iota_xor_fusion.order.refs_0_, ...), custom_call_target="tpu_custom_call" | custom-call | tf_op jit(solution)/shard_map/layer/pallas_call | solution.py:344
  134.5 2.7 collective-permute-start.25
  140.3 5.3 %collective-permute-done.16 = bf16[1,2,2,32,512]{4,3,2,1,0:T(8,128)(2,1)S(1)} collective-permute-done((bf16[1,2,2,32,512]{4,3,2,1,0:T(8,128)(2,1)S(1)}, bf16[1,2,2,32,512]{4,3,2,1,0:T(8,128)(2,1)S(1)}, u32[]{:S(2)}, u32[]{:S(2)}) %collective-permute-start.16) | collective-permute-done | bytes 131104 | tf_op jit(solution)/shard_map/ppermute | solution.py:37
  149.2 11.4 %ffn_out.1 = (bf16[2,384,512]{2,1,0:T(8,128)(2,1)}, bf16[2,384,512]{2,1,0:T(8,128)(2,1)}, bf16[2,384,512]{2,1,0:T(8,128)(2,1)}, bf16[2,384,512]{2,1,0:T(8,128)(2,1)}) custom-call(s32[8]{0:T(128)} %iota_xor_fusion.order.refs_0_, bf16[384,1024]{1,0:T(8,128)(2,1)} %get-tuple-element.31.refs_1_, bf16[1024,4096]{1,0:T(8,128)(2,1)} %refs_2_.3, ...), custom_call_target="tpu_custom_call" | custom-call | tf_op jit(solution)/shard_map/ffn_out/pallas_call | solution.py:441
  161.6 3.7 %collective-permute-start.21 = (bf16[2,384,512]{2,1,0:T(8,128)(2,1)}, bf16[2,384,512]{2,1,0:T(8,128)(2,1)}, u32[]{:S(2)}, u32[]{:S(2)}) collective-permute-start(bf16[2,384,512]{2,1,0:T(8,128)(2,1)} %get-tuple-element.36), channel_id=1, source_target_pairs={{0,3},{1,2},{2,1},{3,0},{4,7},{5,6},{6,5},{7,4},{8,11},{9,10},{10,... | collective-permute-start | bytes 2359304 | tf_op jit(solution)/shard_map/ppermute | solution.py:37
  165.3 4.4 %collective-permute-done.24.refs_2_ = bf16[2,384,512]{2,1,0:T(8,128)(2,1)} collective-permute-done((bf16[2,384,512]{2,1,0:T(8,128)(2,1)}, bf16[2,384,512]{2,1,0:T(8,128)(2,1)}, u32[]{:S(2)}, u32[]{:S(2)}) %collective-permute-start.24) | collective-permute-done | bytes 786464 | tf_op jit(solution)/shard_map/ppermute | solution.py:37
  169.7 3.5 %collective-permute-done.25.refs_3_ = bf16[2,384,512]{2,1,0:T(8,128)(2,1)} collective-permute-done((bf16[2,384,512]{2,1,0:T(8,128)(2,1)}, bf16[2,384,512]{2,1,0:T(8,128)(2,1)}, u32[]{:S(2)}, u32[]{:S(2)}) %collective-permute-start.25) | collective-permute-done | bytes 786464 | tf_op jit(solution)/shard_map/ppermute | solution.py:37
  178.3 14.7 %collective-permute-done.26.refs_4_ = bf16[384,512]{1,0:T(8,128)(2,1)} collective-permute-done((bf16[384,512]{1,0:T(8,128)(2,1)}, bf16[384,512]{1,0:T(8,128)(2,1)}, u32[]{:S(2)}, u32[]{:S(2)}) %collective-permute-start.26) | collective-permute-done | bytes 393248 | tf_op jit(solution)/shard_map/ppermute | solution.py:37
  199.6 5.2 %kernel_grads.1 = (f32[384,512]{1,0:T(8,128)S(1)}, bf16[32,384]{1,0:T(8,128)(2,1)S(1)}) custom-call(bf16[2,384,512]{2,1,0:T(8,128)(2,1)S(1)} %copy-done.9, bf16[2,384,512]{2,1,0:T(8,128)(2,1)} %collective-permute-done.23.refs_1_, bf16[2,384,512]{2,1,0:T(8,128)(2,1)} %collective-permute-done.24.refs_2_, bf16[2,384,512]{2,1,0:T(8,128)(2,1)} %collective-permute-done.25.refs_3_, ...), custom_call_target="tpu_custom_call" | custom-call | tf_op jit(solution)/shard_map/kernel_grads/pallas_call | solution.py:506
  207.0 3.6 %collective-permute-done.29 = bf16[1,32,384]{2,1,0:T(8,128)(2,1)S(1)} collective-permute-done((bf16[1,32,384]{2,1,0:T(8,128)(2,1)S(1)}, bf16[1,32,384]{2,1,0:T(8,128)(2,1)S(1)}, u32[]{:S(2)}, u32[]{:S(2)}) %collective-permute-start.29) | collective-permute-done | bytes 24608 | tf_op jit(solution)/shard_map/ppermute | solution.py:37
  213.5 2.8 %collective-permute-done.30 = bf16[2,32,384]{2,1,0:T(8,128)(2,1)S(1)} collective-permute-done((bf16[2,32,384]{2,1,0:T(8,128)(2,1)S(1)}, bf16[2,32,384]{2,1,0:T(8,128)(2,1)S(1)}, u32[]{:S(2)}, u32[]{:S(2)}) %collective-permute-start.30) | collective-permute-done | bytes 49184 | tf_op jit(solution)/shard_map/ppermute | solution.py:37
  221.1 6.1 %collective-permute-done.33 = bf16[32,4096]{1,0:T(8,128)(2,1)S(1)} collective-permute-done((bf16[32,4096]{1,0:T(8,128)(2,1)S(1)}, bf16[32,4096]{1,0:T(8,128)(2,1)S(1)}, u32[]{:S(2)}, u32[]{:S(2)}) %collective-permute-start.33) | collective-permute-done | bytes 262176 | tf_op jit(solution)/shard_map/ppermute | solution.py:37
  229.2 4.8 %hidden_grads.1 = (f32[384,512]{1,0:T(8,128)}, f32[100,512]{1,0:T(8,128)S(1)}) custom-call(f32[384,512]{1,0:T(8,128)S(1)} %get-tuple-element.41.refs_0_, bf16[8,512]{1,0:T(8,128)(2,1)S(1)} %collective-permute-done.27.refs_1_, bf16[8,512]{1,0:T(8,128)(2,1)S(1)} %collective-permute-done.28.refs_2_, f32[384,32]{1,0:T(8,128)S(1)} %copy-done.12, ...), custom_call_target="tpu_custom_call" | custom-call | tf_op jit(solution)/shard_map/hidden_grads/pallas_call | solution.py:591
  237.5 4.9 %collective-permute-done.35 = bf16[100,512]{1,0:T(8,128)(2,1)S(1)} collective-permute-done((bf16[100,512]{1,0:T(8,128)(2,1)S(1)}, bf16[100,512]{1,0:T(8,128)(2,1)S(1)}, u32[]{:S(2)}, u32[]{:S(2)}) %collective-permute-start.35) | collective-permute-done | bytes 102432 | tf_op jit(solution)/shard_map/ppermute | solution.py:37
  242.5 7.9 %collective-permute-done.38 = bf16[32,4096]{1,0:T(8,128)(2,1)S(1)} collective-permute-done((bf16[32,4096]{1,0:T(8,128)(2,1)S(1)}, bf16[32,4096]{1,0:T(8,128)(2,1)S(1)}, u32[]{:S(2)}, u32[]{:S(2)}) %collective-permute-start.38) | collective-permute-done | bytes 262176 | tf_op jit(solution)/shard_map/ppermute | solution.py:37
  250.6 3.6 %collective-permute-start.37 = (bf16[100,512]{1,0:T(8,128)(2,1)S(1)}, bf16[100,512]{1,0:T(8,128)(2,1)S(1)}, u32[]{:S(2)}, u32[]{:S(2)}) collective-permute-start(bf16[100,512]{1,0:T(8,128)(2,1)S(1)} %add_convert_fusion.4), channel_id=1, source_target_pairs={{0,32},{8,40},{16,48},{24,56},{32,0},{40,8},{48,16},{56,24},{64,96... | collective-permute-start | bytes 307208 | tf_op jit(solution)/shard_map/ppermute | solution.py:37
  256.5 5.5 %collective-permute-done.37 = bf16[100,512]{1,0:T(8,128)(2,1)S(1)} collective-permute-done((bf16[100,512]{1,0:T(8,128)(2,1)S(1)}, bf16[100,512]{1,0:T(8,128)(2,1)S(1)}, u32[]{:S(2)}, u32[]{:S(2)}) %collective-permute-start.37) | collective-permute-done | bytes 102432 | tf_op jit(solution)/shard_map/ppermute | solution.py:37
  263.6 2.4 convert_bitcast_fusion
  (175 shorter events, 72.5 us)
Async XLA Ops:
  7.2 79.3 %all-gather.3.cloned.1.call-start = ((), (), s32[]{:S(2)}) async-start(), calls=%async_computation.2 | async-start | bytes 3538944 | tf_op jit(solution)/shard_map/all_gather | solution.py:693
  7.9 255.7 %reduce-scatter.2.cloned.1.call-start = ((), (), s32[]{:S(2)}) async-start(), calls=%async_computation.1 | async-start | bytes 17825792 | tf_op jit(solution)/shard_map/reduce_scatter | solution.py:719
  10.0 12.3 %collective-permute-start.2 = (bf16[384,512]{1,0:T(8,128)(2,1)S(1)}, bf16[384,512]{1,0:T(8,128)(2,1)S(1)}, u32[]{:S(2)}, u32[]{:S(2)}) collective-permute-start(bf16[384,512]{1,0:T(8,128)(2,1)S(1)} %fusion.refs_0_.refs_6_), channel_id=1, source_target_pairs={{0,4},{1,5},{2,6},{3,7},{4,0},{5,1},{6,2},{7,3},{8,12},{9,13},{10,... | collective-permute-start | bytes 1179656 | tf_op jit(solution)/shard_map/ppermute | solution.py:37
  13.2 13.8 %collective-permute-start = (bf16[384,512]{1,0:T(8,128)(2,1)S(1)}, bf16[384,512]{1,0:T(8,128)(2,1)S(1)}, u32[]{:S(2)}, u32[]{:S(2)}) collective-permute-start(bf16[384,512]{1,0:T(8,128)(2,1)S(1)} %fusion.refs_0_.refs_6_), channel_id=1, source_target_pairs={{0,1},{1,0},{2,3},{3,2},{4,5},{5,4},{6,7},{7,6},{8,9},{9,8},{10,11... | collective-permute-start | bytes 1179656 | tf_op jit(solution)/shard_map/ppermute | solution.py:37
  15.1 13.5 %collective-permute-start.1 = (bf16[384,512]{1,0:T(8,128)(2,1)S(1)}, bf16[384,512]{1,0:T(8,128)(2,1)S(1)}, u32[]{:S(2)}, u32[]{:S(2)}) collective-permute-start(bf16[384,512]{1,0:T(8,128)(2,1)S(1)} %fusion.refs_0_.refs_6_), channel_id=1, source_target_pairs={{0,3},{1,2},{2,1},{3,0},{4,7},{5,6},{6,5},{7,4},{8,11},{9,10},{10,... | collective-permute-start | bytes 1179656 | tf_op jit(solution)/shard_map/ppermute | solution.py:37
  22.3 18.4 %collective-permute-start.3 = (bf16[384,512]{1,0:T(8,128)(2,1)S(1)}, bf16[384,512]{1,0:T(8,128)(2,1)S(1)}, u32[]{:S(2)}, u32[]{:S(2)}) collective-permute-start(bf16[384,512]{1,0:T(8,128)(2,1)S(1)} %collective-permute-done.2.refs_3_), channel_id=1, source_target_pairs={{0,1},{1,0},{2,3},{3,2},{4,5},{5,4},{6,7},{7,6},{8,9},{9,8},{10,11... | collective-permute-start | bytes 1179656 | tf_op jit(solution)/shard_map/ppermute | solution.py:37
  24.4 19.7 %collective-permute-start.4 = (bf16[384,512]{1,0:T(8,128)(2,1)S(1)}, bf16[384,512]{1,0:T(8,128)(2,1)S(1)}, u32[]{:S(2)}, u32[]{:S(2)}) collective-permute-start(bf16[384,512]{1,0:T(8,128)(2,1)S(1)} %collective-permute-done.2.refs_3_), channel_id=1, source_target_pairs={{0,3},{1,2},{2,1},{3,0},{4,7},{5,6},{6,5},{7,4},{8,11},{9,10},{10,... | collective-permute-start | bytes 1179656 | tf_op jit(solution)/shard_map/ppermute | solution.py:37
  27.0 19.8 %collective-permute-start.5 = (bf16[192,512]{1,0:T(8,128)(2,1)S(1)}, bf16[192,512]{1,0:T(8,128)(2,1)S(1)}, u32[]{:S(2)}, u32[]{:S(2)}) collective-permute-start(bf16[192,512]{1,0:T(8,128)(2,1)S(1)} %slice.126), channel_id=1, source_target_pairs={{0,3},{1,2},{2,1},{3,0},{4,7},{5,6},{6,5},{7,4},{8,11},{9,10},{10,... | collective-permute-start | bytes 589832 | tf_op jit(solution)/shard_map/ppermute | solution.py:37
  29.3 17.5 %collective-permute-start.6 = (bf16[192,512]{1,0:T(8,128)(2,1)}, bf16[192,512]{1,0:T(8,128)(2,1)S(1)}, u32[]{:S(2)}, u32[]{:S(2)}) collective-permute-start(bf16[192,512]{1,0:T(8,128)(2,1)} %slice.127), channel_id=1, source_target_pairs={{0,1},{1,0},{2,3},{3,2},{4,5},{5,4},{6,7},{7,6},{8,9},{9,8},{10,11... | collective-permute-start | bytes 589832 | tf_op jit(solution)/shard_map/ppermute | solution.py:37
  41.4 8.7 %collective-permute-start.7 = (bf16[192,512]{1,0:T(8,128)(2,1)}, bf16[192,512]{1,0:T(8,128)(2,1)S(1)}, u32[]{:S(2)}, u32[]{:S(2)}) collective-permute-start(bf16[192,512]{1,0:T(8,128)(2,1)} %slice.128), channel_id=1, source_target_pairs={{0,3},{1,2},{2,1},{3,0},{4,7},{5,6},{6,5},{7,4},{8,11},{9,10},{10,... | collective-permute-start | bytes 589832 | tf_op jit(solution)/shard_map/ppermute | solution.py:37
  70.4 15.3 %collective-permute-start.15 = (bf16[2,1,2,32,512]{4,3,2,1,0:T(8,128)(2,1)S(1)}, bf16[2,1,2,32,512]{4,3,2,1,0:T(8,128)(2,1)S(1)}, u32[]{:S(2)}, u32[]{:S(2)}) collective-permute-start(bf16[2,1,2,32,512]{4,3,2,1,0:T(8,128)(2,1)S(1)} %get-tuple-element.67), channel_id=1, source_target_pairs={{0,2},{1,3},{2,0},{3,1},{4,6},{5,7},{6,4},{7,5},{8,10},{9,11},{10,... | collective-permute-start | bytes 393224 | tf_op jit(solution)/shard_map/ppermute | solution.py:37
  77.0 18.1 %collective-permute-start.13 = (f32[4,32,384]{2,1,0:T(8,128)S(1)}, f32[4,32,384]{2,1,0:T(8,128)S(1)}, u32[]{:S(2)}, u32[]{:S(2)}) collective-permute-start(f32[4,32,384]{2,1,0:T(8,128)S(1)} %pad_maximum_fusion.3), channel_id=1, source_target_pairs={{0,4},{1,5},{2,6},{3,7},{4,0},{5,1},{6,2},{7,3},{8,12},{9,13},{10,... | collective-permute-start | bytes 589832 | tf_op jit(solution)/shard_map/ppermute | solution.py:37
  81.4 14.5 %collective-permute-start.10 = (bf16[8,8,512]{2,1,0:T(8,128)(2,1)S(1)}, bf16[8,8,512]{2,1,0:T(8,128)(2,1)S(1)}, u32[]{:S(2)}, u32[]{:S(2)}) collective-permute-start(bf16[8,8,512]{2,1,0:T(8,128)(2,1)S(1)} %get-tuple-element.72), channel_id=1, source_target_pairs={{8,0},{16,8},{24,16},{32,24},{40,32},{48,40},{56,48},{64,56},{72,6... | collective-permute-start | bytes 196616 | tf_op jit(solution)/shard_map/ppermute | solution.py:699
  82.7 13.2 %collective-permute-start.9 = (bf16[8,8,512]{2,1,0:T(8,128)(2,1)S(1)}, bf16[8,8,512]{2,1,0:T(8,128)(2,1)S(1)}, u32[]{:S(2)}, u32[]{:S(2)}) collective-permute-start(bf16[8,8,512]{2,1,0:T(8,128)(2,1)S(1)} %get-tuple-element.73), channel_id=1, source_target_pairs={{0,8},{8,16},{16,24},{24,32},{32,40},{40,48},{48,56},{56,64},{64,7... | collective-permute-start | bytes 196616 | tf_op jit(solution)/shard_map/ppermute | solution.py:698
  132.4 29.3 %collective-permute-start.23 = (bf16[2,384,512]{2,1,0:T(8,128)(2,1)}, bf16[2,384,512]{2,1,0:T(8,128)(2,1)}, u32[]{:S(2)}, u32[]{:S(2)}) collective-permute-start(bf16[2,384,512]{2,1,0:T(8,128)(2,1)} %get-tuple-element.38), channel_id=1, source_target_pairs={{0,1},{1,0},{2,3},{3,2},{4,5},{5,4},{6,7},{7,6},{8,9},{9,8},{10,11... | collective-permute-start | bytes 2359304 | tf_op jit(solution)/shard_map/ppermute | solution.py:37
  133.0 36.8 %collective-permute-start.24 = (bf16[2,384,512]{2,1,0:T(8,128)(2,1)}, bf16[2,384,512]{2,1,0:T(8,128)(2,1)}, u32[]{:S(2)}, u32[]{:S(2)}) collective-permute-start(bf16[2,384,512]{2,1,0:T(8,128)(2,1)} %get-tuple-element.39), channel_id=1, source_target_pairs={{0,2},{1,3},{2,0},{3,1},{4,6},{5,7},{6,4},{7,5},{8,10},{9,11},{10,... | collective-permute-start | bytes 2359304 | tf_op jit(solution)/shard_map/ppermute | solution.py:37
  134.5 38.8 %collective-permute-start.25 = (bf16[2,384,512]{2,1,0:T(8,128)(2,1)}, bf16[2,384,512]{2,1,0:T(8,128)(2,1)}, u32[]{:S(2)}, u32[]{:S(2)}) collective-permute-start(bf16[2,384,512]{2,1,0:T(8,128)(2,1)} %get-tuple-element.40), channel_id=1, source_target_pairs={{0,3},{1,2},{2,1},{3,0},{4,7},{5,6},{6,5},{7,4},{8,11},{9,10},{10,... | collective-permute-start | bytes 2359304 | tf_op jit(solution)/shard_map/ppermute | solution.py:37
  137.2 8.4 %collective-permute-start.16 = (bf16[1,2,2,32,512]{4,3,2,1,0:T(8,128)(2,1)S(1)}, bf16[1,2,2,32,512]{4,3,2,1,0:T(8,128)(2,1)S(1)}, u32[]{:S(2)}, u32[]{:S(2)}) collective-permute-start(bf16[1,2,2,32,512]{4,3,2,1,0:T(8,128)(2,1)S(1)} %get-tuple-element.65), channel_id=1, source_target_pairs={{0,4},{1,5},{2,6},{3,7},{4,0},{5,1},{6,2},{7,3},{8,12},{9,13},{10,... | collective-permute-start | bytes 393224 | tf_op jit(solution)/shard_map/ppermute | solution.py:37
  138.0 9.6 %collective-permute-start.17 = (f32[8,32]{1,0:T(8,128)S(1)}, f32[8,32]{1,0:T(8,128)S(1)}, u32[]{:S(2)}, u32[]{:S(2)}) collective-permute-start(f32[8,32]{1,0:T(8,128)S(1)} %get-tuple-element.71), channel_id=1, source_target_pairs={{0,8},{8,16},{16,24},{24,32},{32,40},{40,48},{48,56},{56,64},{64,7... | collective-permute-start | bytes 3080 | tf_op jit(solution)/shard_map/ppermute | solution.py:44
  160.6 50.9 %collective-permute-start.19 = (bf16[2,384,512]{2,1,0:T(8,128)(2,1)}, bf16[2,384,512]{2,1,0:T(8,128)(2,1)}, u32[]{:S(2)}, u32[]{:S(2)}) collective-permute-start(bf16[2,384,512]{2,1,0:T(8,128)(2,1)} %get-tuple-element.34), channel_id=1, source_target_pairs={{0,1},{1,0},{2,3},{3,2},{4,5},{5,4},{6,7},{7,6},{8,9},{9,8},{10,11... | collective-permute-start | bytes 2359304 | tf_op jit(solution)/shard_map/ppermute | solution.py:37
  160.6 50.9 %collective-permute-start.20 = (bf16[2,384,512]{2,1,0:T(8,128)(2,1)}, bf16[2,384,512]{2,1,0:T(8,128)(2,1)}, u32[]{:S(2)}, u32[]{:S(2)}) collective-permute-start(bf16[2,384,512]{2,1,0:T(8,128)(2,1)} %get-tuple-element.35), channel_id=1, source_target_pairs={{0,2},{1,3},{2,0},{3,1},{4,6},{5,7},{6,4},{7,5},{8,10},{9,11},{10,... | collective-permute-start | bytes 2359304 | tf_op jit(solution)/shard_map/ppermute | solution.py:37
  161.6 49.8 %collective-permute-start.21 = (bf16[2,384,512]{2,1,0:T(8,128)(2,1)}, bf16[2,384,512]{2,1,0:T(8,128)(2,1)}, u32[]{:S(2)}, u32[]{:S(2)}) collective-permute-start(bf16[2,384,512]{2,1,0:T(8,128)(2,1)} %get-tuple-element.36), channel_id=1, source_target_pairs={{0,3},{1,2},{2,1},{3,0},{4,7},{5,6},{6,5},{7,4},{8,11},{9,10},{10,... | collective-permute-start | bytes 2359304 | tf_op jit(solution)/shard_map/ppermute | solution.py:37
  175.6 17.4 %collective-permute-start.26 = (bf16[384,512]{1,0:T(8,128)(2,1)}, bf16[384,512]{1,0:T(8,128)(2,1)}, u32[]{:S(2)}, u32[]{:S(2)}) collective-permute-start(bf16[384,512]{1,0:T(8,128)(2,1)} %fusion.5), channel_id=1, source_target_pairs={{0,4},{1,5},{2,6},{3,7},{4,0},{5,1},{6,2},{7,3},{8,12},{9,13},{10,... | collective-permute-start | bytes 1179656 | tf_op jit(solution)/shard_map/ppermute | solution.py:37
  206.9 9.5 %collective-permute-start.32 = (bf16[32,4096]{1,0:T(8,128)(2,1)S(1)}, bf16[32,4096]{1,0:T(8,128)(2,1)S(1)}, u32[]{:S(2)}, u32[]{:S(2)}) collective-permute-start(bf16[32,4096]{1,0:T(8,128)(2,1)S(1)} %convert_element_type.165), channel_id=1, source_target_pairs={{0,8},{8,0},{16,24},{24,16},{32,40},{40,32},{48,56},{56,48},{64,72... | collective-permute-start | bytes 786440 | tf_op jit(solution)/shard_map/ppermute | solution.py:37
  213.0 16.2 %collective-permute-start.22 = (bf16[384,512]{1,0:T(8,128)(2,1)S(1)}, bf16[384,512]{1,0:T(8,128)(2,1)S(1)}, u32[]{:S(2)}, u32[]{:S(2)}) collective-permute-start(bf16[384,512]{1,0:T(8,128)(2,1)S(1)} %fusion.4), channel_id=1, source_target_pairs={{0,4},{1,5},{2,6},{3,7},{4,0},{5,1},{6,2},{7,3},{8,12},{9,13},{10,... | collective-permute-start | bytes 1179656 | tf_op jit(solution)/shard_map/ppermute | solution.py:37
  216.5 10.7 %collective-permute-start.33 = (bf16[32,4096]{1,0:T(8,128)(2,1)S(1)}, bf16[32,4096]{1,0:T(8,128)(2,1)S(1)}, u32[]{:S(2)}, u32[]{:S(2)}) collective-permute-start(bf16[32,4096]{1,0:T(8,128)(2,1)S(1)} %add_convert_fusion.3), channel_id=1, source_target_pairs={{0,16},{8,24},{16,0},{24,8},{32,48},{40,56},{48,32},{56,40},{64,80... | collective-permute-start | bytes 786440 | tf_op jit(solution)/shard_map/ppermute | solution.py:37
  216.6 12.6 %collective-permute-start.27 = (bf16[8,512]{1,0:T(8,128)(2,1)S(1)}, bf16[8,512]{1,0:T(8,128)(2,1)S(1)}, u32[]{:S(2)}, u32[]{:S(2)}) collective-permute-start(bf16[8,512]{1,0:T(8,128)(2,1)S(1)} %get-tuple-element.63), channel_id=1, source_target_pairs={{0,8},{8,16},{16,24},{24,32},{32,40},{40,48},{48,56},{56,64},{64,7... | collective-permute-start | bytes 24584 | tf_op jit(solution)/shard_map/ppermute | solution.py:44
  217.9 11.3 %collective-permute-start.28 = (bf16[8,512]{1,0:T(8,128)(2,1)S(1)}, bf16[8,512]{1,0:T(8,128)(2,1)S(1)}, u32[]{:S(2)}, u32[]{:S(2)}) collective-permute-start(bf16[8,512]{1,0:T(8,128)(2,1)S(1)} %get-tuple-element.62), channel_id=1, source_target_pairs={{8,0},{16,8},{24,16},{32,24},{40,32},{48,40},{56,48},{64,56},{72,6... | collective-permute-start | bytes 24584 | tf_op jit(solution)/shard_map/ppermute | solution.py:45
  236.4 14.1 %collective-permute-start.38 = (bf16[32,4096]{1,0:T(8,128)(2,1)S(1)}, bf16[32,4096]{1,0:T(8,128)(2,1)S(1)}, u32[]{:S(2)}, u32[]{:S(2)}) collective-permute-start(bf16[32,4096]{1,0:T(8,128)(2,1)S(1)} %get-tuple-element.60), channel_id=1, source_target_pairs={{0,64},{8,72},{16,80},{24,88},{32,96},{40,104},{48,112},{56,120},{... | collective-permute-start | bytes 786440 | tf_op jit(solution)/shard_map/ppermute | solution.py:37
  242.4 8.2 %collective-permute-start.36 = (bf16[100,512]{1,0:T(8,128)(2,1)S(1)}, bf16[100,512]{1,0:T(8,128)(2,1)S(1)}, u32[]{:S(2)}, u32[]{:S(2)}) collective-permute-start(bf16[100,512]{1,0:T(8,128)(2,1)S(1)} %add_convert_fusion.5), channel_id=1, source_target_pairs={{0,16},{8,24},{16,0},{24,8},{32,48},{40,56},{48,32},{56,40},{64,80... | collective-permute-start | bytes 307208 | tf_op jit(solution)/shard_map/ppermute | solution.py:37
  250.5 12.2 %collective-permute-start.39 = (bf16[32,4096]{1,0:T(8,128)(2,1)S(1)}, bf16[32,4096]{1,0:T(8,128)(2,1)S(1)}, u32[]{:S(2)}, u32[]{:S(2)}) collective-permute-start(bf16[32,4096]{1,0:T(8,128)(2,1)S(1)} %add_convert_fusion.2), channel_id=1, source_target_pairs={{0,32},{8,40},{16,48},{24,56},{32,0},{40,8},{48,16},{56,24},{64,96... | collective-permute-start | bytes 786440 | tf_op jit(solution)/shard_map/ppermute | solution.py:37
  250.6 11.4 %collective-permute-start.37 = (bf16[100,512]{1,0:T(8,128)(2,1)S(1)}, bf16[100,512]{1,0:T(8,128)(2,1)S(1)}, u32[]{:S(2)}, u32[]{:S(2)}) collective-permute-start(bf16[100,512]{1,0:T(8,128)(2,1)S(1)} %add_convert_fusion.4), channel_id=1, source_target_pairs={{0,32},{8,40},{16,48},{24,56},{32,0},{40,8},{48,16},{56,24},{64,96... | collective-permute-start | bytes 307208 | tf_op jit(solution)/shard_map/ppermute | solution.py:37
  (45 other events, 653.9 us)
Sparse Core Ops, SparseCore 0:
  10.3 69.6 all-gather.2
  132.5 122.0 reduce-scatter.1
